TPU v7x, 32 devices: a whole 2x2x4 slice. The times are simulated.
32 devices in a mesh: dp: 4 (over y, x), seq: 2 (over core), tensor: 4 (over z).
Axes of the slice: x: 2, y: 2, z: 4, core: 2. Of those that a mesh axis runs over, the one named last changes fastest.
Arguments:
- tokens: bfloat16 [8, 512, 1536], P('dp', ('seq', 'tensor')), may hold values from -6 to 6
- segments: int32 [8, 512], P('dp', 'seq'), may hold values from 0 to 3, never falling along the last dimension, each value on 1 to 192 neighbouring positions
- input_gain: float32 [1536], replicated, may hold values from 0.5 to 1.5
- gate_proj: bfloat16 [1536, 3072], P(('dp', 'seq'), 'tensor'), may hold values from -0.15625 to 0.15625
- inner_proj: bfloat16 [1536, 3072], P(('dp', 'seq'), 'tensor'), may hold values from -0.15625 to 0.15625
- state_proj: bfloat16 [1536, 256], P(('dp', 'seq')), may hold values from -0.15625 to 0.15625
- step_proj: bfloat16 [1536, 48], P(('dp', 'seq'), 'tensor'), may hold values from -0.15625 to 0.15625
- conv_inner: float32 [4, 3072], replicated, may hold values from -3 to 3
- inner_bias: float32 [3072], replicated, may hold values from -0.5 to 0.5
- conv_state: float32 [4, 256], replicated, may hold values from -3 to 3
- state_bias: float32 [256], replicated, may hold values from -0.5 to 0.5
- step_bias: float32 [48], replicated, may hold values from -4.6 to -2.3
- log_rates: float32 [48], replicated, may hold values from -5.8 to 0.7
- skip_gain: float32 [48], replicated, may hold values from 0.5 to 1.5
- gated_gain: float32 [3072], replicated, may hold values from 0.5 to 1.5
- output_proj: bfloat16 [3072, 1536], P('tensor', ('dp', 'seq')), may hold values from -0.109375 to 0.109375
- cotangent: bfloat16 [8, 512, 1536], P('dp', ('seq', 'tensor')), may hold values from -6 to 6
Outputs:
- block_out: bfloat16 [8, 512, 1536], P('dp', ('seq', 'tensor'))
- grad_tokens: float32 [8, 512, 1536], P('dp', ('seq', 'tensor'))
- grad_input_gain: float32 [1536], replicated
- grad_gate_proj: float32 [1536, 3072], P(('dp', 'seq'), 'tensor')
- grad_inner_proj: float32 [1536, 3072], P(('dp', 'seq'), 'tensor')
- grad_state_proj: float32 [1536, 256], P(('dp', 'seq'))
- grad_step_proj: float32 [1536, 48], P(('dp', 'seq'), 'tensor')
- grad_conv_inner: float32 [4, 3072], replicated
- grad_inner_bias: float32 [3072], replicated
- grad_conv_state: float32 [4, 256], replicated
- grad_state_bias: float32 [256], replicated
- grad_step_bias: float32 [48], replicated
- grad_log_rates: float32 [48], replicated
- grad_skip_gain: float32 [48], replicated
- grad_gated_gain: float32 [3072], replicated
- grad_output_proj: float32 [3072, 1536], P('tensor', ('dp', 'seq'))
Inputs may be any that keep to these rules, and one draw needn't show every extreme that they name: `segments`: segment ids never fall along a sequence; a document has at most 3 * 512 // (2 * max(4, 0)) tokens.
All inputs are finite; a program needn't handle non-finite values.
Results may differ from a plain program's by a relative error of at most 0.012.
The roundings to bfloat16 on the way count: a program that leaves them out, or rounds other values in their place, can miss the bound.
Values may be sent and summed in bfloat16 or wider, within the bound.
A program may use at most 128 MiB of HBM per device.

v0:
```python
import jax
import jax.numpy as jnp
from jax import lax
from jax.sharding import PartitionSpec as P

HEAD_DIM = 64
STATE = 128
KERNEL = 4
BLOCK = 256


EPS = 1e-05
HIGH = lax.Precision.HIGHEST


def passed_along(block, axis, distance):
    devices = range(lax.axis_size(axis))
    route = [(i - distance, i) for i in devices if i - distance in devices]
    return lax.ppermute(block, axis, route)


def entering_2(shard, axis, join, neutral):
    place = lax.axis_index(axis)
    gathered = jax.tree.map(
        lambda a, kind: lax.all_gather(a.astype(kind), axis), shard, (jnp.bfloat16, jnp.bfloat16)
    )
    state = jax.tree.map(lambda a, e: jnp.zeros_like(a) + jnp.asarray(e, a.dtype), shard, neutral)

    def one(hop, state):
        return join(
            state,
            jax.tree.map(
                lambda a, own: lax.dynamic_index_in_dim(a, hop, 0, False).astype(own.dtype),
                gathered,
                shard,
            ),
        )

    return lax.fori_loop(0, place, one, state)


def carried_in(shard, axis, combine, identity):
    length, here = (lax.axis_size(axis), lax.axis_index(axis))
    everything = jax.tree.map(
        lambda part, kind: lax.all_gather(part.astype(kind), axis),
        shard,
        jax.tree.map(lambda a: jnp.bfloat16 if a.dtype == jnp.float32 else a.dtype, shard),
    )
    start = jax.tree.map(
        lambda part, zero: jnp.broadcast_to(jnp.asarray(zero, part.dtype), part.shape),
        shard,
        identity,
    )

    def hop(k, before):
        at = length - 1 - k
        reached = at > here
        new = combine(
            before, jax.tree.map(lambda part, own: part[at].astype(own.dtype), everything, shard)
        )
        return jax.tree.map(lambda a, b: jnp.where(reached, a, b), new, before)

    return lax.fori_loop(0, length, hop, start)


def chain_link(earlier, later):
    return (earlier[0] * later[0], later[0][:, :, None, None] * earlier[1] + later[1])


def causal_mix(padded, seg_padded, kernel_w, kernel_b):
    margin = KERNEL - 1
    length = padded.shape[1] - margin
    seg_now = seg_padded[:, margin:]
    result = kernel_b + kernel_w[0] * padded[:, margin:]
    for offset in range(1, KERNEL):
        moved = padded[:, margin - offset : margin - offset + length]
        same_doc = (seg_padded[:, margin - offset : margin - offset + length] == seg_now).astype(
            jnp.float32
        )
        result = result + kernel_w[offset] * moved * same_doc[:, :, None]
    return result


def blocked(values, pieces):
    return values.reshape((values.shape[0], pieces, values.shape[1] // pieces) + values.shape[2:])


def block_sums(inner, deltas, log_decay, b_proj, seg_blocks, before):
    pieces = seg_blocks.shape[1]
    running = jnp.cumsum(blocked(log_decay, pieces), axis=2)
    same_end = (seg_blocks == seg_blocks[:, :, -1:]).astype(jnp.float32)
    to_end = (
        jnp.exp(running[:, :, -1:, :] - running) * same_end[:, :, :, None] * blocked(deltas, pieces)
    )
    inflow = jnp.einsum(
        "scjhp,scjn->schpn",
        to_end[..., None] * blocked(inner, pieces),
        blocked(b_proj, pieces),
        precision=HIGH,
    )
    passing = (
        jnp.exp(running[:, :, -1, :])
        * (seg_blocks[:, :, -1] == before).astype(jnp.float32)[:, :, None]
    )
    return (inflow, passing)


def state_reads(incoming, log_decay, c_proj, inflow, passing, seg_blocks, before):
    pieces = seg_blocks.shape[1]
    running = jnp.cumsum(blocked(log_decay, pieces), axis=2)
    memory = incoming
    entering = [memory]
    memory = passing[:, 0, :, None, None] * memory + inflow[:, 0]
    stacked = jnp.stack(entering, axis=1)
    entry = jnp.exp(running) * (seg_blocks == before[:, :, None]).astype(jnp.float32)[..., None]
    from_state = (
        jnp.einsum("scin,schpn->scihp", blocked(c_proj, pieces), stacked, precision=HIGH)
        * entry[..., None]
    )
    return (from_state, memory)


def per_device(
    tokens,
    segments,
    input_gain,
    gate_proj,
    inner_proj,
    state_proj,
    step_proj,
    conv_inner,
    inner_bias,
    conv_state,
    state_bias,
    step_bias,
    log_rates,
    skip_gain,
    gated_gain,
    output_proj,
    cotangent,
):
    tensor_count = lax.axis_size("tensor")
    tensor_rank = lax.axis_index("tensor")
    residual = tokens.astype(jnp.float32)
    rms_in = lax.rsqrt(jnp.mean(residual * residual, axis=-1, keepdims=True) + EPS)
    normed_own = (residual * rms_in * input_gain).astype(jnp.bfloat16)
    normed, cot_rows = (
        lax.all_gather(normed_own, "tensor", axis=1, tiled=True),
        lax.all_gather(cotangent, "tensor", axis=1, tiled=True),
    )
    gate_full, inner_full, state_full, step_full, output_full = (
        lax.all_gather(gate_proj, ("dp", "seq"), axis=0, tiled=True),
        lax.all_gather(inner_proj, ("dp", "seq"), axis=0, tiled=True),
        lax.all_gather(state_proj, ("dp", "seq"), axis=0, tiled=True),
        lax.all_gather(step_proj, ("dp", "seq"), axis=0, tiled=True),
        lax.all_gather(output_proj, ("dp", "seq"), axis=1, tiled=True),
    )
    gate_in = jnp.dot(normed, gate_full, preferred_element_type=jnp.float32)
    inner_low = jnp.dot(normed, inner_full, preferred_element_type=jnp.float32).astype(jnp.bfloat16)
    state_low = jnp.dot(normed, state_full, preferred_element_type=jnp.float32).astype(jnp.bfloat16)
    step_raw = jnp.dot(normed, step_full, preferred_element_type=jnp.float32)
    margin = KERNEL - 1
    seg_float = segments.astype(jnp.float32)
    prior_inner, prior_state, prior_seg = passed_along(
        (
            inner_low[:, -margin:],
            state_low[:, -margin:],
            seg_float[:, -margin:].astype(jnp.bfloat16),
        ),
        "seq",
        1,
    )
    padded_inner = jnp.concatenate([prior_inner, inner_low], axis=1).astype(jnp.float32)
    padded_state = jnp.concatenate([prior_state, state_low], axis=1).astype(jnp.float32)
    seg_padded = jnp.concatenate([prior_seg.astype(jnp.float32), seg_float], axis=1)
    pieces = segments.shape[1] // BLOCK
    seg_blocks = blocked(seg_float, pieces)
    before = jnp.concatenate(
        [prior_seg[:, -1:].astype(jnp.float32), seg_blocks[:, :-1, -1]], axis=1
    )
    width_here = inner_full.shape[1]
    heads_here = step_full.shape[1]
    chan_start = tensor_rank * width_here
    head_start = tensor_rank * heads_here
    kernel_here = lax.dynamic_slice_in_dim(conv_inner, chan_start, width_here, 1)
    bias_here = lax.dynamic_slice_in_dim(inner_bias, chan_start, width_here, 0)
    gain_here = lax.dynamic_slice_in_dim(gated_gain, chan_start, width_here, 0)
    shift_here = lax.dynamic_slice_in_dim(step_bias, head_start, heads_here, 0)
    rates_here = lax.dynamic_slice_in_dim(log_rates, head_start, heads_here, 0)
    skip_here = lax.dynamic_slice_in_dim(skip_gain, head_start, heads_here, 0)

    def mixer_front(
        pad_inner, pad_state, raw_steps, kernel_w, kernel_b, state_w, state_b, step_shift, rate_logs
    ):
        inner = jax.nn.silu(causal_mix(pad_inner, seg_padded, kernel_w, kernel_b))
        inner = inner.reshape(inner.shape[0], inner.shape[1], -1, HEAD_DIM)
        both_maps = jax.nn.silu(causal_mix(pad_state, seg_padded, state_w, state_b))
        b_proj = both_maps[:, :, :STATE]
        c_proj = both_maps[:, :, STATE:]
        deltas = jax.nn.softplus(raw_steps + step_shift)
        log_decay = deltas * -jnp.exp(rate_logs)
        inflow, passing = block_sums(inner, deltas, log_decay, b_proj, seg_blocks, before)
        return (inner, deltas, log_decay, b_proj, c_proj, inflow, passing)

    def mixer_rear(inner, deltas, log_decay, b_proj, c_proj, inflow, passing, incoming, skips):
        running = jnp.cumsum(blocked(log_decay, pieces), axis=2)
        places = jnp.arange(running.shape[2])
        allowed = (seg_blocks[:, :, :, None] == seg_blocks[:, :, None, :]) & (
            places[:, None] >= places[None, :]
        )
        inside = allowed[..., None]
        decays = jnp.where(
            inside,
            jnp.exp(jnp.where(inside, running[:, :, :, None, :] - running[:, :, None, :, :], 0.0)),
            0.0,
        )
        scores = jnp.einsum(
            "scin,scjn->scij", blocked(c_proj, pieces), blocked(b_proj, pieces), precision=HIGH
        )
        mixing = decays * scores[..., None] * blocked(deltas, pieces)[:, :, None, :, :]
        direct = jnp.einsum("scijh,scjhp->scihp", mixing, blocked(inner, pieces), precision=HIGH)
        from_state, outgoing = state_reads(
            incoming, log_decay, c_proj, inflow, passing, seg_blocks, before
        )
        heads_out = (direct + from_state).reshape(inner.shape) + skips[:, None] * inner
        return (heads_out.reshape(inner.shape[0], inner.shape[1], -1), outgoing)

    front_args = (
        padded_inner,
        padded_state,
        step_raw,
        kernel_here,
        bias_here,
        conv_state,
        state_bias,
        shift_here,
        rates_here,
    )
    front_vals = mixer_front(*front_args)
    inner, deltas, log_decay, b_proj, c_proj, inflow, passing = front_vals
    span_decay = jnp.ones(passing[:, 0].shape, jnp.float32)
    span_state = jnp.zeros(inflow[:, 0].shape, jnp.float32)
    span_state = passing[:, 0, :, None, None] * span_state + inflow[:, 0]
    span_decay = span_decay * passing[:, 0]
    identity = (jnp.ones_like(span_decay), jnp.zeros_like(span_state))
    incoming = entering_2((span_decay, span_state), "seq", chain_link, identity)[1]
    mixed, outgoing = mixer_rear(*front_vals, incoming, skip_here)
    sigmoid_z = jax.nn.sigmoid(gate_in)
    silu_z = gate_in * sigmoid_z
    gated = mixed * silu_z
    full_width = tensor_count * gated.shape[-1]
    square_sum = lax.psum(jnp.sum(gated * gated, axis=-1), "tensor")
    rms_gate = lax.rsqrt(square_sum / full_width + EPS)[..., None]
    gate_normed = (gated * rms_gate * gain_here).astype(jnp.bfloat16)
    partial_out = jnp.dot(gate_normed, output_full, preferred_element_type=jnp.float32)
    branch_rows = lax.psum_scatter(partial_out, "tensor", scatter_dimension=1, tiled=True)
    block_out = (residual + branch_rows).astype(jnp.bfloat16)
    grad_output = jnp.einsum(
        "srk,srd->kd", gate_normed, cot_rows, preferred_element_type=jnp.float32
    )
    grad_gn = jnp.einsum("srd,kd->srk", cot_rows, output_full, preferred_element_type=jnp.float32)
    scaled = grad_gn * gain_here
    dot_sum = lax.psum(jnp.sum(scaled * gated, axis=-1), "tensor")
    grad_gain_here = jnp.sum(grad_gn * gated * rms_gate, axis=(0, 1))
    grad_gated = rms_gate * scaled - gated * rms_gate**3 * (dot_sum / full_width)[..., None]
    grad_mixed = grad_gated * silu_z
    grad_gate_in = (grad_gated * mixed * sigmoid_z * (1.0 + gate_in * (1.0 - sigmoid_z))).astype(
        jnp.bfloat16
    )
    front_vals, front_back = jax.vjp(mixer_front, *front_args)
    unused_rear, rear_back = jax.vjp(mixer_rear, *front_vals, incoming, skip_here)
    inner, deltas, log_decay, b_proj, c_proj, inflow, passing = front_vals
    grad_blocks = blocked(grad_mixed.reshape(inner.shape), pieces)
    unused_reads, read_back = jax.vjp(
        lambda memory_in: state_reads(
            memory_in, log_decay, c_proj, inflow, passing, seg_blocks, before
        )[0],
        incoming,
    )
    local_grad = read_back(grad_blocks)[0]
    outgoing_grad = carried_in((span_decay, local_grad), "seq", chain_link, identity)[1]
    rear_grads = rear_back((grad_mixed, outgoing_grad))
    grad_skip_here = rear_grads[8]
    (
        pad_grad_inner,
        pad_grad_state,
        grad_step_raw,
        grad_kernel_here,
        grad_bias_here,
        grad_conv_state,
        grad_state_bias,
        grad_shift_here,
        grad_rates_here,
    ) = front_back(tuple(rear_grads[:7]))
    from_next_inner, from_next_state = passed_along(
        (pad_grad_inner[:, :margin], pad_grad_state[:, :margin]), "seq", -1
    )
    grad_inner_pre = jnp.concatenate(
        [pad_grad_inner[:, margin:-margin], pad_grad_inner[:, -margin:] + from_next_inner], axis=1
    )
    grad_state_part = jnp.concatenate(
        [pad_grad_state[:, margin:-margin], pad_grad_state[:, -margin:] + from_next_state], axis=1
    )
    grad_state_pre = lax.psum(grad_state_part, "tensor").astype(jnp.bfloat16)
    grad_inner_low = grad_inner_pre.astype(jnp.bfloat16)
    grad_step_low = grad_step_raw.astype(jnp.bfloat16)
    grad_normed = jnp.einsum(
        "srk,dk->srd", grad_gate_in, gate_full, preferred_element_type=jnp.float32
    )
    grad_normed = grad_normed + jnp.einsum(
        "srk,dk->srd", grad_inner_low, inner_full, preferred_element_type=jnp.float32
    )
    grad_normed = grad_normed + jnp.einsum(
        "srk,dk->srd", grad_step_low, step_full, preferred_element_type=jnp.float32
    )
    grad_rows = lax.psum_scatter(grad_normed, "tensor", scatter_dimension=1, tiled=True)
    own_rows = tokens.shape[1]
    state_mine = lax.dynamic_slice_in_dim(grad_state_pre, tensor_rank * own_rows, own_rows, 1)
    grad_rows = grad_rows + jnp.einsum(
        "srk,dk->srd", state_mine, state_full, preferred_element_type=jnp.float32
    )
    grad_gate_w = jnp.einsum(
        "srd,srk->dk", normed, grad_gate_in, preferred_element_type=jnp.float32
    )
    grad_inner_w = jnp.einsum(
        "srd,srk->dk", normed, grad_inner_low, preferred_element_type=jnp.float32
    )
    grad_state_w = jnp.einsum(
        "srd,srk->dk", normed, grad_state_pre, preferred_element_type=jnp.float32
    )
    grad_step_w = jnp.einsum(
        "srd,srk->dk", normed, grad_step_low, preferred_element_type=jnp.float32
    )
    shard_gate, shard_inner, shard_state, shard_step, shard_output = (
        lax.psum_scatter(grad_gate_w, ("dp", "seq"), scatter_dimension=0, tiled=True),
        lax.psum_scatter(grad_inner_w, ("dp", "seq"), scatter_dimension=0, tiled=True),
        lax.psum_scatter(grad_state_w, ("dp", "seq"), scatter_dimension=0, tiled=True),
        lax.psum_scatter(grad_step_w, ("dp", "seq"), scatter_dimension=0, tiled=True),
        lax.psum_scatter(grad_output, ("dp", "seq"), scatter_dimension=1, tiled=True),
    )
    scaled_in = grad_rows * input_gain
    grad_input_gain = jnp.sum(grad_rows * residual * rms_in, axis=(0, 1))
    grad_tokens = (
        cotangent.astype(jnp.float32)
        + rms_in * scaled_in
        - residual * rms_in**3 * jnp.mean(scaled_in * residual, axis=-1, keepdims=True)
    )

    def placed(whole, piece_grad, start, axis_number):
        return lax.dynamic_update_slice_in_dim(
            jnp.zeros_like(whole), piece_grad, start, axis_number
        )

    smalls = lax.psum(
        (
            grad_input_gain,
            placed(conv_inner, grad_kernel_here, chan_start, 1),
            placed(inner_bias, grad_bias_here, chan_start, 0),
            grad_conv_state,
            grad_state_bias,
            placed(step_bias, grad_shift_here, head_start, 0),
            placed(log_rates, grad_rates_here, head_start, 0),
            placed(skip_gain, grad_skip_here, head_start, 0),
            placed(gated_gain, grad_gain_here, chan_start, 0),
        ),
        ("dp", "seq", "tensor"),
    )
    return (
        block_out,
        grad_tokens,
        smalls[0],
        shard_gate,
        shard_inner,
        shard_state,
        shard_step,
        smalls[1],
        smalls[2],
        smalls[3],
        smalls[4],
        smalls[5],
        smalls[6],
        smalls[7],
        smalls[8],
        shard_output,
    )


def solution(mesh):
    placed = (
        P("dp", ("seq", "tensor"), None),
        P("dp", "seq"),
        P(),
        P(("dp", "seq"), "tensor"),
        P(("dp", "seq"), "tensor"),
        P(("dp", "seq"), None),
        P(("dp", "seq"), "tensor"),
        P(),
        P(),
        P(),
        P(),
        P(),
        P(),
        P(),
        P(),
        P("tensor", ("dp", "seq")),
        P("dp", ("seq", "tensor"), None),
    )
    return jax.shard_map(
        per_device,
        mesh=mesh,
        in_specs=placed,
        out_specs=(
            P("dp", ("seq", "tensor"), None),
            P("dp", ("seq", "tensor"), None),
            P(),
            P(("dp", "seq"), "tensor"),
            P(("dp", "seq"), "tensor"),
            P(("dp", "seq"), None),
            P(("dp", "seq"), "tensor"),
            P(),
            P(),
            P(),
            P(),
            P(),
            P(),
            P(),
            P(),
            P("tensor", ("dp", "seq")),
        ),
        check_vma=False,
    )
```

profile of v0, /device:TPU:0, one launch (start us, length us, event | category | flops | bytes accessed | tf_op | source)
XLA Modules:
  0.0 836.2 jit_solution(3779227781878507344)
XLA Ops:
  18.4 10.1 %all-gather.2 = bf16[8,192,12]{1,2,0:T(8,128)(2,1)S(1)} all-gather(bf16[1,192,12]{1,2,0:T(8,128)(2,1)S(1)} %bitcast.296), channel_id=1, replica_groups=mesh['dp'=4,'seq'=2,'tensor'=4] {'dp','seq'}, dimensions={0}, use_global_device_ids=true | all-gather | bytes 41472 | tf_op jit(solution)/shard_map/all_gather | solution.py:155
  29.4 10.4 %all_gather.38 = bf16[1536,256]{1,0:T(8,128)(2,1)S(1)} all-gather(bf16[192,256]{1,0:T(8,128)(2,1)S(1)} %copy-done.32), channel_id=1, replica_groups=mesh['dp'=4,'seq'=2,'tensor'=4] {'dp','seq'}, dimensions={0}, use_global_device_ids=true | all-gather | bytes 884736 | tf_op jit(solution)/shard_map/all_gather | solution.py:154
  41.1 10.2 %all-gather.9.cloned.1.call-done = bf16[2,256,1536]{2,1,0:T(8,128)(2,1)} async-done(((bf16[2,64,1536]{2,1,0:T(8,128)(2,1)}), bf16[2,256,1536]{2,1,0:T(8,128)(2,1)}) %all-gather.9.cloned.1.call-update) | async-done | bytes 1572880 | tf_op jit(solution)/shard_map/all_gather | solution.py:148
  62.0 19.0 %all-gather.11.cloned.1.call-done = bf16[1536,768]{1,0:T(8,128)(2,1)} async-done(((bf16[192,768]{1,0:T(8,128)(2,1)}), bf16[1536,768]{1,0:T(8,128)(2,1)}) %all-gather.11.cloned.1.call-update) | async-done | bytes 2359312 | tf_op jit(solution)/shard_map/all_gather | solution.py:153
  101.8 8.4 %bitcast_add_fusion = f32[2,1,256,12,64]{2,4,3,0,1:T(8,128)} fusion(f32[2,256,12,64]{1,3,2,0:T(8,128)S(1)} %fusion.85, f32[2,256,12,64]{1,3,2,0:T(8,128)S(1)} %bitcast.274, f32[2,256,12]{1,2,0:T(8,128)S(1)} %get-tuple-element.300, f32[2,256,256]{2,1,0:T(8,128)S(1)} %copy-done.28, f32[2,256,12]{1,2,0:T(8,128)S(1)} %fusion.108, ...), kind=kOutput, calls=%fused_computation.59 | convolution fusion | flops 1216610304 | bytes 5447680 | tf_op jit(solution)/shard_map/scijh,scjhp->scihp/dot_general | solution.py:221
  113.4 6.6 multiply_reduce_fusion.9
  119.9 12.2 %psum.84 = f32[2,256]{1,0:T(2,128)S(1)} all-reduce(f32[2,256]{1,0:T(2,128)S(1)} %get-tuple-element.279), channel_id=1, replica_groups=mesh['dp'=4,'seq'=2,'tensor'=4] {'tensor'}, use_global_device_ids=true, to_apply=%region_6.7 | all-reduce | flops 512 | bytes 4096 | tf_op jit(solution)/shard_map/psum | solution.py:252
  132.2 18.4 %all-gather.17.cloned.1.call-done = bf16[2,256,1536]{2,1,0:T(8,128)(2,1)} async-done(((bf16[2,64,1536]{2,1,0:T(8,128)(2,1)}), bf16[2,256,1536]{2,1,0:T(8,128)(2,1)}) %all-gather.17.cloned.1.call-update) | async-done | bytes 1572880 | tf_op jit(solution)/shard_map/all_gather | solution.py:149
  150.6 29.5 %all-gather.15.cloned.1.call-done = bf16[768,1536]{0,1:T(8,128)(2,1)} async-done(((bf16[768,192]{0,1:T(8,128)(2,1)}), bf16[768,1536]{0,1:T(8,128)(2,1)}) %all-gather.15.cloned.1.call-update) | async-done | bytes 2359312 | tf_op jit(solution)/shard_map/all_gather | solution.py:156
  180.1 5.8 multiply_reduce_fusion.1
  185.9 12.1 %psum.85 = f32[2,256]{1,0:T(2,128)S(1)} all-reduce(f32[2,256]{1,0:T(2,128)S(1)} %get-tuple-element.221), channel_id=1, replica_groups=mesh['dp'=4,'seq'=2,'tensor'=4] {'tensor'}, use_global_device_ids=true, to_apply=%region_9.10 | all-reduce | flops 512 | bytes 4096 | tf_op jit(solution)/shard_map/psum | solution.py:263
  197.9 5.6 multiply_reduce_fusion.2
  211.4 11.0 %fusion.6 = (f32[2,256,12]{1,2,0:T(8,128)S(1)}, f32[2,256,12]{1,2,0:T(8,128)S(1)}, f32[2,256,12]{1,2,0:T(8,128)}, f32[2,256,256]{2,1,0:T(8,128)}) fusion(f32[2,256,12]{1,2,0:T(8,128)S(1)} %get-tuple-element.300, f32[2,256,256]{2,1,0:T(8,128)S(1)} %copy-done.29, f32[2,256,12]{1,2,0:T(8,128)S(1)} %copy-done.51, pred[2,256,256]{2,1,0:T(8,128)(4,1)S(1)} %copy-done.31, ...), kind=kOutput, calls=%fused_computation.20 | convolution fusion | flops 1231403008 | bytes 4448256 | tf_op jit(solution)/shard_map/transpose(jvp(scijh,scjhp->scihp))/dot_general | solution.py:221
  222.3 6.7 fusion.3
  229.1 5.0 reduce-window.34
  235.4 6.3 all-gather.1
  256.4 5.0 reduce-window.36
  261.5 5.0 reduce-window.30
  275.3 4.3 multiply_reduce_fusion.6
  294.3 5.8 fusion.21
  300.2 4.2 fusion.55
  313.4 43.6 %all-reduce.25 = bf16[2,256,256]{2,1,0:T(8,128)(2,1)S(1)} all-reduce(f32[2,256,256]{2,1,0:T(8,128)S(1)} %pad_maximum_fusion.1), channel_id=1, replica_groups=mesh['dp'=4,'seq'=2,'tensor'=4] {'tensor'}, use_global_device_ids=true, to_apply=%region_27.28 | all-reduce | flops 131072 | bytes 786432 | tf_op jit(solution)/shard_map/psum | solution.py:304
  382.7 5.0 convolution_bitcast_fusion
  388.8 3.6 convolution_bitcast_fusion.2
  393.6 3.7 convolution_bitcast_fusion.1
  397.3 7.1 reduce-scatter.22.cloned.1.call-done
  406.0 61.1 %reduce-scatter.10.cloned.1.call-done = f32[2,64,1536]{2,1,0:T(8,128)} async-done(((f32[2,256,1536]{2,1,0:T(8,128)}), f32[2,64,1536]{2,1,0:T(8,128)}) %reduce-scatter.10.cloned.1.call-update) | async-done | bytes 786448 | tf_op jit(solution)/shard_map/reduce_scatter | solution.py:256
  469.7 39.6 %reduce-scatter.18.cloned.1.call-done = f32[192,256]{1,0:T(8,128)} async-done(((f32[1536,256]{1,0:T(8,128)}), f32[192,256]{1,0:T(8,128)}) %reduce-scatter.18.cloned.1.call-update) | async-done | bytes 196624 | tf_op jit(solution)/shard_map/reduce_scatter | solution.py:337
  509.3 134.3 %all-reduce.24.cloned.1.call-done = (f32[1536]{0:T(1024)}, f32[4,3072]{1,0:T(4,128)}, f32[3072]{0:T(1024)}, f32[4,256]{1,0:T(4,128)}, f32[256]{0:T(256)}, /*inde...) async-done(((f32[1536]{0:T(1024)}, f32[4,3072]{1,0:T(4,128)}, f32[3072]{0:T(1024)}, f32[4,256]{1,0:T(4,128)}, f32[256]{0:T(256)}, /*index=5*/f32[48]{0:T(128)}, ...) | async-done | bytes 85584 | tf_op jit(solution)/shard_map/psum | solution.py:354
  643.5 58.9 %reduce-scatter.20.cloned.1.call-done = f32[768,192]{0,1:T(8,128)} async-done(((f32[768,1536]{0,1:T(8,128)}), f32[768,192]{0,1:T(8,128)}) %reduce-scatter.20.cloned.1.call-update) | async-done | bytes 589840 | tf_op jit(solution)/shard_map/reduce_scatter | solution.py:339
  702.4 57.7 %reduce-scatter.14.cloned.1.call-done = f32[192,768]{1,0:T(8,128)} async-done(((f32[1536,768]{1,0:T(8,128)}), f32[192,768]{1,0:T(8,128)}) %reduce-scatter.14.cloned.1.call-update) | async-done | bytes 589840 | tf_op jit(solution)/shard_map/reduce_scatter | solution.py:335
  760.1 57.8 %reduce-scatter.16.cloned.1.call-done = f32[192,768]{1,0:T(8,128)} async-done(((f32[1536,768]{1,0:T(8,128)}), f32[192,768]{1,0:T(8,128)}) %reduce-scatter.16.cloned.1.call-update) | async-done | bytes 589840 | tf_op jit(solution)/shard_map/reduce_scatter | solution.py:336
  (370 shorter events, 149.2 us)
Async XLA Ops:
  7.2 44.1 %all-gather.9.cloned.1.call-start = ((), (), s32[]{:S(2)}) async-start(), calls=%async_computation.7 | async-start | bytes 1966080 | tf_op jit(solution)/shard_map/all_gather | solution.py:148
  11.5 69.6 %all-gather.11.cloned.1.call-start = ((), (), s32[]{:S(2)}) async-start(), calls=%async_computation.8 | async-start | bytes 2654208 | tf_op jit(solution)/shard_map/all_gather | solution.py:153
  12.2 101.1 %all-gather.13.cloned.1.call-start = ((), (), s32[]{:S(2)}) async-start(), calls=%async_computation.9 | async-start | bytes 2654208 | tf_op jit(solution)/shard_map/all_gather | solution.py:152
  13.0 137.6 %all-gather.17.cloned.1.call-start = ((), (), s32[]{:S(2)}) async-start(), calls=%async_computation.12 | async-start | bytes 1966080 | tf_op jit(solution)/shard_map/all_gather | solution.py:149
  13.5 166.6 %all-gather.15.cloned.1.call-start = ((), (), s32[]{:S(2)}) async-start(), calls=%async_computation.10 | async-start | bytes 2654208 | tf_op jit(solution)/shard_map/all_gather | solution.py:156
  13.7 27.1 %collective-permute-start.1 = (bf16[2,3]{1,0:T(2,128)(2,1)S(1)}, bf16[2,3]{1,0:T(2,128)(2,1)S(1)}, u32[]{:S(2)}, u32[]{:S(2)}) collective-permute-start(bf16[2,3]{1,0:T(2,128)(2,1)S(1)} %slice.305), channel_id=1, source_target_pairs={{0,4},{1,5},{2,6},{3,7},{8,12},{9,13},{10,14},{11,15},{16,20},{17,... | collective-permute-start | bytes 44 | tf_op jit(solution)/shard_map/ppermute | solution.py:19
  16.1 362.8 %reduce-scatter.12.cloned.1.call-start = ((), (), s32[]{:S(2)}) async-start(), calls=%async_computation.13 | async-start | bytes 3932160 | tf_op jit(solution)/shard_map/reduce_scatter | solution.py:316
  16.3 37.7 %copy-start.78 = (f32[12]{0:T(128)}, f32[12]{0:T(128)S(1)}, u32[]{:S(2)}) copy-start(f32[12]{0:T(128)S(1)} %fusion.120) | copy-start | bytes 148
  18.0 42.0 %copy-start.62 = (f32[1,256]{1,0:T(1,128)}, f32[1,256]{1,0:T(1,128)S(1)}, u32[]{:S(2)}) copy-start(f32[1,256]{1,0:T(1,128)S(1)} %get-tuple-element.303) | copy-start | bytes 3076
  18.0 42.1 %copy-start.64 = (f32[1,256]{1,0:T(1,128)}, f32[1,256]{1,0:T(1,128)S(1)}, u32[]{:S(2)}) copy-start(f32[1,256]{1,0:T(1,128)S(1)} %get-tuple-element.304) | copy-start | bytes 3076
  18.0 42.1 %copy-start.66 = (f32[1,256]{1,0:T(1,128)}, f32[1,256]{1,0:T(1,128)S(1)}, u32[]{:S(2)}) copy-start(f32[1,256]{1,0:T(1,128)S(1)} %get-tuple-element.305) | copy-start | bytes 3076
  18.0 42.1 %copy-start.68 = (f32[1,256]{1,0:T(1,128)}, f32[1,256]{1,0:T(1,128)S(1)}, u32[]{:S(2)}) copy-start(f32[1,256]{1,0:T(1,128)S(1)} %get-tuple-element.306) | copy-start | bytes 3076
  40.7 47.1 %copy-start.41 = (f32[768]{0:T(1024)}, f32[768]{0:T(1024)S(1)}, u32[]{:S(2)}) copy-start(f32[768]{0:T(1024)S(1)} %get-tuple-element.232) | copy-start | bytes 9220
  40.8 47.1 %copy-start.43 = (f32[768]{0:T(1024)}, f32[768]{0:T(1024)S(1)}, u32[]{:S(2)}) copy-start(f32[768]{0:T(1024)S(1)} %get-tuple-element.233) | copy-start | bytes 9220
  55.8 46.0 %copy-start.50 = (f32[2,256,12]{1,2,0:T(8,128)}, f32[2,256,12]{1,2,0:T(8,128)S(1)}, u32[]{:S(2)}) copy-start(f32[2,256,12]{1,2,0:T(8,128)S(1)} %fusion.108) | copy-start | bytes 73732
  56.6 3.3 collective-permute-start.2
  84.1 3.6 collective-permute-start
  132.2 65.8 %copy-start.45 = (f32[2,256]{1,0:T(2,128)}, f32[2,256]{1,0:T(2,128)S(1)}, u32[]{:S(2)}) copy-start(f32[2,256]{1,0:T(2,128)S(1)} %get-tuple-element.311) | copy-start | bytes 6148
  280.3 5.2 collective-permute-start.3
  291.1 113.3 %reduce-scatter.22.cloned.1.call-start = ((), (), s32[]{:S(2)}) async-start(), calls=%async_computation.18 | async-start | bytes 884736
  294.0 173.1 %reduce-scatter.10.cloned.1.call-start = ((), (), s32[]{:S(2)}) async-start(), calls=%async_computation.11 | async-start | bytes 3932160 | tf_op jit(solution)/shard_map/reduce_scatter | solution.py:256
  300.1 209.2 %reduce-scatter.18.cloned.1.call-start = ((), (), s32[]{:S(2)}) async-start(), calls=%async_computation.16 | async-start | bytes 1769472 | tf_op jit(solution)/shard_map/reduce_scatter | solution.py:337
  310.2 3.1 collective-permute-start.4
  311.8 45.2 %copy-start.8 = (bf16[2,256,1536]{2,1,0:T(8,128)(2,1)S(1)}, bf16[2,256,1536]{2,1,0:T(8,128)(2,1)}, u32[]{:S(2)}) copy-start(bf16[2,256,1536]{2,1,0:T(8,128)(2,1)} %all-gather.9.cloned.1.call-done) | copy-start | bytes 4718596
  358.8 284.7 %all-reduce.24.cloned.1.call-start = ((), (), s32[]{:S(2)}) async-start(), calls=%async_computation.19 | async-start | bytes 177152 | tf_op jit(solution)/shard_map/psum | solution.py:354
  382.4 320.0 %reduce-scatter.20.cloned.1.call-start = ((), (), s32[]{:S(2)}) async-start(), calls=%async_computation.17 | async-start | bytes 5308416 | tf_op jit(solution)/shard_map/reduce_scatter | solution.py:339
  387.7 372.4 %reduce-scatter.14.cloned.1.call-start = ((), (), s32[]{:S(2)}) async-start(), calls=%async_computation.14 | async-start | bytes 5308416 | tf_op jit(solution)/shard_map/reduce_scatter | solution.py:335
  392.5 425.5 %reduce-scatter.16.cloned.1.call-start = ((), (), s32[]{:S(2)}) async-start(), calls=%async_computation.15 | async-start | bytes 5308416 | tf_op jit(solution)/shard_map/reduce_scatter | solution.py:336
  397.2 69.9 %copy-start.19 = (f32[2,64,1536]{2,1,0:T(8,128)S(1)}, f32[2,64,1536]{2,1,0:T(8,128)}, u32[]{:S(2)}) copy-start(f32[2,64,1536]{2,1,0:T(8,128)} %get-tuple-element.321) | copy-start | bytes 2359300
  397.2 69.9 %copy-start.24 = (bf16[2,64,1536]{2,1,0:T(8,128)(2,1)S(1)}, bf16[2,64,1536]{2,1,0:T(8,128)(2,1)}, u32[]{:S(2)}) copy-start(bf16[2,64,1536]{2,1,0:T(8,128)(2,1)} %param.37) | copy-start | bytes 1179652
  397.2 69.9 %copy-start.59 = (f32[2,64]{1,0:T(2,128)S(1)}, f32[2,64]{1,0:T(2,128)}, u32[]{:S(2)}) copy-start(f32[2,64]{1,0:T(2,128)} %copy-done.58) | copy-start | bytes 1540
  397.2 69.9 %copy-start.75 = (f32[2,64]{1,0:T(2,128)S(1)}, f32[2,64]{1,0:T(2,128)}, u32[]{:S(2)}) copy-start(f32[2,64]{1,0:T(2,128)} %get-tuple-element.316) | copy-start | bytes 1540
  (71 other events, 375.0 us)
Sparse Core Ops, SparseCore 0:
  11.6 39.7 all-gather.8
  53.2 27.7 all-gather.10
  82.9 28.8 all-gather.12
  113.3 37.2 all-gather.16
  152.3 27.7 all-gather.14
  291.2 75.0 reduce-scatter.11
  369.5 34.8 reduce-scatter.21
  406.7 60.3 reduce-scatter.9
  471.0 38.2 reduce-scatter.17
  516.7 126.8 all-reduce.23
  647.6 54.7 reduce-scatter.19
  706.3 53.7 reduce-scatter.13
  764.1 53.7 reduce-scatter.15
where the time goes:
time: 845 us; the launch traced here: 836 us
  waiting for transfers between devices  497 us (59%)
  blocking collectives  98.9 us (12%)
  matrix products  94.8 us (11%)
  local copies, waits for them, and re-layouts  62 us (7%)
  other arithmetic  57.8 us (7%)
  between operations  15.6 us (2%)
  starting transfers between devices  9.65 us (1%)
    psum x1, waiting for transfers between devices, per_device(): lax.psum((grad_input_gain, placed(conv_inner, grad_kernel_here, chan_star...  134 us
    reduce_scatter x1, waiting for transfers between devices, per_device(): lax.psum_scatter(partial_out, 'tensor', scatter_dimension=1, tiled=True)  61.1 us
    reduce_scatter x1, waiting for transfers between devices, per_device(): lax.psum_scatter(grad_output, ('dp', 'seq'), scatter_dimension=1, tiled=T...  58.9 us
    reduce_scatter x1, waiting for transfers between devices, per_device(): lax.psum_scatter(grad_inner_w, ('dp', 'seq'), scatter_dimension=0, tiled=...  57.8 us
    reduce_scatter x1, waiting for transfers between devices, per_device(): lax.psum_scatter(grad_gate_w, ('dp', 'seq'), scatter_dimension=0, tiled=T...  57.7 us
    psum x1, blocking collectives, per_device(): grad_state_pre = lax.psum(grad_state_part, 'tensor').astype(jnp.bfloat16)  43.6 us
    reduce_scatter x1, waiting for transfers between devices, per_device(): lax.psum_scatter(grad_state_w, ('dp', 'seq'), scatter_dimension=0, tiled=...  39.6 us
    all_gather x1, waiting for transfers between devices, per_device(): lax.all_gather(output_proj, ('dp', 'seq'), axis=1, tiled=True)  29.5 us
  transfers between devices with their start and end apart: 18, of which 12 were waited for; matrix products, arithmetic and copies ran while one was open for 13% of the time, Pallas kernels for 0%

commit v1 on v0

--- a/solution.py
+++ b/solution.py
@@ -1,6 +1,10 @@
+import functools
+
 import jax
 import jax.numpy as jnp
 from jax import lax
+from jax.experimental import pallas as pl
+from jax.experimental.pallas import tpu as pltpu
 from jax.sharding import PartitionSpec as P
 
 HEAD_DIM = 64
@@ -118,6 +122,1291 @@
         * entry[..., None]
     )
     return (from_state, memory)
+
+
+MESH = pl.DeviceIdType.MESH
+BF = jnp.bfloat16
+F32 = jnp.float32
+
+
+def _peers():
+    dp, seq, t = lax.axis_index("dp"), lax.axis_index("seq"), lax.axis_index("tensor")
+    x, y = lax.rem(dp, 2), lax.div(dp, 2)
+    x_dp = dp + 1 - 2 * x
+    y_dp = dp + 2 - 4 * y
+    d_dp = 3 - dp
+    return dp, seq, t, x_dp, y_dp, d_dp
+
+
+def _dev(dp, seq, t):
+    return {"dp": dp, "seq": seq, "tensor": t}
+
+
+def _plane_barrier(n):
+    dp, seq, t, x_dp, y_dp, d_dp = _peers()
+    bar = pltpu.get_barrier_semaphore()
+    for who in (_dev(dp, 1 - seq, t), _dev(x_dp, seq, t), _dev(y_dp, seq, t)):
+        pl.semaphore_signal(bar, inc=1, device_id=who, device_id_type=MESH)
+
+    for step in range(1, n):
+        pl.semaphore_signal(
+            bar, inc=1, device_id=_dev(dp, seq, lax.rem(t + step, n)), device_id_type=MESH
+        )
+    pl.semaphore_wait(bar, 3 + n - 1)
+
+
+class _Line:
+    def __init__(self, n, ref, rows, ssem, rsem, own=None):
+        self.n, self.ref, self.rows, self.ssem, self.rsem = n, ref, rows, ssem, rsem
+        self.own = own
+
+    def block(self, o):
+        return self.ref.at[:, pl.ds(pl.multiple_of(o * self.rows, self.rows), self.rows), :]
+
+    def copy(self, o, direction, own=False):
+        dp, seq, t = lax.axis_index("dp"), lax.axis_index("seq"), lax.axis_index("tensor")
+        return pltpu.make_async_remote_copy(
+            src_ref=self.own if own else self.block(o),
+            dst_ref=self.block(o),
+            send_sem=self.ssem.at[0 if direction > 0 else 1, o],
+            recv_sem=self.rsem.at[o],
+            device_id=_dev(dp, seq, t + direction),
+            device_id_type=MESH,
+        )
+
+    def step(self, d):
+        n, t = self.n, lax.axis_index("tensor")
+        for way in (1, -1):
+            o = t - way * d
+            here = jnp.logical_and(o >= 0, o < n)
+            nxt = jnp.logical_and(t + way >= 0, t + way < n)
+
+            @pl.when(here)
+            def _(o=o, way=way, nxt=nxt):
+                if d > 0:
+                    self.copy(o, way).wait_recv()
+
+                @pl.when(nxt)
+                def _():
+                    self.copy(o, way, d == 0 and self.own is not None).start()
+
+    def finish(self):
+        n, t = self.n, lax.axis_index("tensor")
+        for d in range(n):
+            for way in (1, -1):
+                o = t - way * d
+                ok = jnp.logical_and(
+                    jnp.logical_and(o >= 0, o < n),
+                    jnp.logical_and(t + way >= 0, t + way < n),
+                )
+
+                @pl.when(ok)
+                def _(o=o, way=way):
+                    self.copy(o, way).wait_send()
+
+
+class _Plane:
+    def __init__(self, own, full, ssem, rsem, lsem):
+        self.own, self.full, self.ssem, self.rsem, self.lsem = own, full, ssem, rsem, lsem
+
+    def copy(self, src, block, who, s):
+        return pltpu.make_async_remote_copy(
+            src_ref=src,
+            dst_ref=self.full.at[block],
+            send_sem=self.ssem.at[s],
+            recv_sem=self.rsem.at[s],
+            device_id=who,
+            device_id_type=MESH,
+        )
+
+    def begin(self):
+        dp, seq, t, x_dp, y_dp, d_dp = _peers()
+        me = dp * 2 + seq
+        pltpu.make_async_copy(self.own, self.full.at[me], self.lsem).start()
+        self.copy(self.own, me, _dev(x_dp, seq, t), 0).start()
+        self.copy(self.own, me, _dev(y_dp, seq, t), 1).start()
+        self.copy(self.own, me, _dev(dp, 1 - seq, t), 3).start()
+
+    def forward(self):
+        dp, seq, t, x_dp, y_dp, d_dp = _peers()
+        bx, by = x_dp * 2 + seq, y_dp * 2 + seq
+        self.copy(self.own, bx, _dev(x_dp, seq, t), 0).wait_recv()
+        self.copy(self.own, by, _dev(y_dp, seq, t), 1).wait_recv()
+
+        @pl.when(seq == 0)
+        def _():
+            self.copy(self.full.at[by], by, _dev(x_dp, seq, t), 2).start()
+
+        @pl.when(seq == 1)
+        def _():
+            self.copy(self.full.at[bx], bx, _dev(y_dp, seq, t), 2).start()
+
+        self.copy(self.full.at[bx], bx, _dev(dp, 1 - seq, t), 4).start()
+        self.copy(self.full.at[by], by, _dev(dp, 1 - seq, t), 5).start()
+
+    def share(self):
+        dp, seq, t, x_dp, y_dp, d_dp = _peers()
+        bd = d_dp * 2 + seq
+        self.copy(self.own, bd, _dev(x_dp, seq, t), 2).wait_recv()
+        self.copy(self.full.at[bd], bd, _dev(dp, 1 - seq, t), 6).start()
+
+    def arrive(self):
+        dp, seq, t, x_dp, y_dp, d_dp = _peers()
+        me = dp * 2 + seq
+        pltpu.make_async_copy(self.own, self.full.at[me], self.lsem).wait()
+        for s in (3, 4, 5, 6):
+            self.copy(self.own, me, _dev(dp, 1 - seq, t), s).wait_recv()
+
+    def finish(self):
+        dp, seq, t, x_dp, y_dp, d_dp = _peers()
+        me = dp * 2 + seq
+        for s in range(7):
+            self.copy(self.own, me, _dev(dp, 1 - seq, t), s).wait_send()
+
+
+def gather_kernel(n, tok, gain, wg, wi, ws, wt, normed, fg, fi, fs, ft, zs, zr, ps, pr, ls):
+    t = lax.axis_index("tensor")
+    rows = tok.shape[1]
+    _plane_barrier(n)
+    planes = [
+        _Plane(own, full, ps.at[i], pr.at[i], ls.at[i])
+        for i, (own, full) in enumerate(((ws, fs), (wt, ft), (wi, fi), (wg, fg)))
+    ]
+    for p in planes[:3]:
+        p.begin()
+    mine = pl.ds(pl.multiple_of(t * rows, rows), rows)
+    for s in range(tok.shape[0]):
+        v = tok[s].astype(F32)
+        rms = lax.rsqrt(jnp.mean(v * v, axis=-1, keepdims=True) + EPS)
+        normed[s, mine, :] = (v * rms * gain[...]).astype(BF)
+    a = _Line(n, normed, rows, zs, zr)
+    a.step(0)
+    planes[3].begin()
+    for p in planes[:3]:
+        p.forward()
+    a.step(1)
+    planes[3].forward()
+    for p in planes[:3]:
+        p.share()
+    for d in range(2, n):
+        a.step(d)
+    planes[3].share()
+    for p in planes:
+        p.arrive()
+    a.finish()
+    for p in planes:
+        p.finish()
+
+
+def gather_all(n, tokens, gain, weights):
+    seqs, rows, width = tokens.shape
+    vm = pl.BlockSpec(memory_space=pltpu.VMEM)
+    full = lambda w: jax.ShapeDtypeStruct((8,) + w.shape, w.dtype)
+    act = jax.ShapeDtypeStruct((seqs, n * rows, width), BF)
+    return pl.pallas_call(
+        functools.partial(gather_kernel, n),
+        out_shape=(act,) + tuple(full(w) for w in weights),
+        in_specs=[vm] * 6,
+        out_specs=(vm,) * 5,
+        scratch_shapes=[
+            pltpu.SemaphoreType.DMA((2, n)),
+            pltpu.SemaphoreType.DMA((n,)),
+            pltpu.SemaphoreType.DMA((4, 7)),
+            pltpu.SemaphoreType.DMA((4, 7)),
+            pltpu.SemaphoreType.DMA((4,)),
+        ],
+        compiler_params=pltpu.CompilerParams(
+            collective_id=0, has_side_effects=True, vmem_limit_bytes=60 << 20
+        ),
+        name="gather_all",
+    )(tokens, gain.reshape(1, width), *weights)
+
+
+def _line_reduce(n, part, left, right, ssem, rsem):
+    dp, seq, t = lax.axis_index("dp"), lax.axis_index("seq"), lax.axis_index("tensor")
+    rows = left.shape[2]
+
+    def copy(src, box, o, way):
+        return pltpu.make_async_remote_copy(
+            src_ref=src, dst_ref=box.at[o],
+            send_sem=ssem.at[0 if way > 0 else 1, o], recv_sem=rsem.at[0 if way > 0 else 1, o],
+            device_id=_dev(dp, seq, t + way), device_id_type=MESH,
+        )
+
+    def block(o):
+        return part.at[:, pl.ds(pl.multiple_of(o * rows, rows), rows), :]
+
+    def step(k):
+        for way, box, place in ((1, left, t), (-1, right, n - 1 - t)):
+            target = lambda j: n - 1 - j if way > 0 else j
+            if k == 0:
+                @pl.when(place == 0)
+                def _():
+                    for j in range(n - 1):
+                        copy(block(target(j)), box, target(j), way).start()
+            else:
+                @pl.when(jnp.logical_and(place > 0, place <= k))
+                def _():
+                    o = target(k - place)
+                    copy(block(o), box, o, way).wait_recv()
+                    for s in range(part.shape[0]):
+                        own = part[s, pl.ds(pl.multiple_of(o * rows, rows), rows), :].astype(F32)
+                        box[o, s] = (box[o, s].astype(F32) + own).astype(BF)
+                    copy(box.at[o], box, o, way).start()
+
+    def final(out):
+        mine = pl.ds(pl.multiple_of(t * rows, rows), rows)
+        for s in range(part.shape[0]):
+            out[s] = part[s, mine, :].astype(F32)
+
+        @pl.when(t > 0)
+        def _():
+            copy(left.at[0], left, t, 1).wait_recv()
+            for s in range(part.shape[0]):
+                out[s] = out[s] + left[t, s].astype(F32)
+
+        @pl.when(t < n - 1)
+        def _():
+            copy(left.at[0], right, t, -1).wait_recv()
+            for s in range(part.shape[0]):
+                out[s] = out[s] + right[t, s].astype(F32)
+
+    def finish():
+        for j in range(n - 1):
+            for way, box, o in ((1, left, n - 1 - j), (-1, right, j)):
+                sends = (t < o) if way > 0 else (t > o)
+
+                @pl.when(sends)
+                def _():
+                    copy(box.at[o], box, o, way).wait_send()
+
+    return step, final, finish
+
+
+class _PlaneReduce:
+    def __init__(self, part, pair, box, ssem, rsem):
+        self.part, self.pair, self.box, self.ssem, self.rsem = part, pair, box, ssem, rsem
+
+    def copy(self, src, dst, who, s):
+        return pltpu.make_async_remote_copy(
+            src_ref=src, dst_ref=dst, send_sem=self.ssem.at[s], recv_sem=self.rsem.at[s],
+            device_id=who, device_id_type=MESH,
+        )
+
+    def begin(self):
+        dp, seq, t, x_dp, y_dp, d_dp = _peers()
+        for slot, chip in enumerate((d_dp, x_dp, y_dp, dp)):
+            self.copy(self.part.at[chip * 2 + 1 - seq], self.pair.at[slot], _dev(dp, 1 - seq, t), slot).start()
+
+    def _paired(self, slot, chip, also=None):
+        dp, seq, t, x_dp, y_dp, d_dp = _peers()
+        self.copy(self.pair.at[slot], self.pair.at[slot], _dev(dp, 1 - seq, t), slot).wait_recv()
+        v = self.part[chip * 2 + seq].astype(F32) + self.pair[slot].astype(F32)
+        self.pair[slot] = v.astype(BF)
+
+    def send_far(self):
+        dp, seq, t, x_dp, y_dp, d_dp = _peers()
+        for slot, chip in enumerate((d_dp, x_dp, y_dp)):
+            self._paired(slot, chip)
+            if slot == 0:
+                @pl.when(seq == 0)
+                def _():
+                    self.copy(self.pair.at[0], self.box.at[2], _dev(x_dp, seq, t), 4).start()
+
+                @pl.when(seq == 1)
+                def _():
+                    self.copy(self.pair.at[0], self.box.at[2], _dev(y_dp, seq, t), 4).start()
+
+        @pl.when(seq == 0)
+        def _():
+            self.copy(self.pair.at[1], self.box.at[0], _dev(x_dp, seq, t), 5).start()
+
+        @pl.when(seq == 1)
+        def _():
+            self.copy(self.pair.at[2], self.box.at[1], _dev(y_dp, seq, t), 6).start()
+
+    def send_near(self):
+        dp, seq, t, x_dp, y_dp, d_dp = _peers()
+        self.copy(self.pair.at[0], self.box.at[2], _dev(dp, seq, t), 4).wait_recv()
+
+        @pl.when(seq == 0)
+        def _():
+            self.box[2] = (self.box[2].astype(F32) + self.pair[2].astype(F32)).astype(BF)
+            self.copy(self.box.at[2], self.box.at[1], _dev(y_dp, seq, t), 6).start()
+
+        @pl.when(seq == 1)
+        def _():
+            self.box[2] = (self.box[2].astype(F32) + self.pair[1].astype(F32)).astype(BF)
+            self.copy(self.box.at[2], self.box.at[0], _dev(x_dp, seq, t), 5).start()
+
+    def final(self, out):
+        dp, seq, t, x_dp, y_dp, d_dp = _peers()
+        self.copy(self.pair.at[3], self.pair.at[3], _dev(dp, seq, t), 3).wait_recv()
+        self.copy(self.pair.at[0], self.box.at[0], _dev(dp, seq, t), 5).wait_recv()
+        self.copy(self.pair.at[0], self.box.at[1], _dev(dp, seq, t), 6).wait_recv()
+        out[...] = (
+            self.part[dp * 2 + seq].astype(F32) + self.pair[3].astype(F32)
+            + self.box[0].astype(F32) + self.box[1].astype(F32)
+        )
+
+    def finish(self):
+        dp, seq, t, x_dp, y_dp, d_dp = _peers()
+        for s in range(7):
+            self.copy(self.pair.at[0], self.box.at[0], _dev(dp, 1 - seq, t), s).wait_send()
+
+
+class _Smalls:
+    def __init__(self, n, box, line, ssem, rsem):
+        self.n, self.box, self.line, self.ssem, self.rsem = n, box, line, ssem, rsem
+
+    def copy(self, j, who):
+        return pltpu.make_async_remote_copy(
+            src_ref=self.box.at[2 * j], dst_ref=self.box.at[2 * j + 1],
+            send_sem=self.ssem.at[j], recv_sem=self.rsem.at[j],
+            device_id=who, device_id_type=MESH,
+        )
+
+    def near(self, j):
+        dp, seq, t, x_dp, y_dp, d_dp = _peers()
+        return (_dev(dp, 1 - seq, t), _dev(x_dp, seq, t), _dev(y_dp, seq, t))[j]
+
+    def begin(self, value):
+        self.box[0] = value
+        self.copy(0, self.near(0)).start()
+
+    def step(self, j):
+        self.copy(j, self.near(j)).wait_recv()
+        total = self.box[2 * j] + self.box[2 * j + 1]
+        if j < 2:
+            self.box[2 * j + 2] = total
+            self.copy(j + 1, self.near(j + 1)).start()
+        else:
+            t = lax.axis_index("tensor")
+            self.line[t] = total
+            for o in range(self.n):
+                @pl.when(t != o)
+                def _(o=o):
+                    self.across(t, o).start()
+
+    def across(self, src, who):
+        dp, seq, t = lax.axis_index("dp"), lax.axis_index("seq"), lax.axis_index("tensor")
+        return pltpu.make_async_remote_copy(
+            src_ref=self.line.at[src], dst_ref=self.line.at[src],
+            send_sem=self.ssem.at[3 + who], recv_sem=self.rsem.at[3 + src],
+            device_id=_dev(dp, seq, who), device_id_type=MESH,
+        )
+
+    def final(self):
+        t = lax.axis_index("tensor")
+        for o in range(self.n):
+            @pl.when(t != o)
+            def _(o=o):
+                self.across(o, o).wait_recv()
+
+    def finish(self):
+        t = lax.axis_index("tensor")
+        for j in range(3):
+            self.copy(j, self.near(j)).wait_send()
+        for o in range(self.n):
+            @pl.when(t != o)
+            def _(o=o):
+                self.across(t, o).wait_send()
+
+
+class _LineSum:
+    def __init__(self, n, part, box, out, ssem, rsem):
+        self.n, self.part, self.box, self.out, self.ssem, self.rsem = n, part, box, out, ssem, rsem
+
+    def copy(self, phase, src_block, dst_ref, who, origin):
+        dp, seq = lax.axis_index("dp"), lax.axis_index("seq")
+        return pltpu.make_async_remote_copy(
+            src_ref=src_block, dst_ref=dst_ref,
+            send_sem=self.ssem.at[phase, who], recv_sem=self.rsem.at[phase, origin],
+            device_id=_dev(dp, seq, who), device_id_type=MESH,
+        )
+
+    def scatter(self):
+        t = lax.axis_index("tensor")
+        for o in range(self.n):
+            @pl.when(t != o)
+            def _(o=o):
+                self.copy(0, self.part.at[o], self.box.at[t], o, t).start()
+
+    def gather(self):
+        t = lax.axis_index("tensor")
+        total = self.part[t].astype(F32)
+        for o in range(self.n):
+            @pl.when(t != o)
+            def _(o=o):
+                self.copy(0, self.part.at[o], self.box.at[o], o, o).wait_recv()
+
+            @pl.when(t == o)
+            def _(o=o):
+                self.box[o] = jnp.zeros(self.box.shape[1:], self.box.dtype)
+        for o in range(self.n):
+            total = total + self.box[o].astype(F32)
+        self.out[t] = total.astype(self.out.dtype)
+        for o in range(self.n):
+            @pl.when(t != o)
+            def _(o=o):
+                self.copy(1, self.out.at[t], self.out.at[t], o, t).start()
+
+    def arrive(self):
+        t = lax.axis_index("tensor")
+        for o in range(self.n):
+            @pl.when(t != o)
+            def _(o=o):
+                self.copy(1, self.out.at[o], self.out.at[o], o, o).wait_recv()
+
+    def finish(self):
+        t = lax.axis_index("tensor")
+        for o in range(self.n):
+            @pl.when(t != o)
+            def _(o=o):
+                self.copy(0, self.part.at[o], self.box.at[o], o, o).wait_send()
+                self.copy(1, self.part.at[o], self.box.at[o], o, o).wait_send()
+
+
+LANES = 128
+
+
+def _split(v, parts):
+    out = []
+    for _ in range(parts):
+        b = v.astype(BF)
+        out.append(b)
+        v = v - b.astype(F32)
+    return jnp.concatenate(out, axis=1)
+
+
+def _dot(a, b, ca=1, cb=0):
+    return lax.dot_general(a, b, (((ca,), (cb,)), ((), ())), preferred_element_type=F32)
+
+
+def _iota(shape, axis):
+    return lax.broadcasted_iota(jnp.int32, shape, axis)
+
+
+def _spreader(rows, p):
+    head = lax.rem(_iota((rows, LANES), 0), LANES)
+    return (head == 2 * p + lax.div(_iota((rows, LANES), 1), HEAD_DIM)).astype(F32).astype(BF)
+
+
+def _folder(rows, p):
+    chan = lax.rem(_iota((rows, LANES), 0), LANES)
+    return (_iota((rows, LANES), 1) == 2 * p + lax.div(chan, HEAD_DIM)).astype(F32).astype(BF)
+
+
+def _sig(v):
+    return 1.0 / (1.0 + jnp.exp(-v))
+
+
+def _three(v):
+    return v[:, :LANES] + v[:, LANES : 2 * LANES] + v[:, 2 * LANES :]
+
+
+def _head_scalars(raw, hp, marks, length):
+    v = raw + hp[0:1, :]
+    delta = jnp.maximum(v, 0.0) + jnp.log1p(jnp.exp(-jnp.abs(v)))
+    log_decay = -delta * jnp.exp(hp[1:2, :])
+    lower = (_iota((length, length), 0) >= _iota((length, length), 1)).astype(F32).astype(BF)
+    running = _three(_dot(lower, _split(log_decay, 3)))
+    entry = jnp.exp(running) * marks[:, 4:5]
+    to_end = jnp.exp(running[length - 1 :, :] - running) * marks[:, 5:6]
+    return v, delta, log_decay, running, entry, to_end
+
+
+def _marks(rows):
+    full = jnp.concatenate([rows, jnp.zeros((LANES - rows.shape[0], rows.shape[1]), F32)], axis=0)
+    return full.T
+
+
+def _bias_matrix(rows, marks, length):
+    ok = (_iota((length, length), 0) >= _iota((length, length), 1)) & (
+        marks[:, 0:1] == rows[0:1, :]
+    )
+    return jnp.where(ok, 0.0, -1e30)
+
+
+def _conv(pad, marks, taps, bias, length):
+    total = bias + taps[0:1, :] * pad[8 : 8 + length, :]
+    for k in range(1, KERNEL):
+        total = total + taps[k : k + 1, :] * (pad[8 - k : 8 - k + length, :] * marks[:, k : k + 1])
+    return total
+
+
+def mix_fwd_kernel(n, pre_i, old_i, pre_s, old_s, raw, rows, hp, taps_i, bias_i, taps_s, bias_s,
+                   cot, wo, normed, wg, y, u_i, u_s, entry_o, incoming, gate, cot_full, fo,
+                   pad, run3, run_t, bias_m, scores, heads_hl, inflow, zs, zr, ps, pr, ls, hs):
+    t = lax.axis_index("tensor")
+    seqs, length, width = pre_i.shape
+    pairs = width // LANES
+    _plane_barrier(n)
+    line = _Line(n, cot_full, cot.shape[1], zs, zr, cot)
+    plane = _Plane(wo, fo, ps, pr, ls.at[0])
+    own = pltpu.make_async_copy(cot, line.block(t), ls.at[1])
+    own.start()
+    line.step(0)
+    plane.begin()
+
+    def one(s, _):
+        rw = rows[s]
+        marks = _marks(rw)
+        v, delta, log_decay, running, entry, to_end = _head_scalars(raw[s], hp, marks, length)
+        entry_o[s] = entry
+        run3[...] = _split(running, 3)
+        run_t[...] = running.T
+        bias_m[...] = _bias_matrix(rw, marks, length)
+        heads_hl[0] = _split(delta, 2)
+        heads_hl[1] = _split(to_end, 2)
+        maps = []
+        for half in range(2):
+            ch = slice(half * STATE, (half + 1) * STATE)
+            pad[0:8, :] = old_s[s, :, ch].astype(F32)
+            pad[8:, :] = pre_s[s, :, ch].astype(F32)
+            u = _conv(pad, marks, taps_s[:, ch], bias_s[:, ch], length)
+            u_s[s, :, ch] = u
+            maps.append((u * _sig(u)).astype(BF))
+        b_map, c_map = maps
+        scores[...] = _dot(c_map, b_map, 1, 1)
+
+        def pair(p, _):
+            @pl.when(jnp.logical_and(s == 1, p == 0))
+            def _():
+                line.step(1)
+                plane.forward()
+
+            @pl.when(jnp.logical_and(s == 1, p == 4))
+            def _():
+                plane.share()
+
+            ch = pl.ds(pl.multiple_of(p * LANES, LANES), LANES)
+            at = pl.ds(pl.multiple_of(t * width + p * LANES, LANES), LANES)
+            pad[0:8, :] = old_i[s, :, ch].astype(F32)
+            pad[8:, :] = pre_i[s, :, ch].astype(F32)
+            u = _conv(pad, marks, taps_i[:, at], bias_i[:, at], length)
+            u_i[s, :, ch] = u
+            x = u * _sig(u)
+            spread = _spreader(2 * LANES, p)
+            xd = x * _dot(heads_hl[0], spread)
+            inflow[s, :, ch] = _dot(b_map, (xd * _dot(heads_hl[1], spread)).astype(BF), 0, 0).astype(BF)
+            skip = _dot(_split(hp[...], 2), spread)[2:3, :]
+            total = skip * x
+            xb = xd.astype(BF)
+            lane = lax.div(_iota(xb.shape, 1), HEAD_DIM)
+            for a in range(2):
+                h = 2 * p + a
+                pick = (lax.rem(_iota((3 * LANES, length), 0), LANES) == h).astype(F32).astype(BF)
+                decay = jnp.exp(_dot(run3[...], pick) - run_t[pl.ds(h, 1), :] + bias_m[...])
+                mixing = (decay * scores[...]).astype(BF)
+                total = total + _dot(mixing, jnp.where(lane == a, xb, jnp.zeros_like(xb)))
+            y[s, :, ch] = total
+            return 0
+
+        lax.fori_loop(0, pairs, pair, 0)
+        return 0
+
+    lax.fori_loop(0, seqs, one, 0)
+    dp, seq = lax.axis_index("dp"), lax.axis_index("seq")
+    handed = pltpu.make_async_remote_copy(
+        src_ref=inflow, dst_ref=incoming, send_sem=hs.at[0], recv_sem=hs.at[1],
+        device_id=_dev(dp, 1 - seq, t), device_id_type=MESH,
+    )
+
+    @pl.when(seq == 0)
+    def _():
+        handed.start()
+        incoming[...] = jnp.zeros_like(incoming)
+
+    line.step(2)
+    flat = normed[...].reshape(seqs * length, normed.shape[2])
+
+    def gate_part(c, _):
+        ch = pl.ds(pl.multiple_of(c * 2 * LANES, 2 * LANES), 2 * LANES)
+        part = _dot(flat, wg[:, :, ch].reshape(normed.shape[2], 2 * LANES))
+        gate[:, :, ch] = part.reshape(seqs, length, 2 * LANES)
+        return 0
+
+    lax.fori_loop(0, width // (2 * LANES), gate_part, 0)
+    for d in range(3, n):
+        line.step(d)
+    plane.arrive()
+    own.wait()
+
+    @pl.when(seq == 0)
+    def _():
+        handed.wait_send()
+
+    @pl.when(seq == 1)
+    def _():
+        handed.wait_recv()
+
+    line.finish()
+    plane.finish()
+
+
+def _mixer_call(kernel, ins, outs, scratch, name, cost, number):
+    vm = pl.BlockSpec(memory_space=pltpu.VMEM)
+    return pl.pallas_call(
+        kernel,
+        out_shape=outs,
+        in_specs=[vm] * len(ins),
+        out_specs=(vm,) * len(outs),
+        scratch_shapes=scratch,
+        compiler_params=pltpu.CompilerParams(
+            collective_id=number, has_side_effects=True, vmem_limit_bytes=60 << 20
+        ),
+        cost_estimate=pl.CostEstimate(flops=cost, bytes_accessed=1 << 20, transcendentals=0),
+        name=name,
+    )(*ins)
+
+
+def mix_fwd(n, pre_i, old_i, pre_s, old_s, raw, rows, hp, taps_i, bias_i, taps_s, bias_s, cot, wo,
+            normed, wg):
+    seqs, length, width = pre_i.shape
+    sd = jax.ShapeDtypeStruct
+    return _mixer_call(
+        functools.partial(mix_fwd_kernel, n),
+        (pre_i, old_i, pre_s, old_s, raw, rows, hp, taps_i, bias_i, taps_s, bias_s, cot, wo,
+         normed, wg),
+        (
+            sd((seqs, length, width), F32),
+            sd((seqs, length, width), F32),
+            sd((seqs, length, 2 * STATE), F32),
+            sd((seqs, length, LANES), F32),
+            sd((seqs, STATE, width), BF),
+            sd((seqs, length, width), F32),
+            sd((seqs, length, cot.shape[2]), BF),
+            sd((8,) + wo.shape, BF),
+        ),
+        [
+            pltpu.VMEM((8 + length, LANES), F32),
+            pltpu.VMEM((length, 3 * LANES), BF),
+            pltpu.VMEM((LANES, length), F32),
+            pltpu.VMEM((length, length), F32),
+            pltpu.VMEM((length, length), F32),
+            pltpu.VMEM((2, length, 2 * LANES), BF),
+            pltpu.VMEM((seqs, STATE, width), BF),
+            pltpu.SemaphoreType.DMA((2, n)),
+            pltpu.SemaphoreType.DMA((n,)),
+            pltpu.SemaphoreType.DMA((7,)),
+            pltpu.SemaphoreType.DMA((7,)),
+            pltpu.SemaphoreType.DMA((2,)),
+            pltpu.SemaphoreType.DMA((2,)),
+        ],
+        "mix_fwd",
+        4 * 10**9,
+        3,
+    )
+
+
+def gate_kernel(n, y_part, u_s, entry, h0, gate, cot, wo, gain, tokens_in,
+                d_mixed, d_gate, lam, po, go, gg, g_gain,
+                mixed, gated, grad_gn, normed, local, acc, box, ss, rs, hs):
+    dp, seq, t = lax.axis_index("dp"), lax.axis_index("seq"), lax.axis_index("tensor")
+    seqs, length, width = y_part.shape
+    model = cot.shape[2]
+    wide = 2 * LANES
+    bar = pltpu.get_barrier_semaphore()
+    pl.semaphore_signal(bar, inc=1, device_id=_dev(dp, 1 - seq, t), device_id_type=MESH)
+    for step in range(1, n):
+        pl.semaphore_signal(
+            bar, inc=1, device_id=_dev(dp, seq, lax.rem(t + step, n)), device_id_type=MESH
+        )
+    acc[...] = jnp.zeros_like(acc)
+    g_gain[...] = jnp.zeros_like(g_gain)
+
+    def spread_of(s, c):
+        heads = _split(entry[s], 2)
+        head = lax.rem(_iota((wide, wide), 0), LANES)
+        one = head == 4 * c + lax.div(_iota((wide, wide), 1), HEAD_DIM)
+        return _dot(heads, one.astype(F32).astype(BF))
+
+    def maps(s):
+        u = u_s[s, :, STATE:]
+        return (u * _sig(u)).astype(BF)
+
+    def first(c, _):
+        ch = pl.ds(pl.multiple_of(c * wide, wide), wide)
+        at = pl.ds(pl.multiple_of(t * width + c * wide, wide), wide)
+        w = wo[:, :, ch].reshape(model, wide)
+        for s in range(seqs):
+            g = _dot(cot[s], w)
+            grad_gn[s, :, ch] = g
+            m = y_part[s, :, ch] + spread_of(s, c) * _dot(maps(s), h0[s, :, ch])
+            z = gate[s, :, ch]
+            gd = m * (z * _sig(z))
+            mixed[s, :, ch] = m
+            gated[s, :, ch] = gd
+            sq, ds = gd * gd, g * gain[:, at] * gd
+            acc[0, s] += sq[:, :LANES] + sq[:, LANES:]
+            acc[1, s] += ds[:, :LANES] + ds[:, LANES:]
+        return 0
+
+    lax.fori_loop(0, width // wide, first, 0)
+    ones = jnp.ones((8, wide), F32).astype(BF)
+    row = _iota((8, length), 0)
+    mine = jnp.zeros((8, length), F32)
+    for kind in range(2):
+        for s in range(seqs):
+            sums = _dot(ones, _split(acc[kind, s], 2), 1, 1)
+            mine = jnp.where(row == kind * seqs + s, sums, mine)
+    box[t] = mine
+    pl.semaphore_wait(bar, n)
+
+    def copy(src, who):
+        return pltpu.make_async_remote_copy(
+            src_ref=box.at[src], dst_ref=box.at[src], send_sem=ss.at[who], recv_sem=rs.at[src],
+            device_id=_dev(dp, seq, who), device_id_type=MESH,
+        )
+
+    for o in range(n):
+        @pl.when(t != o)
+        def _(o=o):
+            copy(t, o).start()
+    for o in range(n):
+        @pl.when(t != o)
+        def _(o=o):
+            copy(o, o).wait_recv()
+    full_width = n * width
+    cols = _marks(jnp.sum(box[...], axis=0) / full_width)
+
+    def second(c, _):
+        ch = pl.ds(pl.multiple_of(c * wide, wide), wide)
+        at = pl.ds(pl.multiple_of(t * width + c * wide, wide), wide)
+        gn = gain[:, at]
+        for s in range(seqs):
+            rms = lax.rsqrt(cols[:, s : s + 1] + EPS)
+            mean = cols[:, seqs + s : seqs + s + 1]
+            g, gd, m, z = grad_gn[s, :, ch], gated[s, :, ch], mixed[s, :, ch], gate[s, :, ch]
+            sg = _sig(z)
+            scaled = gd * rms
+            normed[s, :, ch] = (scaled * gn).astype(BF)
+            g_gain[0:1, ch] += jnp.sum(g * scaled, axis=0, keepdims=True)
+            d_gd = rms * (g * gn) - scaled * (rms * rms * mean)
+            dm = d_gd * (z * sg)
+            d_mixed[s, :, ch] = dm
+            d_gate[s, :, ch] = (d_gd * m * sg * (1.0 + z * (1.0 - sg))).astype(BF)
+            ed = (spread_of(s, c) * dm).astype(BF)
+            local[s, :, ch] = _dot(maps(s), ed, 0, 0).astype(BF)
+        return 0
+
+    lax.fori_loop(0, width // wide, second, 0)
+    handed = pltpu.make_async_remote_copy(
+        src_ref=local, dst_ref=lam, send_sem=hs.at[0], recv_sem=hs.at[1],
+        device_id=_dev(dp, 1 - seq, t), device_id_type=MESH,
+    )
+
+    @pl.when(seq == 1)
+    def _():
+        handed.start()
+        lam[...] = jnp.zeros_like(lam)
+
+    blocks = 2
+    rows = blocks * wo.shape[1]
+
+    def third(b, _):
+        ch = pl.ds(pl.multiple_of(b * rows, LANES), rows)
+        w = wo[pl.ds(b * blocks, blocks)].reshape(rows, width)
+        total = None
+        for s in range(seqs):
+            po[s, :, ch] = _dot(normed[s], w, 1, 1).astype(BF)
+            part = _dot(cot[s, :, ch], normed[s], 0, 0)
+            total = part if total is None else total + part
+        go[pl.ds(b * blocks, blocks)] = total.reshape(blocks, wo.shape[1], width).astype(BF)
+        total = None
+        for s in range(seqs):
+            part = _dot(tokens_in[s, :, ch], d_gate[s], 0, 0)
+            total = part if total is None else total + part
+        gg[pl.ds(b * blocks, blocks)] = total.reshape(blocks, wo.shape[1], width).astype(BF)
+        return 0
+
+    lax.fori_loop(0, model // rows, third, 0)
+
+    @pl.when(seq == 1)
+    def _():
+        handed.wait_send()
+
+    @pl.when(seq == 0)
+    def _():
+        handed.wait_recv()
+
+    for o in range(n):
+        @pl.when(t != o)
+        def _(o=o):
+            copy(o, o).wait_send()
+
+
+def gate_stage(n, y_part, u_s, entry, h0, gate, cot, wo, gain, tokens_in):
+    seqs, length, width = y_part.shape
+    sd = jax.ShapeDtypeStruct
+    whole = pltpu.VMEM((seqs, length, width), F32)
+    return _mixer_call(
+        functools.partial(gate_kernel, n),
+        (y_part, u_s, entry, h0, gate, cot, wo, gain, tokens_in),
+        (
+            sd((seqs, length, width), F32),
+            sd((seqs, length, width), BF),
+            sd((seqs, STATE, width), BF),
+            sd((seqs, length, cot.shape[2]), BF),
+            sd(wo.shape, BF),
+            sd(wo.shape, BF),
+            sd((8, width), F32),
+        ),
+        [
+            whole, whole, whole,
+            pltpu.VMEM((seqs, length, width), BF),
+            pltpu.VMEM((seqs, STATE, width), BF),
+            pltpu.VMEM((2, seqs, length, LANES), F32),
+            pltpu.VMEM((n, 8, length), F32),
+            pltpu.SemaphoreType.DMA((n,)),
+            pltpu.SemaphoreType.DMA((n,)),
+            pltpu.SemaphoreType.DMA((2,)),
+        ],
+        "gate_stage",
+        6 * 10**9,
+        2,
+    )
+
+
+def mix_bwd_kernel(n, dy_r, u_i, u_s, pre_i, old_i, pre_s, old_s, raw, rows, h0, lam, hp,
+                   taps_i, taps_s, po, go, gg,
+                   d_i, d_s, d_raw, sm_i, sm_s, sm_h, o_po, o_go, o_gg,
+                   pad, moved, run3, run_t, bias_m, scores, d_scores, heads_hl,
+                   acc_r, acc_c, acc_d, acc_q, d_b, d_c, lo, ro, xo, bo, xg, bg,
+                   head_i, tail_i, head_s, tail_s, next_i, next_s, zs, zr, ps, pr, hs):
+    t = lax.axis_index("tensor")
+    seqs, length, width = pre_i.shape
+    pairs = width // LANES
+    _plane_barrier(n)
+    step_o, final_o, finish_o = _line_reduce(n, po, lo, ro, zs, zr)
+    planes = (
+        _PlaneReduce(go, xo, bo, ps.at[0], pr.at[0]), _PlaneReduce(gg, xg, bg, ps.at[1], pr.at[1])
+    )
+    step_o(0)
+    for plane in planes:
+        plane.begin()
+    sm_i[...] = jnp.zeros_like(sm_i)
+    sm_s[...] = jnp.zeros_like(sm_s)
+    sm_h[...] = jnp.zeros_like(sm_h)
+    moved[0:8, :] = jnp.zeros((8, LANES), F32)
+    moved[8 + length :, :] = jnp.zeros((8, LANES), F32)
+
+    def conv_back(du, marks, taps, s, ch, d_o, head_o, tail_o, sm):
+        total = None
+        for k in range(KERNEL):
+            m = du if k == 0 else du * marks[:, k : k + 1]
+            moved[8 : 8 + length, :] = m
+            sm[k : k + 1, ch] += jnp.sum(m * pad[8 - k : 8 - k + length, :], axis=0, keepdims=True)
+            part = taps[k : k + 1, :] * moved[k : k + 8 + length, :]
+            total = part if total is None else total + part
+        sm[4:5, ch] += jnp.sum(du, axis=0, keepdims=True)
+        head_o[s, :, ch] = total[0:8, :]
+        d_o[s, :, ch] = total[8:, :].astype(BF)
+        tail_o[s, :, ch] = total[length - 8 :, :]
+
+    def one(s, _):
+        rw = rows[s]
+        marks = _marks(rw)
+        v, delta, log_decay, running, entry, to_end = _head_scalars(raw[s], hp, marks, length)
+        run3[...] = _split(running, 3)
+        run_t[...] = running.T
+        bias_m[...] = _bias_matrix(rw, marks, length)
+        heads_hl[0] = _split(delta, 2)
+        heads_hl[1] = _split(to_end, 2)
+        heads_hl[2] = _split(entry, 2)
+        ub, uc = u_s[s, :, :STATE], u_s[s, :, STATE:]
+        sb, sc = _sig(ub), _sig(uc)
+        b_map, c_map = (ub * sb).astype(BF), (uc * sc).astype(BF)
+        scores[...] = _dot(c_map, b_map, 1, 1)
+        d_scores[...] = jnp.zeros_like(d_scores)
+        for acc in (acc_r, acc_c, acc_d, acc_q, d_b, d_c):
+            acc[...] = jnp.zeros_like(acc)
+
+        def pair(p, _):
+            @pl.when(jnp.logical_and(s == 0, p == 2))
+            def _():
+                planes[0].send_far()
+
+            @pl.when(jnp.logical_and(s == 0, p == 3))
+            def _():
+                planes[1].send_far()
+
+            @pl.when(jnp.logical_and(s == 0, p == 5))
+            def _():
+                step_o(1)
+
+            @pl.when(jnp.logical_and(s == 1, p == 2))
+            def _():
+                planes[0].send_near()
+
+            @pl.when(jnp.logical_and(s == 1, p == 5))
+            def _():
+                planes[1].send_near()
+
+            @pl.when(jnp.logical_and(s == 1, p == 4))
+            def _():
+                step_o(2)
+
+            ch = pl.ds(pl.multiple_of(p * LANES, LANES), LANES)
+            at = pl.ds(pl.multiple_of(t * width + p * LANES, LANES), LANES)
+            u = u_i[s, :, ch]
+            sg = _sig(u)
+            x = u * sg
+            dy = dy_r[s, :, ch]
+            spread, fold = _spreader(2 * LANES, p), _folder(2 * LANES, p)
+            dl = _dot(heads_hl[0], spread)
+            q = _dot(heads_hl[1], spread)
+            e = _dot(heads_hl[2], spread)
+            xd = x * dl
+            xb, db = xd.astype(BF), dy.astype(BF)
+            h_in, l_in = h0[s, :, ch], lam[s, :, ch]
+            c_h = _dot(c_map, h_in)
+            b_l = _dot(b_map, l_in)
+            qx, ed = q * xd, e * dy
+            d_b[...] += _dot(qx.astype(BF), l_in, 1, 1)
+            d_c[...] += _dot(ed.astype(BF), h_in, 1, 1)
+            late = qx * b_l
+            dxd = q * b_l
+            lane = lax.div(_iota(xb.shape, 1), HEAD_DIM)
+            for a in range(2):
+                h = 2 * p + a
+                pick = (lax.rem(_iota((3 * LANES, length), 0), LANES) == h).astype(F32).astype(BF)
+                decay = jnp.exp(_dot(run3[...], pick) - run_t[pl.ds(h, 1), :] + bias_m[...])
+                da = jnp.where(lane == a, db, jnp.zeros_like(db))
+                ld = decay * _dot(da, xb, 1, 1)
+                d_scores[...] += ld
+                both = (ld * scores[...]).astype(BF)
+                mixing = (decay * scores[...]).astype(BF)
+                dxd = dxd + _dot(mixing, da, 0, 0)
+                col = (_iota((length, LANES), 1) == h).astype(F32).astype(BF)
+                row = (_iota((LANES, length), 0) == h).astype(F32).astype(BF)
+                acc_r[...] += _dot(both, col)
+                acc_c[...] += _dot(row, both)
+            acc_r[...] += _dot(_split(ed * c_h - late, 2), fold)
+            acc_d[...] += _dot(_split(dxd * x, 2), fold)
+            total = jnp.broadcast_to(jnp.sum(late, axis=0, keepdims=True), (8, LANES))
+            acc_q[...] += _dot(_split(total, 2), fold)
+            skip = _dot(_split(hp[...], 2), spread)[2:3, :]
+            sm_i[5:6, ch] += jnp.sum(dy * x, axis=0, keepdims=True)
+            du = (dxd * dl + skip * dy) * (sg * (1.0 + u * (1.0 - sg)))
+            pad[0:8, :] = old_i[s, :, ch].astype(F32)
+            pad[8:, :] = pre_i[s, :, ch].astype(F32)
+            conv_back(du, marks, taps_i[:, at], s, ch, d_i, head_i, tail_i, sm_i)
+            return 0
+
+        lax.fori_loop(0, pairs, pair, 0)
+        ds = d_scores[...].astype(BF)
+        grads = (d_b[...] + _dot(ds, c_map, 0, 0), d_c[...] + _dot(ds, b_map))
+        for half, (g, u, sg) in enumerate(zip(grads, (ub, uc), (sb, sc))):
+            ch = slice(half * STATE, (half + 1) * STATE)
+            pad[0:8, :] = old_s[s, :, ch].astype(F32)
+            pad[8:, :] = pre_s[s, :, ch].astype(F32)
+            du = g * (sg * (1.0 + u * (1.0 - sg)))
+            conv_back(du, marks, taps_s[:, ch], s, ch, d_s, head_s, tail_s, sm_s)
+        d_run = acc_r[...] - acc_c[...].T
+        last = _iota(d_run.shape, 0) == length - 1
+        d_run = d_run + jnp.where(last, acc_q[0:1, :], 0.0)
+        upper = (_iota((length, length), 0) <= _iota((length, length), 1)).astype(F32).astype(BF)
+        d_log = _three(_dot(upper, _split(d_run, 3)))
+        d_delta = acc_d[...] - d_log * jnp.exp(hp[1:2, :])
+        d_step = d_delta * _sig(v)
+        d_raw[s] = d_step.astype(BF)
+        sm_h[0:1, :] += jnp.sum(d_step, axis=0, keepdims=True)
+        sm_h[1:2, :] += jnp.sum(d_log * log_decay, axis=0, keepdims=True)
+        return 0
+
+    lax.fori_loop(0, seqs, one, 0)
+    for k in range(3, n - 1):
+        step_o(k)
+    dp, seq = lax.axis_index("dp"), lax.axis_index("seq")
+    handed = [
+        pltpu.make_async_remote_copy(
+            src_ref=a, dst_ref=b, send_sem=hs.at[2 * i], recv_sem=hs.at[2 * i + 1],
+            device_id=_dev(dp, 1 - seq, t), device_id_type=MESH,
+        )
+        for i, (a, b) in enumerate(((head_i, next_i), (head_s, next_s)))
+    ]
+
+    @pl.when(seq == 1)
+    def _():
+        for c in handed:
+            c.start()
+
+    planes[0].final(o_go)
+
+    @pl.when(seq == 0)
+    def _():
+        for c, box, tail, out in zip(handed, (next_i, next_s), (tail_i, tail_s), (d_i, d_s)):
+            c.wait_recv()
+            for s in range(seqs):
+                more = jnp.concatenate([jnp.zeros_like(box[s]), box[s]], axis=0)
+                out[s, length - 16 :, :] = (tail[s] + more).astype(BF)
+
+    @pl.when(seq == 1)
+    def _():
+        for c in handed:
+            c.wait_send()
+
+    planes[1].final(o_gg)
+    final_o(o_po)
+    for plane in planes:
+        plane.finish()
+    finish_o()
+
+
+def mix_bwd(n, dy, u_i, u_s, pre_i, old_i, pre_s, old_s, raw, rows, h0, lam, hp, taps_i, taps_s,
+            po, go, gg):
+    seqs, length, width = pre_i.shape
+    model = po.shape[2]
+    box = pltpu.VMEM((n, seqs, length // n, model), BF)
+    sd = jax.ShapeDtypeStruct
+    square = pltpu.VMEM((length, length), F32)
+    tall = pltpu.VMEM((length, LANES), F32)
+    return _mixer_call(
+        functools.partial(mix_bwd_kernel, n),
+        (dy, u_i, u_s, pre_i, old_i, pre_s, old_s, raw, rows, h0, lam, hp, taps_i, taps_s, po, go,
+         gg),
+        (
+            sd((seqs, length, width), BF),
+            sd((seqs, length, 2 * STATE), BF),
+            sd((seqs, length, LANES), BF),
+            sd((8, width), F32),
+            sd((8, 2 * STATE), F32),
+            sd((8, LANES), F32),
+            sd((seqs, length // n, model), F32),
+            sd(go.shape[1:], F32),
+            sd(gg.shape[1:], F32),
+        ),
+        [
+            pltpu.VMEM((8 + length, LANES), F32),
+            pltpu.VMEM((16 + length, LANES), F32),
+            pltpu.VMEM((length, 3 * LANES), BF),
+            pltpu.VMEM((LANES, length), F32),
+            square, square, square,
+            pltpu.VMEM((3, length, 2 * LANES), BF),
+            tall, pltpu.VMEM((LANES, length), F32), tall, pltpu.VMEM((8, LANES), F32), tall, tall,
+            box, box,
+            pltpu.VMEM((4,) + go.shape[1:], BF),
+            pltpu.VMEM((3,) + go.shape[1:], BF),
+            pltpu.VMEM((4,) + gg.shape[1:], BF),
+            pltpu.VMEM((3,) + gg.shape[1:], BF),
+            pltpu.VMEM((seqs, 8, width), F32),
+            pltpu.VMEM((seqs, 16, width), F32),
+            pltpu.VMEM((seqs, 8, 2 * STATE), F32),
+            pltpu.VMEM((seqs, 16, 2 * STATE), F32),
+            pltpu.VMEM((seqs, 8, width), F32),
+            pltpu.VMEM((seqs, 8, 2 * STATE), F32),
+            pltpu.SemaphoreType.DMA((2, n)),
+            pltpu.SemaphoreType.DMA((2, n)),
+            pltpu.SemaphoreType.DMA((2, 7)),
+            pltpu.SemaphoreType.DMA((2, 7)),
+            pltpu.SemaphoreType.DMA((4,)),
+        ],
+        "mix_bwd",
+        8 * 10**9,
+        4,
+    )
+
+
+def reduce_kernel(n, normed, dg, di, ds, dr, wg, wi, ws, wt, gain, sm_i, sm_s, sm_h, g_gain,
+                  o_pg, o_gi, o_gs, o_gt, o_sm,
+                  pg, gi, gs, gt, lg, rg, xi, xs, xt, bi, bs, bt, mb,
+                  xp, xb, xo2, zs, zr, ps, pr, ms, mr, es, er):
+    _plane_barrier(n)
+    seqs, length, width = di.shape
+    model = normed.shape[2]
+    blocks = 2
+    rows = blocks * wi.shape[1]
+    small = _Smalls(n, mb, o_sm, ms, mr)
+    mb[0] = jnp.zeros(mb.shape[1:], F32)
+    mb[0, 0:6, :] = sm_i[0:6, :]
+    mb[0, 6:7, :] = g_gain[0:1, :]
+    for k in range(5):
+        at = 256 * (k % 3)
+        mb[0, 9 + k // 3 : 10 + k // 3, at : at + 256] = sm_s[k : k + 1, :]
+    mb[0, 10:11, 512:640] = sm_h[0:1, :]
+    mb[0, 10:11, 640:768] = sm_h[1:2, :]
+
+    for b in range(model // rows):
+        ch = slice(b * rows, (b + 1) * rows)
+        near = slice(b * blocks, (b + 1) * blocks)
+        w = [r[near].reshape(rows, r.shape[2]) for r in (wg, wi, ws, wt)]
+        total = None
+        for s in range(seqs):
+            part = None
+            for d, one in zip((dg, di, ds, dr), w):
+                more = _dot(d[s], one, 1, 1)
+                part = more if part is None else part + more
+            pg[s, :, ch] = part.astype(BF)
+            part = jnp.sum(part * normed[s, :, ch].astype(F32), axis=0, keepdims=True)
+            total = part if total is None else total + part
+        mb[0, 7 + b // 2 : 8 + b // 2, (b % 2) * rows : (b % 2 + 1) * rows] = total / gain[:, ch]
+    step_g, final_g, finish_g = _line_reduce(n, pg, lg, rg, zs, zr)
+    step_g(0)
+    small.copy(0, small.near(0)).start()
+    planes = [
+        _PlaneReduce(part, pair, box, ps.at[i], pr.at[i])
+        for i, (part, pair, box) in enumerate(((gs, xs, bs), (gt, xt, bt), (gi, xi, bi)))
+    ]
+
+    def weight(d, out):
+        def one(b, _):
+            ch = pl.ds(pl.multiple_of(b * rows, LANES), rows)
+            total = None
+            for s in range(seqs):
+                part = _dot(normed[s, :, ch], d[s], 0, 0)
+                total = part if total is None else total + part
+            out[pl.ds(b * blocks, blocks)] = total.reshape(
+                blocks, wi.shape[1], d.shape[2]
+            ).astype(BF)
+            return 0
+
+        lax.fori_loop(0, model // rows, one, 0)
+
+    weight(ds, gs)
+    planes[0].begin()
+    weight(dr, gt)
+    planes[1].begin()
+    weight(di, gi)
+    planes[2].begin()
+    small.step(0)
+    step_g(1)
+    for p in planes:
+        p.send_far()
+    small.step(1)
+    for p in planes[:2]:
+        p.send_near()
+    small.step(2)
+    step_g(2)
+    planes[2].send_near()
+    for k in range(3, n - 1):
+        step_g(k)
+    planes[0].final(o_gs)
+    planes[1].final(o_gt)
+    quarter = xp.shape[1]
+    for o in range(n):
+        xp[o] = o_gs[o * quarter : (o + 1) * quarter, :].astype(BF)
+    state = _LineSum(n, xp, xb, xo2, es, er)
+    state.scatter()
+    planes[2].final(o_gi)
+    state.gather()
+    small.final()
+    final_g(o_pg)
+    state.arrive()
+    for o in range(n):
+        o_gs[o * quarter : (o + 1) * quarter, :] = xo2[o].astype(F32)
+    for p in planes:
+        p.finish()
+    state.finish()
+    small.finish()
+    finish_g()
+
+
+def reduce_all(n, normed, dg, di, ds, dr, wg, wi, ws, wt, gain, sm_i, sm_s, sm_h, g_gain):
+    seqs, length, model = normed.shape
+    rows = length // n
+    sd = jax.ShapeDtypeStruct
+    box = pltpu.VMEM((n, seqs, rows, model), BF)
+    quarter = pltpu.VMEM((n, ws.shape[1] // n, ws.shape[2]), BF)
+    sums = (16, wi.shape[2])
+    return _mixer_call(
+        functools.partial(reduce_kernel, n),
+        (normed, dg, di, ds, dr, wg, wi, ws, wt, gain, sm_i, sm_s, sm_h, g_gain),
+        (sd((seqs, rows, model), F32),)
+        + tuple(sd(w.shape[1:], F32) for w in (wi, ws, wt))
+        + (sd((n,) + sums, F32),),
+        [pltpu.VMEM((seqs, length, model), BF)]
+        + [pltpu.VMEM(w.shape, BF) for w in (wi, ws, wt)]
+        + [box, box]
+        + [pltpu.VMEM((4,) + w.shape[1:], BF) for w in (wi, ws, wt)]
+        + [pltpu.VMEM((3,) + w.shape[1:], BF) for w in (wi, ws, wt)]
+        + [
+            pltpu.VMEM((6,) + sums, F32),
+            quarter, quarter, quarter,
+            pltpu.SemaphoreType.DMA((2, n)),
+            pltpu.SemaphoreType.DMA((2, n)),
+            pltpu.SemaphoreType.DMA((3, 7)),
+            pltpu.SemaphoreType.DMA((3, 7)),
+            pltpu.SemaphoreType.DMA((3 + n,)),
+            pltpu.SemaphoreType.DMA((3 + n,)),
+            pltpu.SemaphoreType.DMA((2, n)),
+            pltpu.SemaphoreType.DMA((2, n)),
+        ],
+        "reduce_all",
+        6 * 10**9,
+        1,
+    )
+
+
+def emit_kernel(n, heads, tok, cot, gain, branch, rows, gg, gi, gs, gt, go, sms,
+                block_out, g_tok, g_in, o_gg, o_gi, o_gs, o_gt, o_ci, o_ib, o_cs, o_sb,
+                o_shift, o_rate, o_skip, o_gain, o_go):
+    for s in range(tok.shape[0]):
+        v = tok[s].astype(F32)
+        rms = lax.rsqrt(jnp.mean(v * v, axis=-1, keepdims=True) + EPS)
+        block_out[s] = (v + branch[s]).astype(BF)
+        scaled = rows[s] * gain[...]
+        mean = jnp.mean(scaled * v, axis=-1, keepdims=True)
+        g_tok[s] = cot[s].astype(F32) + rms * scaled - v * (rms * rms * rms * mean)
+    o_gg[...] = gg[...]
+    o_gi[...] = gi[...]
+    o_gs[...] = gs[...]
+    o_gt[...] = gt[:, :heads]
+    short = jnp.zeros((256 - go.shape[0], go.shape[1]), F32)
+    o_go[...] = jnp.concatenate([go[...], short], axis=0).T[:, : go.shape[0]]
+    width = sms.shape[2]
+    shared = None
+    head_rows = None
+    for t in range(n):
+        ch = slice(t * width, (t + 1) * width)
+        o_ci[:, ch] = sms[t, 0:4, :]
+        o_ib[:, ch] = sms[t, 4:5, :]
+        o_gain[:, ch] = sms[t, 6:7, :]
+        block = sms[t, 8:16, :]
+        shared = sms[t, 7:11, :] if shared is None else shared + sms[t, 7:11, :]
+        lanes = _iota((3 * width, LANES), 0)
+        chan = lax.rem(lanes, width)
+        to = _iota((3 * width, LANES), 1) == heads * t + lax.div(chan, HEAD_DIM)
+        skips = _dot(_split(sms[t, 0:8, :], 3), to.astype(F32).astype(BF))
+        lanes = lax.rem(_iota((3 * LANES, LANES), 0), LANES)
+        to = (_iota((3 * LANES, LANES), 1) == heads * t + lanes) & (lanes < heads)
+        to = to.astype(F32).astype(BF)
+        shift = _dot(_split(block[:, 512:640], 3), to)
+        rate = _dot(_split(block[:, 640:768], 3), to)
+        new = (skips[5:6, :], shift[2:3, :], rate[2:3, :])
+        head_rows = new if head_rows is None else tuple(a + b for a, b in zip(head_rows, new))
+    every = n * heads
+    o_skip[...] = head_rows[0][:, :every]
+    o_shift[...] = head_rows[1][:, :every]
+    o_rate[...] = head_rows[2][:, :every]
+    g_in[:, :width] = shared[0:1, :]
+    g_in[:, width:] = shared[1:2, :]
+    for k in range(4):
+        at = 256 * (k % 3)
+        o_cs[k : k + 1, :] = shared[2 + k // 3 : 3 + k // 3, at : at + 256]
+    o_sb[...] = shared[3:4, 256:512]
+
+
+def emit_all(n, heads, tok, cot, gain, branch, rows, gg, gi, gs, gt, go, sms):
+    vm = pl.BlockSpec(memory_space=pltpu.VMEM)
+    sd = lambda *shape: jax.ShapeDtypeStruct(shape, F32)
+    width = sms.shape[2]
+    outs = (
+        jax.ShapeDtypeStruct(tok.shape, BF), sd(*tok.shape), sd(1, tok.shape[2]),
+        sd(*gg.shape), sd(*gi.shape), sd(*gs.shape), sd(gt.shape[0], heads),
+        sd(4, n * width), sd(1, n * width), sd(4, 2 * STATE), sd(1, 2 * STATE),
+        sd(1, n * heads), sd(1, n * heads), sd(1, n * heads), sd(1, n * width),
+        sd(go.shape[1], go.shape[0]),
+    )
+    return pl.pallas_call(
+        functools.partial(emit_kernel, n, heads),
+        out_shape=outs,
+        in_specs=[vm] * 11,
+        out_specs=(vm,) * len(outs),
+        compiler_params=pltpu.CompilerParams(vmem_limit_bytes=40 << 20),
+        name="emit_all",
+    )(tok, cot, gain, branch, rows, gg, gi, gs, gt, go, sms)
 
 
 def per_device(
@@ -385,7 +1674,98 @@
     )
 
 
+def per_device_fast(
+    tokens,
+    segments,
+    input_gain,
+    gate_proj,
+    inner_proj,
+    state_proj,
+    step_proj,
+    conv_inner,
+    inner_bias,
+    conv_state,
+    state_bias,
+    step_bias,
+    log_rates,
+    skip_gain,
+    gated_gain,
+    output_proj,
+    cotangent,
+):
+    tensor_count = lax.axis_size("tensor")
+    tensor_rank = lax.axis_index("tensor")
+    heads = step_proj.shape[1]
+    step_wide = jnp.pad(step_proj, ((0, 0), (0, 128 - heads)))
+    normed, g8, i8, s8, t8 = gather_all(
+        tensor_count,
+        tokens,
+        input_gain,
+        (gate_proj, inner_proj, state_proj, step_wide),
+    )
+    width = tokens.shape[2]
+    inner_full = i8.reshape(width, -1)
+    state_full = s8.reshape(width, -1)
+    step_full = t8.reshape(width, -1)
+    width_here = inner_full.shape[1]
+    heads_here = heads
+    head_start = tensor_rank * heads_here
+    margin = 8
+    inner_low = jnp.dot(normed, inner_full, preferred_element_type=jnp.float32).astype(jnp.bfloat16)
+    state_low = jnp.dot(normed, state_full, preferred_element_type=jnp.float32).astype(jnp.bfloat16)
+    prior_inner, prior_state = passed_along(
+        (inner_low[:, -margin:], state_low[:, -margin:]), "seq", 1
+    )
+    step_raw = jnp.dot(normed, step_full, preferred_element_type=jnp.float32)
+    prior_seg = passed_along(segments[:, 1 - KERNEL :], "seq", 1)
+    seg_padded = jnp.concatenate([prior_seg, segments], axis=1)
+    length = segments.shape[1]
+    same = [
+        seg_padded[:, KERNEL - 1 - k : KERNEL - 1 - k + length] == segments for k in range(1, KERNEL)
+    ]
+    same += [segments == prior_seg[:, -1:], segments == segments[:, -1:]]
+    rows = jnp.stack(
+        [segments.astype(jnp.float32)]
+        + [m.astype(jnp.float32) for m in same]
+        + [jnp.zeros(segments.shape, jnp.float32)] * 2,
+        axis=1,
+    )
+    heads_param = jnp.pad(
+        lax.dynamic_slice_in_dim(
+            jnp.stack([step_bias, log_rates, skip_gain]), head_start, heads_here, 1
+        ),
+        ((0, 5), (0, LANES - heads_here)),
+    )
+    y_part, u_inner, u_state, entry, incoming, gate_in, cot_rows, o8 = mix_fwd(
+        tensor_count, inner_low, prior_inner, state_low, prior_state, step_raw, rows, heads_param,
+        conv_inner, inner_bias[None], conv_state, state_bias[None], cotangent, output_proj.T,
+        normed, g8,
+    )
+    grad_mixed, grad_gate_in, outgoing_grad, partial_out, grad_output, grad_gate, grad_gain = gate_stage(
+        tensor_count, y_part, u_state, entry, incoming, gate_in, cot_rows, o8, gated_gain[None], normed
+    )
+    (
+        d_inner, d_state, d_step, sm_i, sm_s, sm_h, branch_rows, shard_output, shard_gate
+    ) = mix_bwd(
+        tensor_count, grad_mixed, u_inner, u_state, inner_low, prior_inner, state_low, prior_state,
+        step_raw, rows, incoming, outgoing_grad, heads_param, conv_inner, conv_state,
+        partial_out, grad_output, grad_gate,
+    )
+    gain_row = input_gain[None]
+    grad_rows, shard_inner, shard_state, shard_step, sms = reduce_all(
+        tensor_count, normed, grad_gate_in, d_inner, d_state, d_step, g8, i8, s8, t8, gain_row,
+        sm_i, sm_s, sm_h, grad_gain,
+    )
+    outs = emit_all(
+        tensor_count, heads, tokens, cotangent, gain_row, branch_rows, grad_rows,
+        shard_gate, shard_inner, shard_state, shard_step, shard_output, sms,
+    )
+    flat = (2, 8, 10, 11, 12, 13, 14)
+    return tuple(o[0] if i in flat else o for i, o in enumerate(outs))
+
+
 def solution(mesh):
+    fast = mesh.shape["dp"] == 4 and mesh.shape["seq"] == 2
     placed = (
         P("dp", ("seq", "tensor"), None),
         P("dp", "seq"),
@@ -406,7 +1786,7 @@
         P("dp", ("seq", "tensor"), None),
     )
     return jax.shard_map(
-        per_device,
+        per_device_fast if fast else per_device,
         mesh=mesh,
         in_specs=placed,
         out_specs=(

time: 845 us -> 217 us (0.26)
  waiting for transfers between devices: 497 us -> 0.01 us
  Pallas kernels: 0 us -> 189 us
  blocking collectives: 98.9 us -> 0 us
  matrix products: 94.8 us -> 6.67 us
  other arithmetic: 57.8 us -> 0.71 us
  local copies, waits for them, and re-layouts: 62 us -> 12.6 us
  between operations: 15.6 us -> 1.04 us
    reduce_scatter x6 -> x0, waiting for transfers between devices: 275 us -> none  [the longest x1 61.1 us: per_device(): lax.psum_scatter(partial_out, 'tensor', scatter_dimension=1, tiled=True)]
    pallas_call x0 -> x6, Pallas kernels: none -> 189 us  [the longest x4 143 us: _mixer_call(): pl.pallas_call(kernel, out_shape=outs, in_specs=[vm] * len(ins), out_spec...]
    psum x1 -> x0, waiting for transfers between devices: 134 us -> none  [per_device(): lax.psum((grad_input_gain, placed(conv_inner, grad_kernel_here, chan_star...]
    dot_general x27 -> x3, matrix products: 94.8 us -> 6.67 us  [the longest x1 3.1 us: per_device_fast(): jnp.dot(normed, inner_full, preferred_element_type=jnp.float32)]
    all_gather x5 -> x0, waiting for transfers between devices: 77.1 us -> none  [the longest x1 29.5 us: per_device(): lax.all_gather(output_proj, ('dp', 'seq'), axis=1, tiled=True)]
    psum x3 -> x0, blocking collectives: 67.9 us -> none  [the longest x1 43.6 us: per_device(): grad_state_pre = lax.psum(grad_state_part, 'tensor').astype(jnp.bfloat16)]
    all_gather x5 -> x0, blocking collectives: 31 us -> none  [the longest x1 10.4 us: per_device(): lax.all_gather(state_proj, ('dp', 'seq'), axis=0, tiled=True)]
    reduce_sum x11 -> x0, other arithmetic: 21.7 us -> none  [the longest x2 6.92 us: mixer_rear(): skips[:, None] * inner]
  transfers between devices with their start and end apart: 18 -> 3, of which waited for: 12 -> 0; matrix products, arithmetic and copies ran while one was open for 13% -> 5% of each run, Pallas kernels for 0% -> 20%
where the time goes in v1:
time: 217 us; the launch traced here: 216 us
  Pallas kernels  189 us (87%)
  local copies, waits for them, and re-layouts  12.6 us (6%)
  matrix products  6.67 us (3%)
  starting transfers between devices  6.13 us (3%)
    pallas_call x4, Pallas kernels, _mixer_call(): pl.pallas_call(kernel, out_shape=outs, in_specs=[vm] * len(ins), out_spec...  143 us
    pallas_call x1, Pallas kernels, gather_all(): pl.pallas_call(functools.partial(gather_kernel, n), out_shape=(act,) + tu...  42.6 us
    unnamed x45, local copies, waits for them, and re-layouts  8.18 us
    ppermute x3, starting transfers between devices, passed_along(): return lax.ppermute(block, axis, route)  6.13 us
  transfers between devices with their start and end apart: 3, of which 0 were waited for; matrix products, arithmetic and copies ran while one was open for 5% of the time, Pallas kernels for 20%

profile of v1, /device:TPU:0, one launch (start us, length us, event | category | flops | bytes accessed | tf_op | source)
XLA Modules:
  0.0 216.1 jit_solution(5525549888938246501)
XLA Ops:
  0.6 0.8 slice.26
  1.4 2.4 %collective-permute-start.2 = (s32[2,3]{1,0:T(2,128)S(1)}, s32[2,3]{1,0:T(2,128)S(1)}, u32[]{:S(2)}, u32[]{:S(2)}) collective-permute-start(s32[2,3]{1,0:T(2,128)S(1)} %slice.26), channel_id=1, source_target_pairs={{0,4},{1,5},{2,6},{3,7},{8,12},{9,13},{10,14},{11,15},{16,20},{17,... | collective-permute-start | bytes 80 | tf_op jit(solution)/shard_map/ppermute | solution.py:23
  3.8 1.3 broadcast_in_dim.12.gain
  5.1 0.8 copy.38
  5.9 0.6 pad.8.wt
  6.5 42.6 %gather_all.1 = (bf16[2,256,1536]{2,1,0:T(8,128)(2,1)}, bf16[8,192,768]{2,1,0:T(8,128)(2,1)}, bf16[8,192,768]{2,1,0:T(8,128)(2,1)}, bf16[8,192,256]{2,1,0:T(8,128)(2,1)}, bf16[8,192,128]{2,1,0:T(8,128)(2,1)}) custom-call(bf16[2,64,1536]{2,1,0:T(8,128)(2,1)} %tok.3, f32[1,1536]{1,0:T(1,128)} %broadcast_in_dim.12.gain, bf16[192,768]{1,0:T(8,128)(2,1)} %wg.1, ...), custom_call_target="tpu_custom_call" | custom-call | tf_op jit(solution)/shard_map/gather_all/pallas_call | solution.py:306
  49.1 2.3 %convolution_convert_fusion.1.pre_s = bf16[2,256,256]{2,1,0:T(8,128)(2,1)S(1)} fusion(bf16[2,256,1536]{2,1,0:T(8,128)(2,1)} %get-tuple-element.66.normed.tokens_in, bf16[1536,256,1]{1,0,2:T(8,128)(2,1)} %bitcast.37), kind=kOutput, calls=%fused_computation.1 | convolution fusion | flops 402784256 | bytes 2621440 | tf_op jit(solution)/shard_map/dot_general | solution.py:1715
  51.5 2.3 %collective-permute-start.1 = (bf16[2,8,256]{2,1,0:T(8,128)(2,1)S(1)}, bf16[2,8,256]{2,1,0:T(8,128)(2,1)S(1)}, u32[]{:S(2)}, u32[]{:S(2)}) collective-permute-start(bf16[2,8,256]{2,1,0:T(8,128)(2,1)S(1)} %slice.33), channel_id=1, source_target_pairs={{0,4},{1,5},{2,6},{3,7},{8,12},{9,13},{10,14},{11,15},{16,20},{17,... | collective-permute-start | bytes 24584 | tf_op jit(solution)/shard_map/ppermute | solution.py:23
  53.8 3.1 %convolution_convert_fusion.pre_i = bf16[2,256,768]{2,1,0:T(8,128)(2,1)S(1)} fusion(bf16[2,256,1536]{2,1,0:T(8,128)(2,1)S(1)} %copy-done.11, bf16[1536,768,1]{1,0,2:T(8,128)(2,1)} %bitcast.36), kind=kOutput, calls=%fused_computation | convolution fusion | flops 1208352768 | bytes 4718592 | tf_op jit(solution)/shard_map/dot_general | solution.py:1714
  57.0 1.4 collective-permute-start
  58.4 0.2 slice_reduce_fusion
  58.7 1.3 fusion.4.raw
  60.0 0.1 constant_dynamic-slice_fusion
  60.0 0.6 pad.9.hp
  60.6 0.2 slice_reduce_fusion.1
  60.8 0.1 compare_convert_fusion.2
  61.0 0.6 stack.63.rows
  61.6 0.6 copy-done.20
  62.2 0.0 copy-done.19
  62.2 35.4 %mix_fwd.1 = (f32[2,256,768]{2,1,0:T(8,128)}, f32[2,256,768]{2,1,0:T(8,128)}, f32[2,256,256]{2,1,0:T(8,128)}, f32[2,256,128]{2,1,0:T(8,128)}, bf16[2,128,768]{2,...) custom-call(bf16[2,256,768]{2,1,0:T(8,128)(2,1)} %copy-done.14, ...), custom_call_target="tpu_custom_call" | custom-call | flops 4000000000 | bytes 1048576 | tf_op jit(solution)/shard_map/mix_fwd/pallas_call | solution.py:750
  97.6 20.7 %gate_stage.1 = (f32[2,256,768]{2,1,0:T(8,128)}, bf16[2,256,768]{2,1,0:T(8,128)(2,1)}, bf16[2,128,768]{2,1,0:T(8,128)(2,1)}, bf16[2,256,1536]{2,1,0:T(8,128)(2,1...) custom-call(f32[2,256,768]{2,1,0:T(8,128)} %get-tuple-element.71.y_part, ...), custom_call_target="tpu_custom_call" | custom-call | flops 6000000000 | bytes 1048576 | tf_op jit(solution)/shard_map/gate_stage/pallas_call | solution.py:750
  118.3 36.0 %mix_bwd.1 = (bf16[2,256,768]{2,1,0:T(8,128)(2,1)}, bf16[2,256,256]{2,1,0:T(8,128)(2,1)}, bf16[2,256,128]{2,1,0:T(8,128)(2,1)}, f32[8,768]{1,0:T(8,128)}, f32[8,...) custom-call(f32[2,256,768]{2,1,0:T(8,128)} %get-tuple-element.78.dy_r, ...), custom_call_target="tpu_custom_call" | custom-call | flops 8000000000 | bytes 1048576 | tf_op jit(solution)/shard_map/mix_bwd/pallas_call | solution.py:750
  154.4 51.4 %reduce_all.1 = (f32[2,64,1536]{2,1,0:T(8,128)}, f32[192,768]{1,0:T(8,128)}, f32[192,256]{1,0:T(8,128)}, f32[192,128]{1,0:T(8,128)}, f32[4,16,768]{2,1,0:T(8,128)}) custom-call(bf16[2,256,1536]{2,1,0:T(8,128)(2,1)} %get-tuple-element.66.normed.tokens_in, bf16[2,256,768]{2,1,0:T(8,128)(2,1)} %get-tuple-element.85.dg, ...), custom_call_target="tpu_custom_call" | custom-call | flops 6000000000 | bytes 1048576 | tf_op jit(solution)/shard_map/reduce_all/pallas_call | solution.py:750
  205.9 1.1 copy-done.2
  207.0 1.1 copy-done.5
  208.1 0.9 copy-done.7
  209.0 0.9 copy-done.8
  209.9 0.9 copy-done.9
  210.8 2.9 %emit_all.1 = (bf16[2,64,1536]{2,1,0:T(8,128)(2,1)}, f32[2,64,1536]{2,1,0:T(8,128)}, f32[1,1536]{1,0:T(1,128)S(1)}, f32[192,768]{1,0:T(8,128)}, f32[192,768]{1,0...) custom-call(bf16[2,64,1536]{2,1,0:T(8,128)(2,1)S(1)} %copy-done, ...), custom_call_target="tpu_custom_call" | custom-call | tf_op jit(solution)/shard_map/emit_all/pallas_call | solution.py:1402
  213.7 0.7 copy.41
  214.4 1.1 copy.42
  215.4 0.6 reduce.2
  (49 shorter events, 0.1 us)
Async XLA Ops:
  1.4 59.2 %collective-permute-start.2 = (s32[2,3]{1,0:T(2,128)S(1)}, s32[2,3]{1,0:T(2,128)S(1)}, u32[]{:S(2)}, u32[]{:S(2)}) collective-permute-start(s32[2,3]{1,0:T(2,128)S(1)} %slice.26), channel_id=1, source_target_pairs={{0,4},{1,5},{2,6},{3,7},{8,12},{9,13},{10,14},{11,15},{16,20},{17,... | collective-permute-start | bytes 80 | tf_op jit(solution)/shard_map/ppermute | solution.py:23
  49.1 4.7 %copy-start.11 = (bf16[2,256,1536]{2,1,0:T(8,128)(2,1)S(1)}, bf16[2,256,1536]{2,1,0:T(8,128)(2,1)}, u32[]{:S(2)}) copy-start(bf16[2,256,1536]{2,1,0:T(8,128)(2,1)} %get-tuple-element.66.normed.tokens_in) | copy-start | bytes 4718596
  51.4 5.5 %copy-start.18 = (bf16[2,256,256]{2,1,0:T(8,128)(2,1)}, bf16[2,256,256]{2,1,0:T(8,128)(2,1)S(1)}, u32[]{:S(2)}) copy-start(bf16[2,256,256]{2,1,0:T(8,128)(2,1)S(1)} %convolution_convert_fusion.1.pre_s) | copy-start | bytes 786436
  51.5 10.1 %collective-permute-start.1 = (bf16[2,8,256]{2,1,0:T(8,128)(2,1)S(1)}, bf16[2,8,256]{2,1,0:T(8,128)(2,1)S(1)}, u32[]{:S(2)}, u32[]{:S(2)}) collective-permute-start(bf16[2,8,256]{2,1,0:T(8,128)(2,1)S(1)} %slice.33), channel_id=1, source_target_pairs={{0,4},{1,5},{2,6},{3,7},{8,12},{9,13},{10,14},{11,15},{16,20},{17,... | collective-permute-start | bytes 24584 | tf_op jit(solution)/shard_map/ppermute | solution.py:23
  53.8 4.6 %copy-start.13 = (s32[2,256]{1,0:T(2,128)S(1)}, s32[2,256]{1,0:T(2,128)}, u32[]{:S(2)}) copy-start(s32[2,256]{1,0:T(2,128)} %param.18) | copy-start | bytes 6148
  53.8 4.8 %copy-start.12 = (bf16[8,192,128]{2,1,0:T(8,128)(2,1)S(1)}, bf16[8,192,128]{2,1,0:T(8,128)(2,1)}, u32[]{:S(2)}) copy-start(bf16[8,192,128]{2,1,0:T(8,128)(2,1)} %get-tuple-element.69.wt) | copy-start | bytes 1179652
  56.9 4.7 %copy-start.14 = (bf16[2,256,768]{2,1,0:T(8,128)(2,1)}, bf16[2,256,768]{2,1,0:T(8,128)(2,1)S(1)}, u32[]{:S(2)}) copy-start(bf16[2,256,768]{2,1,0:T(8,128)(2,1)S(1)} %convolution_convert_fusion.pre_i) | copy-start | bytes 2359300
  57.0 3.0 %copy-start.15 = (f32[48]{0:T(128)S(1)}, f32[48]{0:T(128)}, u32[]{:S(2)}) copy-start(f32[48]{0:T(128)} %param.30) | copy-start | bytes 580
  57.0 3.0 %copy-start.16 = (f32[48]{0:T(128)S(1)}, f32[48]{0:T(128)}, u32[]{:S(2)}) copy-start(f32[48]{0:T(128)} %param.29) | copy-start | bytes 580
  57.0 3.0 %copy-start.17 = (f32[48]{0:T(128)S(1)}, f32[48]{0:T(128)}, u32[]{:S(2)}) copy-start(f32[48]{0:T(128)} %param.28) | copy-start | bytes 580
  57.0 4.6 %collective-permute-start = (bf16[2,8,768]{2,1,0:T(8,128)(2,1)S(1)}, bf16[2,8,768]{2,1,0:T(8,128)(2,1)S(1)}, u32[]{:S(2)}, u32[]{:S(2)}) collective-permute-start(bf16[2,8,768]{2,1,0:T(8,128)(2,1)S(1)} %slice.32), channel_id=1, source_target_pairs={{0,4},{1,5},{2,6},{3,7},{8,12},{9,13},{10,14},{11,15},{16,20},{17,... | collective-permute-start | bytes 73736 | tf_op jit(solution)/shard_map/ppermute | solution.py:23
  61.6 0.6 copy-start.20
  61.6 0.6 copy-start.19
  154.3 51.5 %copy-start = (bf16[2,64,1536]{2,1,0:T(8,128)(2,1)S(1)}, bf16[2,64,1536]{2,1,0:T(8,128)(2,1)}, u32[]{:S(2)}) copy-start(bf16[2,64,1536]{2,1,0:T(8,128)(2,1)} %tok.3) | copy-start | bytes 1179652
  154.3 51.5 %copy-start.1 = (f32[2,64,1536]{2,1,0:T(8,128)S(1)}, f32[2,64,1536]{2,1,0:T(8,128)}, u32[]{:S(2)}) copy-start(f32[2,64,1536]{2,1,0:T(8,128)} %get-tuple-element.84.branch) | copy-start | bytes 2359300
  154.3 51.5 %copy-start.3 = (f32[192,768]{1,0:T(8,128)S(1)}, f32[192,768]{1,0:T(8,128)}, u32[]{:S(2)}) copy-start(f32[192,768]{1,0:T(8,128)} %get-tuple-element.98.go) | copy-start | bytes 1769476
  154.3 51.5 %copy-start.4 = (f32[192,768]{1,0:T(8,128)S(1)}, f32[192,768]{1,0:T(8,128)}, u32[]{:S(2)}) copy-start(f32[192,768]{1,0:T(8,128)} %get-tuple-element.94.gg) | copy-start | bytes 1769476
  154.3 51.5 %copy-start.6 = (bf16[2,64,1536]{2,1,0:T(8,128)(2,1)S(1)}, bf16[2,64,1536]{2,1,0:T(8,128)(2,1)}, u32[]{:S(2)}) copy-start(bf16[2,64,1536]{2,1,0:T(8,128)(2,1)} %cot.3) | copy-start | bytes 1179652
  154.4 51.5 %copy-start.10 = (f32[1,1536]{1,0:T(1,128)S(1)}, f32[1,1536]{1,0:T(1,128)}, u32[]{:S(2)}) copy-start(f32[1,1536]{1,0:T(1,128)} %broadcast_in_dim.12.gain) | copy-start | bytes 18436
  205.9 1.1 copy-start.2
  207.0 1.1 copy-start.5
  208.1 0.9 copy-start.7
  209.0 0.9 copy-start.8
  209.9 0.9 copy-start.9

commit v2 on v1

--- a/solution.py
+++ b/solution.py
@@ -316,7 +316,7 @@
             pltpu.SemaphoreType.DMA((4,)),
         ],
         compiler_params=pltpu.CompilerParams(
-            collective_id=0, has_side_effects=True, vmem_limit_bytes=60 << 20
+            collective_id=0, has_side_effects=True, vmem_limit_bytes=28 << 20
         ),
         name="gather_all",
     )(tokens, gain.reshape(1, width), *weights)
@@ -754,7 +754,7 @@
         out_specs=(vm,) * len(outs),
         scratch_shapes=scratch,
         compiler_params=pltpu.CompilerParams(
-            collective_id=number, has_side_effects=True, vmem_limit_bytes=60 << 20
+            collective_id=number, has_side_effects=True, vmem_limit_bytes=28 << 20
         ),
         cost_estimate=pl.CostEstimate(flops=cost, bytes_accessed=1 << 20, transcendentals=0),
         name=name,
@@ -1404,7 +1404,7 @@
         out_shape=outs,
         in_specs=[vm] * 11,
         out_specs=(vm,) * len(outs),
-        compiler_params=pltpu.CompilerParams(vmem_limit_bytes=40 << 20),
+        compiler_params=pltpu.CompilerParams(vmem_limit_bytes=28 << 20),
         name="emit_all",
     )(tok, cot, gain, branch, rows, gg, gi, gs, gt, go, sms)
 

time: 217 us -> 187 us (0.86)
  Pallas kernels: 189 us -> 160 us
  matrix products: 6.67 us -> 2.52 us
  local copies, waits for them, and re-layouts: 12.6 us -> 16.1 us
    pallas_call x4, Pallas kernels: 143 us -> 118 us  [_mixer_call(): pl.pallas_call(kernel, out_shape=outs, in_specs=[vm] * len(ins), out_spec...]
    pallas_call x1, Pallas kernels: 42.6 us -> 38.3 us  [gather_all(): pl.pallas_call(functools.partial(gather_kernel, n), out_shape=(act,) + tu...]
    unnamed x45 -> x55, local copies, waits for them, and re-layouts: 8.18 us -> 10.1 us
  transfers between devices with their start and end apart: 3 -> 3, of which waited for: 0 -> 0; matrix products, arithmetic and copies ran while one was open for 5% -> 5% of each run, Pallas kernels for 20% -> 21%
where the time goes in v2:
time: 187 us; the launch traced here: 186 us
  Pallas kernels  160 us (86%)
  local copies, waits for them, and re-layouts  16.1 us (9%)
  starting transfers between devices  5.98 us (3%)
  matrix products  2.52 us (1%)
    pallas_call x4, Pallas kernels, _mixer_call(): pl.pallas_call(kernel, out_shape=outs, in_specs=[vm] * len(ins), out_spec...  118 us
    pallas_call x1, Pallas kernels, gather_all(): pl.pallas_call(functools.partial(gather_kernel, n), out_shape=(act,) + tu...  38.3 us
    unnamed x55, local copies, waits for them, and re-layouts  10.1 us
    ppermute x3, starting transfers between devices, passed_along(): return lax.ppermute(block, axis, route)  5.98 us
  transfers between devices with their start and end apart: 3, of which 0 were waited for; matrix products, arithmetic and copies ran while one was open for 5% of the time, Pallas kernels for 21%

profile of v2, /device:TPU:0, one launch (start us, length us, event | category | flops | bytes accessed | tf_op | source)
XLA Modules:
  0.0 186.0 jit_solution(349456252839374399)
XLA Ops:
  0.6 0.8 slice.26
  1.4 2.4 %collective-permute-start.2 = (s32[2,3]{1,0:T(2,128)S(1)}, s32[2,3]{1,0:T(2,128)S(1)}, u32[]{:S(2)}, u32[]{:S(2)}) collective-permute-start(s32[2,3]{1,0:T(2,128)S(1)} %slice.26), channel_id=1, source_target_pairs={{0,4},{1,5},{2,6},{3,7},{8,12},{9,13},{10,14},{11,15},{16,20},{17,... | collective-permute-start | bytes 80 | tf_op jit(solution)/shard_map/ppermute | solution.py:23
  3.8 0.7 broadcast_in_dim.12.gain
  4.5 0.8 copy.38
  5.4 1.0 copy-done
  6.3 1.0 copy-done.3
  7.3 1.0 copy-done.4
  8.3 0.9 copy-done.5
  9.2 38.3 %gather_all.1 = (bf16[2,256,1536]{2,1,0:T(8,128)(2,1)S(1)}, bf16[8,192,768]{2,1,0:T(8,128)(2,1)S(1)}, bf16[8,192,768]{2,1,0:T(8,128)(2,1)S(1)}, bf16[8,192,256]{2,1,0:T(8,128)(2,1)S(1)}, bf16[8,192,128]{2,1,0:T(8,128)(2,1)S(1)}) custom-call(bf16[2,64,1536]{2,1,0:T(8,128)(2,1)S(1)} %copy-done, f32[1,1536]{1,0:T(1,128)S(1)} %broadcast_in_dim.12.gain, ...), custom_call_target="tpu_custom_call" | custom-call | tf_op jit(solution)/shard_map/gather_all/pallas_call | solution.py:306
  47.5 0.6 convolution_convert_fusion.1.pre_s
  48.1 1.0 slice.33
  49.2 2.3 %collective-permute-start.1 = (bf16[2,8,256]{2,1,0:T(8,128)(2,1)}, bf16[2,8,256]{2,1,0:T(8,128)(2,1)S(1)}, u32[]{:S(2)}, u32[]{:S(2)}) collective-permute-start(bf16[2,8,256]{2,1,0:T(8,128)(2,1)} %slice.33), channel_id=1, source_target_pairs={{0,4},{1,5},{2,6},{3,7},{8,12},{9,13},{10,14},{11,15},{16,20},{17,... | collective-permute-start | bytes 24584 | tf_op jit(solution)/shard_map/ppermute | solution.py:23
  51.5 1.4 convolution_convert_fusion.pre_i
  53.0 0.6 slice.32
  53.6 1.3 collective-permute-start
  54.9 0.2 slice_reduce_fusion
  55.1 0.6 fusion.4.raw
  56.1 0.6 copy.39
  56.7 0.6 reshape.49
  57.3 0.6 reshape.48
  57.9 0.7 stack.63.rows
  58.7 0.9 copy-done.7
  59.6 1.7 copy-done.10
  61.3 1.0 copy-done.16
  62.3 28.8 %mix_fwd.1 = (f32[2,256,768]{2,1,0:T(8,128)S(1)}, f32[2,256,768]{2,1,0:T(8,128)S(1)}, f32[2,256,256]{2,1,0:T(8,128)S(1)}, f32[2,256,128]{2,1,0:T(8,128)S(1)}, bf...) custom-call(bf16[2,256,768]{2,1,0:T(8,128)(2,1)S(1)} %convolution_co, ...), custom_call_target="tpu_custom_call" | custom-call | flops 4000000000 | bytes 1048576 | tf_op jit(solution)/shard_map/mix_fwd/pallas_call | solution.py:750
  91.1 13.3 %gate_stage.1 = (f32[2,256,768]{2,1,0:T(8,128)S(1)}, bf16[2,256,768]{2,1,0:T(8,128)(2,1)S(1)}, bf16[2,128,768]{2,1,0:T(8,128)(2,1)S(1)}, bf16[2,256,1536]{2,1,0:...) custom-call(f32[2,256,768]{2,1,0:T(8,128)S(1)} %get-tuple-element.71.y_p, ...), custom_call_target="tpu_custom_call" | custom-call | flops 6000000000 | bytes 1048576 | tf_op jit(solution)/shard_map/gate_stage/pallas_call | solution.py:750
  104.5 29.8 %mix_bwd.1 = (bf16[2,256,768]{2,1,0:T(8,128)(2,1)S(1)}, bf16[2,256,256]{2,1,0:T(8,128)(2,1)S(1)}, bf16[2,256,128]{2,1,0:T(8,128)(2,1)S(1)}, f32[8,768]{1,0:T(8,1...) custom-call(f32[2,256,768]{2,1,0:T(8,128)S(1)} %get-tuple-element.78, ...), custom_call_target="tpu_custom_call" | custom-call | flops 8000000000 | bytes 1048576 | tf_op jit(solution)/shard_map/mix_bwd/pallas_call | solution.py:750
  134.3 46.4 %reduce_all.1 = (f32[2,64,1536]{2,1,0:T(8,128)S(1)}, f32[192,768]{1,0:T(8,128)S(1)}, f32[192,256]{1,0:T(8,128)S(1)}, f32[192,128]{1,0:T(8,128)S(1)}, f32[4,16,768]{2,1,0:T(8,128)S(1)}) custom-call(bf16[2,256,1536]{2,1,0:T(8,128)(2,1)S(1)} %get-tuple-element.66.normed.tokens_in, bf16[2,256,768]{2,1,0:T(8,128)(2,1)S(1)} %get-tuple-element.85.dg, ...), custom_call_target="tpu_custom_call" | custom-call | flops 6000000000 | bytes 1048576 | tf_op jit(solution)/shard_map/reduce_all/pallas_call | solution.py:750
  180.7 2.9 %emit_all.1 = (bf16[2,64,1536]{2,1,0:T(8,128)(2,1)}, f32[2,64,1536]{2,1,0:T(8,128)}, f32[1,1536]{1,0:T(1,128)S(1)}, f32[192,768]{1,0:T(8,128)}, f32[192,768]{1,0...) custom-call(bf16[2,64,1536]{2,1,0:T(8,128)(2,1)S(1)} %copy-done.1, ...), custom_call_target="tpu_custom_call" | custom-call | tf_op jit(solution)/shard_map/emit_all/pallas_call | solution.py:1402
  183.6 0.7 copy.41
  184.3 1.1 copy.42
  185.4 0.6 reduce.2
  (59 shorter events, 0.5 us)
Async XLA Ops:
  1.4 54.4 %collective-permute-start.2 = (s32[2,3]{1,0:T(2,128)S(1)}, s32[2,3]{1,0:T(2,128)S(1)}, u32[]{:S(2)}, u32[]{:S(2)}) collective-permute-start(s32[2,3]{1,0:T(2,128)S(1)} %slice.26), channel_id=1, source_target_pairs={{0,4},{1,5},{2,6},{3,7},{8,12},{9,13},{10,14},{11,15},{16,20},{17,... | collective-permute-start | bytes 80 | tf_op jit(solution)/shard_map/ppermute | solution.py:23
  5.3 1.0 copy-start
  6.3 1.0 copy-start.3
  7.3 1.0 copy-start.4
  8.3 0.9 copy-start.5
  47.5 5.4 %copy-start.9 = (bf16[8,192,768]{2,1,0:T(8,128)(2,1)}, bf16[8,192,768]{2,1,0:T(8,128)(2,1)S(1)}, u32[]{:S(2)}) copy-start(bf16[8,192,768]{2,1,0:T(8,128)(2,1)S(1)} %get-tuple-element.70.wg) | copy-start | bytes 7077892
  47.5 5.4 %copy-start.12 = (bf16[8,192,768]{2,1,0:T(8,128)(2,1)}, bf16[8,192,768]{2,1,0:T(8,128)(2,1)S(1)}, u32[]{:S(2)}) copy-start(bf16[8,192,768]{2,1,0:T(8,128)(2,1)S(1)} %get-tuple-element.67.wi) | copy-start | bytes 7077892
  47.5 5.4 %copy-start.14 = (bf16[8,192,256]{2,1,0:T(8,128)(2,1)}, bf16[8,192,256]{2,1,0:T(8,128)(2,1)S(1)}, u32[]{:S(2)}) copy-start(bf16[8,192,256]{2,1,0:T(8,128)(2,1)S(1)} %get-tuple-element.68.ws) | copy-start | bytes 2359300
  48.1 4.8 %copy-start.6 = (bf16[2,256,256]{2,1,0:T(8,128)(2,1)}, bf16[2,256,256]{2,1,0:T(8,128)(2,1)S(1)}, u32[]{:S(2)}) copy-start(bf16[2,256,256]{2,1,0:T(8,128)(2,1)S(1)} %convolution_convert_fusion.1.pre_s) | copy-start | bytes 786436
  49.2 9.5 %collective-permute-start.1 = (bf16[2,8,256]{2,1,0:T(8,128)(2,1)}, bf16[2,8,256]{2,1,0:T(8,128)(2,1)S(1)}, u32[]{:S(2)}, u32[]{:S(2)}) collective-permute-start(bf16[2,8,256]{2,1,0:T(8,128)(2,1)} %slice.33), channel_id=1, source_target_pairs={{0,4},{1,5},{2,6},{3,7},{8,12},{9,13},{10,14},{11,15},{16,20},{17,... | collective-permute-start | bytes 24584 | tf_op jit(solution)/shard_map/ppermute | solution.py:23
  51.5 3.4 %copy-start.22 = (s32[2,256]{1,0:T(2,128)S(1)}, s32[2,256]{1,0:T(2,128)}, u32[]{:S(2)}) copy-start(s32[2,256]{1,0:T(2,128)} %param.18) | copy-start | bytes 6148
  52.9 2.8 %copy-start.23 = (f32[48]{0:T(128)S(1)}, f32[48]{0:T(128)}, u32[]{:S(2)}) copy-start(f32[48]{0:T(128)} %param.30) | copy-start | bytes 580
  52.9 2.8 %copy-start.24 = (f32[48]{0:T(128)S(1)}, f32[48]{0:T(128)}, u32[]{:S(2)}) copy-start(f32[48]{0:T(128)} %param.29) | copy-start | bytes 580
  52.9 2.8 %copy-start.25 = (f32[48]{0:T(128)S(1)}, f32[48]{0:T(128)}, u32[]{:S(2)}) copy-start(f32[48]{0:T(128)} %param.28) | copy-start | bytes 580
  53.0 5.7 %copy-start.2 = (bf16[2,64,1536]{2,1,0:T(8,128)(2,1)S(1)}, bf16[2,64,1536]{2,1,0:T(8,128)(2,1)}, u32[]{:S(2)}) copy-start(bf16[2,64,1536]{2,1,0:T(8,128)(2,1)} %cot.3) | copy-start | bytes 1179652
  53.0 5.7 %copy-start.17 = (f32[4,3072]{1,0:T(4,128)S(1)}, f32[4,3072]{1,0:T(4,128)}, u32[]{:S(2)}) copy-start(f32[4,3072]{1,0:T(4,128)} %taps_i.3) | copy-start | bytes 147460
  53.0 5.7 %copy-start.18 = (f32[3072]{0:T(1024)S(1)}, f32[3072]{0:T(1024)}, u32[]{:S(2)}) copy-start(f32[3072]{0:T(1024)} %param.25) | copy-start | bytes 36868
  53.0 5.7 %copy-start.20 = (f32[4,256]{1,0:T(4,128)S(1)}, f32[4,256]{1,0:T(4,128)}, u32[]{:S(2)}) copy-start(f32[4,256]{1,0:T(4,128)} %taps_s.3) | copy-start | bytes 12292
  53.0 5.7 %copy-start.21 = (f32[256]{0:T(256)S(1)}, f32[256]{0:T(256)}, u32[]{:S(2)}) copy-start(f32[256]{0:T(256)} %param.27) | copy-start | bytes 3076
  53.6 5.0 %collective-permute-start = (bf16[2,8,768]{2,1,0:T(8,128)(2,1)}, bf16[2,8,768]{2,1,0:T(8,128)(2,1)S(1)}, u32[]{:S(2)}, u32[]{:S(2)}) collective-permute-start(bf16[2,8,768]{2,1,0:T(8,128)(2,1)} %slice.32), channel_id=1, source_target_pairs={{0,4},{1,5},{2,6},{3,7},{8,12},{9,13},{10,14},{11,15},{16,20},{17,... | collective-permute-start | bytes 73736 | tf_op jit(solution)/shard_map/ppermute | solution.py:23
  58.7 1.0 copy-start.7
  59.6 1.7 copy-start.10
  61.3 1.0 copy-start.16
  62.3 28.8 %copy-start.19 = (f32[3072]{0:T(1024)S(1)}, f32[3072]{0:T(1024)}, u32[]{:S(2)}) copy-start(f32[3072]{0:T(1024)} %param.31) | copy-start | bytes 36868
  91.1 13.4 %copy-start.8 = (bf16[2,256,256]{2,1,0:T(8,128)(2,1)S(1)}, bf16[2,256,256]{2,1,0:T(8,128)(2,1)}, u32[]{:S(2)}) copy-start(bf16[2,256,256]{2,1,0:T(8,128)(2,1)} %copy-done.6) | copy-start | bytes 786436
  104.4 29.8 %copy-start.11 = (bf16[8,192,768]{2,1,0:T(8,128)(2,1)S(1)}, bf16[8,192,768]{2,1,0:T(8,128)(2,1)}, u32[]{:S(2)}) copy-start(bf16[8,192,768]{2,1,0:T(8,128)(2,1)} %copy-done.9) | copy-start | bytes 7077892
  104.4 29.8 %copy-start.13 = (bf16[8,192,768]{2,1,0:T(8,128)(2,1)S(1)}, bf16[8,192,768]{2,1,0:T(8,128)(2,1)}, u32[]{:S(2)}) copy-start(bf16[8,192,768]{2,1,0:T(8,128)(2,1)} %copy-done.12) | copy-start | bytes 7077892
  104.5 29.8 %copy-start.15 = (bf16[8,192,256]{2,1,0:T(8,128)(2,1)S(1)}, bf16[8,192,256]{2,1,0:T(8,128)(2,1)}, u32[]{:S(2)}) copy-start(bf16[8,192,256]{2,1,0:T(8,128)(2,1)} %copy-done.14) | copy-start | bytes 2359300
  134.3 46.5 %copy-start.1 = (bf16[2,64,1536]{2,1,0:T(8,128)(2,1)S(1)}, bf16[2,64,1536]{2,1,0:T(8,128)(2,1)}, u32[]{:S(2)}) copy-start(bf16[2,64,1536]{2,1,0:T(8,128)(2,1)} %tok.3) | copy-start | bytes 1179652

commit v3 on v2

--- a/solution.py
+++ b/solution.py
@@ -381,6 +381,16 @@
                     copy(box.at[o], box, o, way).wait_send()
 
     return step, final, finish
+
+
+def _line_reduces(n, part, left, right, ssem, rsem):
+    one = lambda s: pl.ds(s, 1)
+    return [
+        _line_reduce(
+            n, part.at[one(s)], left.at[:, one(s)], right.at[:, one(s)], ssem.at[s], rsem.at[s]
+        )
+        for s in range(part.shape[0])
+    ]
 
 
 class _PlaneReduce:
@@ -979,11 +989,12 @@
     seqs, length, width = pre_i.shape
     pairs = width // LANES
     _plane_barrier(n)
-    step_o, final_o, finish_o = _line_reduce(n, po, lo, ro, zs, zr)
+    lines = _line_reduces(n, po, lo, ro, zs, zr)
     planes = (
         _PlaneReduce(go, xo, bo, ps.at[0], pr.at[0]), _PlaneReduce(gg, xg, bg, ps.at[1], pr.at[1])
     )
-    step_o(0)
+    for step, _, _ in lines:
+        step(0)
     for plane in planes:
         plane.begin()
     sm_i[...] = jnp.zeros_like(sm_i)
@@ -1030,11 +1041,12 @@
 
             @pl.when(jnp.logical_and(s == 0, p == 3))
             def _():
+                lines[0][0](1)
                 planes[1].send_far()
 
             @pl.when(jnp.logical_and(s == 0, p == 5))
             def _():
-                step_o(1)
+                lines[0][0](2)
 
             @pl.when(jnp.logical_and(s == 1, p == 2))
             def _():
@@ -1046,7 +1058,7 @@
 
             @pl.when(jnp.logical_and(s == 1, p == 4))
             def _():
-                step_o(2)
+                lines[1][0](1)
 
             ch = pl.ds(pl.multiple_of(p * LANES, LANES), LANES)
             at = pl.ds(pl.multiple_of(t * width + p * LANES, LANES), LANES)
@@ -1117,8 +1129,7 @@
         return 0
 
     lax.fori_loop(0, seqs, one, 0)
-    for k in range(3, n - 1):
-        step_o(k)
+    lines[1][0](2)
     dp, seq = lax.axis_index("dp"), lax.axis_index("seq")
     handed = [
         pltpu.make_async_remote_copy(
@@ -1149,10 +1160,12 @@
             c.wait_send()
 
     planes[1].final(o_gg)
-    final_o(o_po)
+    for s, (_, final, _) in enumerate(lines):
+        final(o_po.at[pl.ds(s, 1)])
     for plane in planes:
         plane.finish()
-    finish_o()
+    for _, _, finish in lines:
+        finish()
 
 
 def mix_bwd(n, dy, u_i, u_s, pre_i, old_i, pre_s, old_s, raw, rows, h0, lam, hp, taps_i, taps_s,
@@ -1197,8 +1210,8 @@
             pltpu.VMEM((seqs, 16, 2 * STATE), F32),
             pltpu.VMEM((seqs, 8, width), F32),
             pltpu.VMEM((seqs, 8, 2 * STATE), F32),
-            pltpu.SemaphoreType.DMA((2, n)),
-            pltpu.SemaphoreType.DMA((2, n)),
+            pltpu.SemaphoreType.DMA((seqs, 2, n)),
+            pltpu.SemaphoreType.DMA((seqs, 2, n)),
             pltpu.SemaphoreType.DMA((2, 7)),
             pltpu.SemaphoreType.DMA((2, 7)),
             pltpu.SemaphoreType.DMA((4,)),
@@ -1228,22 +1241,23 @@
     mb[0, 10:11, 512:640] = sm_h[0:1, :]
     mb[0, 10:11, 640:768] = sm_h[1:2, :]
 
-    for b in range(model // rows):
-        ch = slice(b * rows, (b + 1) * rows)
-        near = slice(b * blocks, (b + 1) * blocks)
-        w = [r[near].reshape(rows, r.shape[2]) for r in (wg, wi, ws, wt)]
-        total = None
-        for s in range(seqs):
+    lines = _line_reduces(n, pg, lg, rg, zs, zr)
+    totals = [None] * (model // rows)
+    for s in range(seqs):
+        for b in range(model // rows):
+            ch = slice(b * rows, (b + 1) * rows)
+            near = slice(b * blocks, (b + 1) * blocks)
             part = None
-            for d, one in zip((dg, di, ds, dr), w):
-                more = _dot(d[s], one, 1, 1)
+            for d, w in zip((dg, di, ds, dr), (wg, wi, ws, wt)):
+                more = _dot(d[s], w[near].reshape(rows, w.shape[2]), 1, 1)
                 part = more if part is None else part + more
             pg[s, :, ch] = part.astype(BF)
             part = jnp.sum(part * normed[s, :, ch].astype(F32), axis=0, keepdims=True)
-            total = part if total is None else total + part
+            totals[b] = part if totals[b] is None else totals[b] + part
+        lines[s][0](0)
+    for b, total in enumerate(totals):
+        ch = slice(b * rows, (b + 1) * rows)
         mb[0, 7 + b // 2 : 8 + b // 2, (b % 2) * rows : (b % 2 + 1) * rows] = total / gain[:, ch]
-    step_g, final_g, finish_g = _line_reduce(n, pg, lg, rg, zs, zr)
-    step_g(0)
     small.copy(0, small.near(0)).start()
     planes = [
         _PlaneReduce(part, pair, box, ps.at[i], pr.at[i])
@@ -1270,18 +1284,17 @@
     planes[1].begin()
     weight(di, gi)
     planes[2].begin()
+    lines[0][0](1)
     small.step(0)
-    step_g(1)
     for p in planes:
         p.send_far()
     small.step(1)
+    lines[0][0](2)
     for p in planes[:2]:
         p.send_near()
     small.step(2)
-    step_g(2)
+    lines[1][0](1)
     planes[2].send_near()
-    for k in range(3, n - 1):
-        step_g(k)
     planes[0].final(o_gs)
     planes[1].final(o_gt)
     quarter = xp.shape[1]
@@ -1289,10 +1302,12 @@
         xp[o] = o_gs[o * quarter : (o + 1) * quarter, :].astype(BF)
     state = _LineSum(n, xp, xb, xo2, es, er)
     state.scatter()
+    lines[1][0](2)
+    state.gather()
     planes[2].final(o_gi)
-    state.gather()
     small.final()
-    final_g(o_pg)
+    for s, (_, final, _) in enumerate(lines):
+        final(o_pg.at[pl.ds(s, 1)])
     state.arrive()
     for o in range(n):
         o_gs[o * quarter : (o + 1) * quarter, :] = xo2[o].astype(F32)
@@ -1300,7 +1315,8 @@
         p.finish()
     state.finish()
     small.finish()
-    finish_g()
+    for _, _, finish in lines:
+        finish()
 
 
 def reduce_all(n, normed, dg, di, ds, dr, wg, wi, ws, wt, gain, sm_i, sm_s, sm_h, g_gain):
@@ -1324,8 +1340,8 @@
         + [
             pltpu.VMEM((6,) + sums, F32),
             quarter, quarter, quarter,
-            pltpu.SemaphoreType.DMA((2, n)),
-            pltpu.SemaphoreType.DMA((2, n)),
+            pltpu.SemaphoreType.DMA((seqs, 2, n)),
+            pltpu.SemaphoreType.DMA((seqs, 2, n)),
             pltpu.SemaphoreType.DMA((3, 7)),
             pltpu.SemaphoreType.DMA((3, 7)),
             pltpu.SemaphoreType.DMA((3 + n,)),

time: 187 us -> 186 us (level)
  no operation moved by 1% of the time
where the time goes in v3:
time: 186 us
  Pallas kernels  159 us (85%)
  local copies, waits for them, and re-layouts  16.1 us (9%)
  starting transfers between devices  5.98 us (3%)
  matrix products  2.52 us (1%)
    pallas_call x4, Pallas kernels, _mixer_call(): pl.pallas_call(kernel, out_shape=outs, in_specs=[vm] * len(ins), out_spec...  118 us
    pallas_call x1, Pallas kernels, gather_all(): pl.pallas_call(functools.partial(gather_kernel, n), out_shape=(act,) + tu...  38.3 us
    unnamed x55, local copies, waits for them, and re-layouts  10.1 us
    ppermute x3, starting transfers between devices, passed_along(): return lax.ppermute(block, axis, route)  5.98 us
  transfers between devices with their start and end apart: 3, of which 0 were waited for; matrix products, arithmetic and copies ran while one was open for 5% of the time, Pallas kernels for 21%

profile of v3, /device:TPU:0, one launch (start us, length us, event | category | flops | bytes accessed | tf_op | source)
XLA Modules:
  0.0 185.9 jit_solution(12543136713381287273)
XLA Ops:
  0.6 0.8 slice.26
  1.4 2.4 %collective-permute-start.2 = (s32[2,3]{1,0:T(2,128)S(1)}, s32[2,3]{1,0:T(2,128)S(1)}, u32[]{:S(2)}, u32[]{:S(2)}) collective-permute-start(s32[2,3]{1,0:T(2,128)S(1)} %slice.26), channel_id=1, source_target_pairs={{0,4},{1,5},{2,6},{3,7},{8,12},{9,13},{10,14},{11,15},{16,20},{17,... | collective-permute-start | bytes 80 | tf_op jit(solution)/shard_map/ppermute | solution.py:23
  3.8 0.7 broadcast_in_dim.12.gain
  4.5 0.8 copy.38
  5.4 1.0 copy-done
  6.3 1.0 copy-done.3
  7.3 1.0 copy-done.4
  8.3 0.9 copy-done.5
  9.2 38.3 %gather_all.1 = (bf16[2,256,1536]{2,1,0:T(8,128)(2,1)S(1)}, bf16[8,192,768]{2,1,0:T(8,128)(2,1)S(1)}, bf16[8,192,768]{2,1,0:T(8,128)(2,1)S(1)}, bf16[8,192,256]{2,1,0:T(8,128)(2,1)S(1)}, bf16[8,192,128]{2,1,0:T(8,128)(2,1)S(1)}) custom-call(bf16[2,64,1536]{2,1,0:T(8,128)(2,1)S(1)} %copy-done, f32[1,1536]{1,0:T(1,128)S(1)} %broadcast_in_dim.12.gain, ...), custom_call_target="tpu_custom_call" | custom-call | tf_op jit(solution)/shard_map/gather_all/pallas_call | solution.py:306
  47.5 0.6 convolution_convert_fusion.1.pre_s
  48.1 1.0 slice.33
  49.2 2.3 %collective-permute-start.1 = (bf16[2,8,256]{2,1,0:T(8,128)(2,1)}, bf16[2,8,256]{2,1,0:T(8,128)(2,1)S(1)}, u32[]{:S(2)}, u32[]{:S(2)}) collective-permute-start(bf16[2,8,256]{2,1,0:T(8,128)(2,1)} %slice.33), channel_id=1, source_target_pairs={{0,4},{1,5},{2,6},{3,7},{8,12},{9,13},{10,14},{11,15},{16,20},{17,... | collective-permute-start | bytes 24584 | tf_op jit(solution)/shard_map/ppermute | solution.py:23
  51.5 1.4 convolution_convert_fusion.pre_i
  53.0 0.6 slice.32
  53.6 1.3 collective-permute-start
  54.9 0.2 slice_reduce_fusion
  55.1 0.6 fusion.4.raw
  56.1 0.6 copy.39
  56.7 0.6 reshape.49
  57.3 0.6 reshape.48
  57.9 0.7 stack.63.rows
  58.7 0.9 copy-done.7
  59.6 1.7 copy-done.10
  61.3 1.0 copy-done.16
  62.3 28.8 %mix_fwd.1 = (f32[2,256,768]{2,1,0:T(8,128)S(1)}, f32[2,256,768]{2,1,0:T(8,128)S(1)}, f32[2,256,256]{2,1,0:T(8,128)S(1)}, f32[2,256,128]{2,1,0:T(8,128)S(1)}, bf...) custom-call(bf16[2,256,768]{2,1,0:T(8,128)(2,1)S(1)} %convolution_co, ...), custom_call_target="tpu_custom_call" | custom-call | flops 4000000000 | bytes 1048576 | tf_op jit(solution)/shard_map/mix_fwd/pallas_call | solution.py:760
  91.1 13.2 %gate_stage.1 = (f32[2,256,768]{2,1,0:T(8,128)S(1)}, bf16[2,256,768]{2,1,0:T(8,128)(2,1)S(1)}, bf16[2,128,768]{2,1,0:T(8,128)(2,1)S(1)}, bf16[2,256,1536]{2,1,0:...) custom-call(f32[2,256,768]{2,1,0:T(8,128)S(1)} %get-tuple-element.71.y_p, ...), custom_call_target="tpu_custom_call" | custom-call | flops 6000000000 | bytes 1048576 | tf_op jit(solution)/shard_map/gate_stage/pallas_call | solution.py:760
  104.3 34.3 %mix_bwd.1 = (bf16[2,256,768]{2,1,0:T(8,128)(2,1)S(1)}, bf16[2,256,256]{2,1,0:T(8,128)(2,1)S(1)}, bf16[2,256,128]{2,1,0:T(8,128)(2,1)S(1)}, f32[8,768]{1,0:T(8,1...) custom-call(f32[2,256,768]{2,1,0:T(8,128)S(1)} %get-tuple-element.78, ...), custom_call_target="tpu_custom_call" | custom-call | flops 8000000000 | bytes 1048576 | tf_op jit(solution)/shard_map/mix_bwd/pallas_call | solution.py:760
  138.7 41.9 %reduce_all.1 = (f32[2,64,1536]{2,1,0:T(8,128)S(1)}, f32[192,768]{1,0:T(8,128)S(1)}, f32[192,256]{1,0:T(8,128)S(1)}, f32[192,128]{1,0:T(8,128)S(1)}, f32[4,16,768]{2,1,0:T(8,128)S(1)}) custom-call(bf16[2,256,1536]{2,1,0:T(8,128)(2,1)S(1)} %get-tuple-element.66.normed.tokens_in, bf16[2,256,768]{2,1,0:T(8,128)(2,1)S(1)} %get-tuple-element.85.dg, ...), custom_call_target="tpu_custom_call" | custom-call | flops 6000000000 | bytes 1048576 | tf_op jit(solution)/shard_map/reduce_all/pallas_call | solution.py:760
  180.6 2.9 %emit_all.1 = (bf16[2,64,1536]{2,1,0:T(8,128)(2,1)}, f32[2,64,1536]{2,1,0:T(8,128)}, f32[1,1536]{1,0:T(1,128)S(1)}, f32[192,768]{1,0:T(8,128)}, f32[192,768]{1,0...) custom-call(bf16[2,64,1536]{2,1,0:T(8,128)(2,1)S(1)} %copy-done.1, ...), custom_call_target="tpu_custom_call" | custom-call | tf_op jit(solution)/shard_map/emit_all/pallas_call | solution.py:1418
  183.5 0.7 copy.41
  184.2 1.1 copy.42
  185.3 0.6 reduce.2
  (59 shorter events, 0.5 us)
Async XLA Ops:
  1.4 54.4 %collective-permute-start.2 = (s32[2,3]{1,0:T(2,128)S(1)}, s32[2,3]{1,0:T(2,128)S(1)}, u32[]{:S(2)}, u32[]{:S(2)}) collective-permute-start(s32[2,3]{1,0:T(2,128)S(1)} %slice.26), channel_id=1, source_target_pairs={{0,4},{1,5},{2,6},{3,7},{8,12},{9,13},{10,14},{11,15},{16,20},{17,... | collective-permute-start | bytes 80 | tf_op jit(solution)/shard_map/ppermute | solution.py:23
  5.3 1.0 copy-start
  6.3 1.0 copy-start.3
  7.3 1.0 copy-start.4
  8.3 0.9 copy-start.5
  47.5 5.4 %copy-start.9 = (bf16[8,192,768]{2,1,0:T(8,128)(2,1)}, bf16[8,192,768]{2,1,0:T(8,128)(2,1)S(1)}, u32[]{:S(2)}) copy-start(bf16[8,192,768]{2,1,0:T(8,128)(2,1)S(1)} %get-tuple-element.70.wg) | copy-start | bytes 7077892
  47.5 5.4 %copy-start.12 = (bf16[8,192,768]{2,1,0:T(8,128)(2,1)}, bf16[8,192,768]{2,1,0:T(8,128)(2,1)S(1)}, u32[]{:S(2)}) copy-start(bf16[8,192,768]{2,1,0:T(8,128)(2,1)S(1)} %get-tuple-element.67.wi) | copy-start | bytes 7077892
  47.5 5.4 %copy-start.14 = (bf16[8,192,256]{2,1,0:T(8,128)(2,1)}, bf16[8,192,256]{2,1,0:T(8,128)(2,1)S(1)}, u32[]{:S(2)}) copy-start(bf16[8,192,256]{2,1,0:T(8,128)(2,1)S(1)} %get-tuple-element.68.ws) | copy-start | bytes 2359300
  48.1 4.8 %copy-start.6 = (bf16[2,256,256]{2,1,0:T(8,128)(2,1)}, bf16[2,256,256]{2,1,0:T(8,128)(2,1)S(1)}, u32[]{:S(2)}) copy-start(bf16[2,256,256]{2,1,0:T(8,128)(2,1)S(1)} %convolution_convert_fusion.1.pre_s) | copy-start | bytes 786436
  49.2 9.5 %collective-permute-start.1 = (bf16[2,8,256]{2,1,0:T(8,128)(2,1)}, bf16[2,8,256]{2,1,0:T(8,128)(2,1)S(1)}, u32[]{:S(2)}, u32[]{:S(2)}) collective-permute-start(bf16[2,8,256]{2,1,0:T(8,128)(2,1)} %slice.33), channel_id=1, source_target_pairs={{0,4},{1,5},{2,6},{3,7},{8,12},{9,13},{10,14},{11,15},{16,20},{17,... | collective-permute-start | bytes 24584 | tf_op jit(solution)/shard_map/ppermute | solution.py:23
  51.5 3.4 %copy-start.22 = (s32[2,256]{1,0:T(2,128)S(1)}, s32[2,256]{1,0:T(2,128)}, u32[]{:S(2)}) copy-start(s32[2,256]{1,0:T(2,128)} %param.18) | copy-start | bytes 6148
  52.9 2.8 %copy-start.23 = (f32[48]{0:T(128)S(1)}, f32[48]{0:T(128)}, u32[]{:S(2)}) copy-start(f32[48]{0:T(128)} %param.30) | copy-start | bytes 580
  52.9 2.8 %copy-start.24 = (f32[48]{0:T(128)S(1)}, f32[48]{0:T(128)}, u32[]{:S(2)}) copy-start(f32[48]{0:T(128)} %param.29) | copy-start | bytes 580
  52.9 2.8 %copy-start.25 = (f32[48]{0:T(128)S(1)}, f32[48]{0:T(128)}, u32[]{:S(2)}) copy-start(f32[48]{0:T(128)} %param.28) | copy-start | bytes 580
  53.0 5.7 %copy-start.2 = (bf16[2,64,1536]{2,1,0:T(8,128)(2,1)S(1)}, bf16[2,64,1536]{2,1,0:T(8,128)(2,1)}, u32[]{:S(2)}) copy-start(bf16[2,64,1536]{2,1,0:T(8,128)(2,1)} %cot.3) | copy-start | bytes 1179652
  53.0 5.7 %copy-start.17 = (f32[4,3072]{1,0:T(4,128)S(1)}, f32[4,3072]{1,0:T(4,128)}, u32[]{:S(2)}) copy-start(f32[4,3072]{1,0:T(4,128)} %taps_i.3) | copy-start | bytes 147460
  53.0 5.7 %copy-start.18 = (f32[3072]{0:T(1024)S(1)}, f32[3072]{0:T(1024)}, u32[]{:S(2)}) copy-start(f32[3072]{0:T(1024)} %param.25) | copy-start | bytes 36868
  53.0 5.7 %copy-start.20 = (f32[4,256]{1,0:T(4,128)S(1)}, f32[4,256]{1,0:T(4,128)}, u32[]{:S(2)}) copy-start(f32[4,256]{1,0:T(4,128)} %taps_s.3) | copy-start | bytes 12292
  53.0 5.7 %copy-start.21 = (f32[256]{0:T(256)S(1)}, f32[256]{0:T(256)}, u32[]{:S(2)}) copy-start(f32[256]{0:T(256)} %param.27) | copy-start | bytes 3076
  53.6 5.0 %collective-permute-start = (bf16[2,8,768]{2,1,0:T(8,128)(2,1)}, bf16[2,8,768]{2,1,0:T(8,128)(2,1)S(1)}, u32[]{:S(2)}, u32[]{:S(2)}) collective-permute-start(bf16[2,8,768]{2,1,0:T(8,128)(2,1)} %slice.32), channel_id=1, source_target_pairs={{0,4},{1,5},{2,6},{3,7},{8,12},{9,13},{10,14},{11,15},{16,20},{17,... | collective-permute-start | bytes 73736 | tf_op jit(solution)/shard_map/ppermute | solution.py:23
  58.7 1.0 copy-start.7
  59.6 1.7 copy-start.10
  61.3 1.0 copy-start.16
  62.3 28.8 %copy-start.19 = (f32[3072]{0:T(1024)S(1)}, f32[3072]{0:T(1024)}, u32[]{:S(2)}) copy-start(f32[3072]{0:T(1024)} %param.31) | copy-start | bytes 36868
  91.1 13.2 %copy-start.8 = (bf16[2,256,256]{2,1,0:T(8,128)(2,1)S(1)}, bf16[2,256,256]{2,1,0:T(8,128)(2,1)}, u32[]{:S(2)}) copy-start(bf16[2,256,256]{2,1,0:T(8,128)(2,1)} %copy-done.6) | copy-start | bytes 786436
  104.3 34.4 %copy-start.11 = (bf16[8,192,768]{2,1,0:T(8,128)(2,1)S(1)}, bf16[8,192,768]{2,1,0:T(8,128)(2,1)}, u32[]{:S(2)}) copy-start(bf16[8,192,768]{2,1,0:T(8,128)(2,1)} %copy-done.9) | copy-start | bytes 7077892
  104.3 34.4 %copy-start.13 = (bf16[8,192,768]{2,1,0:T(8,128)(2,1)S(1)}, bf16[8,192,768]{2,1,0:T(8,128)(2,1)}, u32[]{:S(2)}) copy-start(bf16[8,192,768]{2,1,0:T(8,128)(2,1)} %copy-done.12) | copy-start | bytes 7077892
  104.3 34.4 %copy-start.15 = (bf16[8,192,256]{2,1,0:T(8,128)(2,1)S(1)}, bf16[8,192,256]{2,1,0:T(8,128)(2,1)}, u32[]{:S(2)}) copy-start(bf16[8,192,256]{2,1,0:T(8,128)(2,1)} %copy-done.14) | copy-start | bytes 2359300
  138.7 41.9 %copy-start.1 = (bf16[2,64,1536]{2,1,0:T(8,128)(2,1)S(1)}, bf16[2,64,1536]{2,1,0:T(8,128)(2,1)}, u32[]{:S(2)}) copy-start(bf16[2,64,1536]{2,1,0:T(8,128)(2,1)} %tok.3) | copy-start | bytes 1179652

commit v4 on v3

--- a/solution.py
+++ b/solution.py
@@ -264,62 +264,93 @@
             self.copy(self.own, me, _dev(dp, 1 - seq, t), s).wait_send()
 
 
-def gather_kernel(n, tok, gain, wg, wi, ws, wt, normed, fg, fi, fs, ft, zs, zr, ps, pr, ls):
-    t = lax.axis_index("tensor")
+def gather_kernel(n, tok_far, gain, seg, ws, wt, wi, normed, seg_old, fs, ft, fi,
+                  tok, zs, zr, ps, pr, ls, hs):
+    dp, seq, t = lax.axis_index("dp"), lax.axis_index("seq"), lax.axis_index("tensor")
     rows = tok.shape[1]
+    near = pltpu.make_async_copy(tok_far, tok, ls.at[3])
+    near.start()
     _plane_barrier(n)
     planes = [
         _Plane(own, full, ps.at[i], pr.at[i], ls.at[i])
-        for i, (own, full) in enumerate(((ws, fs), (wt, ft), (wi, fi), (wg, fg)))
+        for i, (own, full) in enumerate(((ws, fs), (wt, ft), (wi, fi)))
     ]
-    for p in planes[:3]:
+    handed = pltpu.make_async_remote_copy(
+        src_ref=seg, dst_ref=seg_old, send_sem=hs.at[0], recv_sem=hs.at[1],
+        device_id=_dev(dp, 1 - seq, t), device_id_type=MESH,
+    )
+
+    @pl.when(seq == 0)
+    def _():
+        handed.start()
+        seg_old[...] = jnp.zeros_like(seg_old)
+
+    for p in planes:
         p.begin()
+    near.wait()
     mine = pl.ds(pl.multiple_of(t * rows, rows), rows)
+    lines = []
     for s in range(tok.shape[0]):
         v = tok[s].astype(F32)
         rms = lax.rsqrt(jnp.mean(v * v, axis=-1, keepdims=True) + EPS)
         normed[s, mine, :] = (v * rms * gain[...]).astype(BF)
-    a = _Line(n, normed, rows, zs, zr)
-    a.step(0)
-    planes[3].begin()
-    for p in planes[:3]:
+        lines.append(_Line(n, normed.at[pl.ds(s, 1)], rows, zs.at[s], zr.at[s]))
+        lines[s].step(0)
+    for line in lines:
+        line.step(1)
+    for p in planes:
         p.forward()
-    a.step(1)
-    planes[3].forward()
-    for p in planes[:3]:
+    lines[0].step(2)
+    for p in planes:
         p.share()
-    for d in range(2, n):
-        a.step(d)
-    planes[3].share()
+    for line in lines[1:]:
+        line.step(2)
+    for d in range(3, n):
+        for line in lines:
+            line.step(d)
     for p in planes:
         p.arrive()
-    a.finish()
+
+    @pl.when(seq == 0)
+    def _():
+        handed.wait_send()
+
+    @pl.when(seq == 1)
+    def _():
+        handed.wait_recv()
+
+    for line in lines:
+        line.finish()
     for p in planes:
         p.finish()
 
 
-def gather_all(n, tokens, gain, weights):
+def gather_all(n, tokens, gain, seg, weights):
     seqs, rows, width = tokens.shape
     vm = pl.BlockSpec(memory_space=pltpu.VMEM)
+    far = pl.BlockSpec(memory_space=pltpu.HBM)
     full = lambda w: jax.ShapeDtypeStruct((8,) + w.shape, w.dtype)
     act = jax.ShapeDtypeStruct((seqs, n * rows, width), BF)
     return pl.pallas_call(
         functools.partial(gather_kernel, n),
-        out_shape=(act,) + tuple(full(w) for w in weights),
-        in_specs=[vm] * 6,
+        out_shape=(act, jax.ShapeDtypeStruct(seg.shape, seg.dtype)) + tuple(full(w) for w in weights),
+        in_specs=[far, vm, vm, far, vm, far],
         out_specs=(vm,) * 5,
         scratch_shapes=[
-            pltpu.SemaphoreType.DMA((2, n)),
-            pltpu.SemaphoreType.DMA((n,)),
-            pltpu.SemaphoreType.DMA((4, 7)),
-            pltpu.SemaphoreType.DMA((4, 7)),
+            pltpu.VMEM(tokens.shape, tokens.dtype),
+            pltpu.SemaphoreType.DMA((seqs, 2, n)),
+            pltpu.SemaphoreType.DMA((seqs, n)),
+            pltpu.SemaphoreType.DMA((3, 7)),
+            pltpu.SemaphoreType.DMA((3, 7)),
             pltpu.SemaphoreType.DMA((4,)),
+            pltpu.SemaphoreType.DMA((2,)),
         ],
         compiler_params=pltpu.CompilerParams(
-            collective_id=0, has_side_effects=True, vmem_limit_bytes=28 << 20
+            collective_id=0, has_side_effects=True, vmem_limit_bytes=16 << 20
         ),
+        cost_estimate=pl.CostEstimate(flops=30 * 10**9, bytes_accessed=1 << 20, transcendentals=0),
         name="gather_all",
-    )(tokens, gain.reshape(1, width), *weights)
+    )(tokens, gain, seg, *weights)
 
 
 def _line_reduce(n, part, left, right, ssem, rsem):
@@ -645,19 +676,74 @@
     return total
 
 
-def mix_fwd_kernel(n, pre_i, old_i, pre_s, old_s, raw, rows, hp, taps_i, bias_i, taps_s, bias_s,
-                   cot, wo, normed, wg, y, u_i, u_s, entry_o, incoming, gate, cot_full, fo,
+def mix_fwd_kernel(n, seg, seg_old, hp, taps_i, bias_i, taps_s, bias_s, cot, wo, wg, normed, wi, ws, wt,
+                   y, u_i, u_s, entry_o, incoming, gate, cot_full, fo, fg,
+                   pre_i, pre_s, old_i, old_s, raw, rows,
                    pad, run3, run_t, bias_m, scores, heads_hl, inflow, zs, zr, ps, pr, ls, hs):
-    t = lax.axis_index("tensor")
+    dp, seq, t = lax.axis_index("dp"), lax.axis_index("seq"), lax.axis_index("tensor")
     seqs, length, width = pre_i.shape
+    model = normed.shape[2]
     pairs = width // LANES
+    wide = 2 * LANES
     _plane_barrier(n)
-    line = _Line(n, cot_full, cot.shape[1], zs, zr, cot)
-    plane = _Plane(wo, fo, ps, pr, ls.at[0])
-    own = pltpu.make_async_copy(cot, line.block(t), ls.at[1])
+    lines = [
+        _Line(n, cot_full.at[pl.ds(s, 1)], cot.shape[1], zs.at[s], zr.at[s], cot.at[pl.ds(s, 1)])
+        for s in range(seqs)
+    ]
+    planes = (_Plane(wg, fg, ps.at[0], pr.at[0], ls.at[0]), _Plane(wo, fo, ps.at[1], pr.at[1], ls.at[1]))
+    whole = _Line(n, cot_full, cot.shape[1], zs, zr)
+    own = pltpu.make_async_copy(cot, whole.block(t), ls.at[2])
     own.start()
-    line.step(0)
-    plane.begin()
+    for line in lines:
+        line.step(0)
+    for plane in planes:
+        plane.begin()
+    flat = normed[...].reshape(seqs * length, model)
+    pre_s[...] = _dot(flat, ws[...].reshape(model, ws.shape[2])).astype(BF).reshape(pre_s.shape)
+
+    def inner_part(c, _):
+        ch = pl.ds(pl.multiple_of(c * wide, wide), wide)
+        part = _dot(flat, wi[:, :, ch].reshape(model, wide))
+        pre_i[:, :, ch] = part.astype(BF).reshape(seqs, length, wide)
+        return 0
+
+    lax.fori_loop(0, width // wide, inner_part, 0)
+    ends = [
+        pltpu.make_async_remote_copy(
+            src_ref=a.at[:, pl.ds(length - 16, 16), :], dst_ref=b,
+            send_sem=hs.at[2 + i], recv_sem=hs.at[4 + i],
+            device_id=_dev(dp, 1 - seq, t), device_id_type=MESH,
+        )
+        for i, (a, b) in enumerate(((pre_i, old_i), (pre_s, old_s)))
+    ]
+
+    @pl.when(seq == 0)
+    def _():
+        for c in ends:
+            c.start()
+        old_i[...] = jnp.zeros_like(old_i)
+        old_s[...] = jnp.zeros_like(old_s)
+
+    raw[...] = _dot(flat, wt[...].reshape(model, LANES)).reshape(raw.shape)
+    for s in range(seqs):
+        now = seg[s : s + 1, :].astype(F32)
+        old = seg_old[s : s + 1, :].astype(F32)
+        both = jnp.broadcast_to(jnp.concatenate([old, now], axis=1), (8, 2 * length))
+        here = jnp.broadcast_to(now, (8, length))
+        place = _iota((8, length), 0)
+        block = jnp.where(place == 0, here, 0.0)
+        others = [pltpu.roll(both, k, 1)[:, length:] for k in range(1, KERNEL)]
+        others += [both[:, length - 1 : length], both[:, 2 * length - 1 :]]
+        for k, other in enumerate(others):
+            block = jnp.where((place == k + 1) & (here == other), 1.0, block)
+        rows[s] = block
+
+    lines[0].step(1)
+
+    @pl.when(seq == 1)
+    def _():
+        for c in ends:
+            c.wait_recv()
 
     def one(s, _):
         rw = rows[s]
@@ -672,7 +758,7 @@
         maps = []
         for half in range(2):
             ch = slice(half * STATE, (half + 1) * STATE)
-            pad[0:8, :] = old_s[s, :, ch].astype(F32)
+            pad[0:8, :] = old_s[s, :, ch].astype(F32)[8:16, :]
             pad[8:, :] = pre_s[s, :, ch].astype(F32)
             u = _conv(pad, marks, taps_s[:, ch], bias_s[:, ch], length)
             u_s[s, :, ch] = u
@@ -681,18 +767,27 @@
         scores[...] = _dot(c_map, b_map, 1, 1)
 
         def pair(p, _):
+            @pl.when(jnp.logical_and(s == 0, p == 4))
+            def _():
+                lines[1].step(1)
+
             @pl.when(jnp.logical_and(s == 1, p == 0))
             def _():
-                line.step(1)
-                plane.forward()
-
-            @pl.when(jnp.logical_and(s == 1, p == 4))
+                for plane in planes:
+                    plane.forward()
+
+            @pl.when(jnp.logical_and(s == 1, p == 1))
             def _():
-                plane.share()
+                lines[0].step(2)
+
+            @pl.when(jnp.logical_and(s == 1, p == 5))
+            def _():
+                lines[1].step(2)
+                planes[0].share()
 
             ch = pl.ds(pl.multiple_of(p * LANES, LANES), LANES)
             at = pl.ds(pl.multiple_of(t * width + p * LANES, LANES), LANES)
-            pad[0:8, :] = old_i[s, :, ch].astype(F32)
+            pad[0:8, :] = old_i[s, :, ch].astype(F32)[8:16, :]
             pad[8:, :] = pre_i[s, :, ch].astype(F32)
             u = _conv(pad, marks, taps_i[:, at], bias_i[:, at], length)
             u_i[s, :, ch] = u
@@ -717,7 +812,6 @@
         return 0
 
     lax.fori_loop(0, seqs, one, 0)
-    dp, seq = lax.axis_index("dp"), lax.axis_index("seq")
     handed = pltpu.make_async_remote_copy(
         src_ref=inflow, dst_ref=incoming, send_sem=hs.at[0], recv_sem=hs.at[1],
         device_id=_dev(dp, 1 - seq, t), device_id_type=MESH,
@@ -728,39 +822,47 @@
         handed.start()
         incoming[...] = jnp.zeros_like(incoming)
 
-    line.step(2)
-    flat = normed[...].reshape(seqs * length, normed.shape[2])
+    planes[1].share()
+    for d in range(3, n):
+        lines[0].step(d)
+    planes[0].arrive()
 
     def gate_part(c, _):
-        ch = pl.ds(pl.multiple_of(c * 2 * LANES, 2 * LANES), 2 * LANES)
-        part = _dot(flat, wg[:, :, ch].reshape(normed.shape[2], 2 * LANES))
-        gate[:, :, ch] = part.reshape(seqs, length, 2 * LANES)
+        ch = pl.ds(pl.multiple_of(c * wide, wide), wide)
+        part = _dot(flat, fg[:, :, ch].reshape(model, wide))
+        gate[:, :, ch] = part.reshape(seqs, length, wide)
         return 0
 
-    lax.fori_loop(0, width // (2 * LANES), gate_part, 0)
+    lax.fori_loop(0, width // wide, gate_part, 0)
     for d in range(3, n):
-        line.step(d)
-    plane.arrive()
+        lines[1].step(d)
+    planes[1].arrive()
     own.wait()
 
     @pl.when(seq == 0)
     def _():
         handed.wait_send()
+        for c in ends:
+            c.wait_send()
 
     @pl.when(seq == 1)
     def _():
         handed.wait_recv()
 
-    line.finish()
-    plane.finish()
-
-
-def _mixer_call(kernel, ins, outs, scratch, name, cost, number):
+    for line in lines:
+        line.finish()
+    for plane in planes:
+        plane.finish()
+
+
+def _mixer_call(kernel, ins, outs, scratch, name, cost, number, far=()):
     vm = pl.BlockSpec(memory_space=pltpu.VMEM)
     return pl.pallas_call(
         kernel,
         out_shape=outs,
-        in_specs=[vm] * len(ins),
+        in_specs=[
+            pl.BlockSpec(memory_space=pltpu.HBM if i in far else pltpu.VMEM) for i in range(len(ins))
+        ],
         out_specs=(vm,) * len(outs),
         scratch_shapes=scratch,
         compiler_params=pltpu.CompilerParams(
@@ -771,14 +873,13 @@
     )(*ins)
 
 
-def mix_fwd(n, pre_i, old_i, pre_s, old_s, raw, rows, hp, taps_i, bias_i, taps_s, bias_s, cot, wo,
-            normed, wg):
-    seqs, length, width = pre_i.shape
+def mix_fwd(n, seg, seg_old, hp, taps_i, bias_i, taps_s, bias_s, cot, wo, wg, normed, wi, ws, wt):
+    seqs, length, model = normed.shape
+    width = wi.shape[2]
     sd = jax.ShapeDtypeStruct
     return _mixer_call(
         functools.partial(mix_fwd_kernel, n),
-        (pre_i, old_i, pre_s, old_s, raw, rows, hp, taps_i, bias_i, taps_s, bias_s, cot, wo,
-         normed, wg),
+        (seg, seg_old, hp, taps_i, bias_i, taps_s, bias_s, cot, wo, wg, normed, wi, ws, wt),
         (
             sd((seqs, length, width), F32),
             sd((seqs, length, width), F32),
@@ -786,8 +887,15 @@
             sd((seqs, length, LANES), F32),
             sd((seqs, STATE, width), BF),
             sd((seqs, length, width), F32),
-            sd((seqs, length, cot.shape[2]), BF),
+            sd((seqs, length, model), BF),
             sd((8,) + wo.shape, BF),
+            sd((8,) + wg.shape, BF),
+            sd((seqs, length, width), BF),
+            sd((seqs, length, 2 * STATE), BF),
+            sd((seqs, 16, width), BF),
+            sd((seqs, 16, 2 * STATE), BF),
+            sd((seqs, length, LANES), F32),
+            sd((seqs, 8, length), F32),
         ),
         [
             pltpu.VMEM((8 + length, LANES), F32),
@@ -797,16 +905,17 @@
             pltpu.VMEM((length, length), F32),
             pltpu.VMEM((2, length, 2 * LANES), BF),
             pltpu.VMEM((seqs, STATE, width), BF),
-            pltpu.SemaphoreType.DMA((2, n)),
-            pltpu.SemaphoreType.DMA((n,)),
-            pltpu.SemaphoreType.DMA((7,)),
-            pltpu.SemaphoreType.DMA((7,)),
-            pltpu.SemaphoreType.DMA((2,)),
-            pltpu.SemaphoreType.DMA((2,)),
+            pltpu.SemaphoreType.DMA((seqs, 2, n)),
+            pltpu.SemaphoreType.DMA((seqs, n)),
+            pltpu.SemaphoreType.DMA((2, 7)),
+            pltpu.SemaphoreType.DMA((2, 7)),
+            pltpu.SemaphoreType.DMA((3,)),
+            pltpu.SemaphoreType.DMA((6,)),
         ],
         "mix_fwd",
-        4 * 10**9,
+        30 * 10**9,
         3,
+        (7, 8, 9),
     )
 
 
@@ -1041,8 +1150,8 @@
 
             @pl.when(jnp.logical_and(s == 0, p == 3))
             def _():
+                planes[1].send_far()
                 lines[0][0](1)
-                planes[1].send_far()
 
             @pl.when(jnp.logical_and(s == 0, p == 5))
             def _():
@@ -1102,7 +1211,7 @@
             skip = _dot(_split(hp[...], 2), spread)[2:3, :]
             sm_i[5:6, ch] += jnp.sum(dy * x, axis=0, keepdims=True)
             du = (dxd * dl + skip * dy) * (sg * (1.0 + u * (1.0 - sg)))
-            pad[0:8, :] = old_i[s, :, ch].astype(F32)
+            pad[0:8, :] = old_i[s, :, ch].astype(F32)[8:16, :]
             pad[8:, :] = pre_i[s, :, ch].astype(F32)
             conv_back(du, marks, taps_i[:, at], s, ch, d_i, head_i, tail_i, sm_i)
             return 0
@@ -1112,7 +1221,7 @@
         grads = (d_b[...] + _dot(ds, c_map, 0, 0), d_c[...] + _dot(ds, b_map))
         for half, (g, u, sg) in enumerate(zip(grads, (ub, uc), (sb, sc))):
             ch = slice(half * STATE, (half + 1) * STATE)
-            pad[0:8, :] = old_s[s, :, ch].astype(F32)
+            pad[0:8, :] = old_s[s, :, ch].astype(F32)[8:16, :]
             pad[8:, :] = pre_s[s, :, ch].astype(F32)
             du = g * (sg * (1.0 + u * (1.0 - sg)))
             conv_back(du, marks, taps_s[:, ch], s, ch, d_s, head_s, tail_s, sm_s)
@@ -1241,6 +1350,31 @@
     mb[0, 10:11, 512:640] = sm_h[0:1, :]
     mb[0, 10:11, 640:768] = sm_h[1:2, :]
 
+    planes = [
+        _PlaneReduce(part, pair, box, ps.at[i], pr.at[i])
+        for i, (part, pair, box) in enumerate(((gs, xs, bs), (gt, xt, bt), (gi, xi, bi)))
+    ]
+
+    def weight(d, out):
+        def one(b, _):
+            ch = pl.ds(pl.multiple_of(b * rows, LANES), rows)
+            total = None
+            for s in range(seqs):
+                part = _dot(normed[s, :, ch], d[s], 0, 0)
+                total = part if total is None else total + part
+            out[pl.ds(b * blocks, blocks)] = total.reshape(
+                blocks, wi.shape[1], d.shape[2]
+            ).astype(BF)
+            return 0
+
+        lax.fori_loop(0, model // rows, one, 0)
+
+    weight(ds, gs)
+    planes[0].begin()
+    weight(dr, gt)
+    planes[1].begin()
+    weight(di, gi)
+    planes[2].begin()
     lines = _line_reduces(n, pg, lg, rg, zs, zr)
     totals = [None] * (model // rows)
     for s in range(seqs):
@@ -1259,31 +1393,6 @@
         ch = slice(b * rows, (b + 1) * rows)
         mb[0, 7 + b // 2 : 8 + b // 2, (b % 2) * rows : (b % 2 + 1) * rows] = total / gain[:, ch]
     small.copy(0, small.near(0)).start()
-    planes = [
-        _PlaneReduce(part, pair, box, ps.at[i], pr.at[i])
-        for i, (part, pair, box) in enumerate(((gs, xs, bs), (gt, xt, bt), (gi, xi, bi)))
-    ]
-
-    def weight(d, out):
-        def one(b, _):
-            ch = pl.ds(pl.multiple_of(b * rows, LANES), rows)
-            total = None
-            for s in range(seqs):
-                part = _dot(normed[s, :, ch], d[s], 0, 0)
-                total = part if total is None else total + part
-            out[pl.ds(b * blocks, blocks)] = total.reshape(
-                blocks, wi.shape[1], d.shape[2]
-            ).astype(BF)
-            return 0
-
-        lax.fori_loop(0, model // rows, one, 0)
-
-    weight(ds, gs)
-    planes[0].begin()
-    weight(dr, gt)
-    planes[1].begin()
-    weight(di, gi)
-    planes[2].begin()
     lines[0][0](1)
     small.step(0)
     for p in planes:
@@ -1713,49 +1822,23 @@
     tensor_rank = lax.axis_index("tensor")
     heads = step_proj.shape[1]
     step_wide = jnp.pad(step_proj, ((0, 0), (0, 128 - heads)))
-    normed, g8, i8, s8, t8 = gather_all(
-        tensor_count,
-        tokens,
-        input_gain,
-        (gate_proj, inner_proj, state_proj, step_wide),
-    )
-    width = tokens.shape[2]
-    inner_full = i8.reshape(width, -1)
-    state_full = s8.reshape(width, -1)
-    step_full = t8.reshape(width, -1)
-    width_here = inner_full.shape[1]
-    heads_here = heads
-    head_start = tensor_rank * heads_here
-    margin = 8
-    inner_low = jnp.dot(normed, inner_full, preferred_element_type=jnp.float32).astype(jnp.bfloat16)
-    state_low = jnp.dot(normed, state_full, preferred_element_type=jnp.float32).astype(jnp.bfloat16)
-    prior_inner, prior_state = passed_along(
-        (inner_low[:, -margin:], state_low[:, -margin:]), "seq", 1
-    )
-    step_raw = jnp.dot(normed, step_full, preferred_element_type=jnp.float32)
-    prior_seg = passed_along(segments[:, 1 - KERNEL :], "seq", 1)
-    seg_padded = jnp.concatenate([prior_seg, segments], axis=1)
-    length = segments.shape[1]
-    same = [
-        seg_padded[:, KERNEL - 1 - k : KERNEL - 1 - k + length] == segments for k in range(1, KERNEL)
-    ]
-    same += [segments == prior_seg[:, -1:], segments == segments[:, -1:]]
-    rows = jnp.stack(
-        [segments.astype(jnp.float32)]
-        + [m.astype(jnp.float32) for m in same]
-        + [jnp.zeros(segments.shape, jnp.float32)] * 2,
-        axis=1,
+    gain_row = input_gain[None]
+    normed, seg_old, s8, t8, i8 = gather_all(
+        tensor_count, tokens, gain_row, segments, (state_proj, step_wide, inner_proj)
     )
     heads_param = jnp.pad(
         lax.dynamic_slice_in_dim(
-            jnp.stack([step_bias, log_rates, skip_gain]), head_start, heads_here, 1
+            jnp.stack([step_bias, log_rates, skip_gain]), tensor_rank * heads, heads, 1
         ),
-        ((0, 5), (0, LANES - heads_here)),
-    )
-    y_part, u_inner, u_state, entry, incoming, gate_in, cot_rows, o8 = mix_fwd(
-        tensor_count, inner_low, prior_inner, state_low, prior_state, step_raw, rows, heads_param,
-        conv_inner, inner_bias[None], conv_state, state_bias[None], cotangent, output_proj.T,
-        normed, g8,
+        ((0, 5), (0, LANES - heads)),
+    )
+    (
+        y_part, u_inner, u_state, entry, incoming, gate_in, cot_rows, o8, g8,
+        inner_low, state_low, prior_inner, prior_state, step_raw, rows,
+    ) = mix_fwd(
+        tensor_count, segments, seg_old, heads_param,
+        conv_inner, inner_bias[None], conv_state, state_bias[None],
+        cotangent, output_proj.T, gate_proj, normed, i8, s8, t8,
     )
     grad_mixed, grad_gate_in, outgoing_grad, partial_out, grad_output, grad_gate, grad_gain = gate_stage(
         tensor_count, y_part, u_state, entry, incoming, gate_in, cot_rows, o8, gated_gain[None], normed
@@ -1767,7 +1850,6 @@
         step_raw, rows, incoming, outgoing_grad, heads_param, conv_inner, conv_state,
         partial_out, grad_output, grad_gate,
     )
-    gain_row = input_gain[None]
     grad_rows, shard_inner, shard_state, shard_step, sms = reduce_all(
         tensor_count, normed, grad_gate_in, d_inner, d_state, d_step, g8, i8, s8, t8, gain_row,
         sm_i, sm_s, sm_h, grad_gain,

time: 186 us -> 167 us (0.90)
  local copies, waits for them, and re-layouts: 16.1 us -> 6.95 us
  starting transfers between devices: 5.98 us -> 0 us
  matrix products: 2.52 us -> 0 us
    ppermute x3 -> x0, starting transfers between devices: 5.98 us -> none  [passed_along(): return lax.ppermute(block, axis, route)]
    unnamed x55 -> x31, local copies, waits for them, and re-layouts: 10.1 us -> 6.15 us
    slice x5 -> x0, local copies, waits for them, and re-layouts: 2.77 us -> none  [the longest x1 1.04 us: per_device_fast(): state_low[:, -margin:]]
    dot_general x3 -> x0, matrix products: 2.52 us -> none  [the longest x1 1.38 us: per_device_fast(): jnp.dot(normed, inner_full, preferred_element_type=jnp.float32)]
    another operation x8 -> x0, local copies, waits for them, and re-layouts: 2.49 us -> none  [per_device_fast(): jnp.stack([segments.astype(jnp.float32)] + [m.astype(jnp.float32) for m i...]
  transfers between devices with their start and end apart: 3 -> 0, of which waited for: 0 -> 0; matrix products, arithmetic and copies ran while one was open for 5% -> 0% of each run, Pallas kernels for 21% -> 0%
where the time goes in v4:
time: 167 us
  Pallas kernels  158 us (95%)
  local copies, waits for them, and re-layouts  6.95 us (4%)
    pallas_call x4, Pallas kernels, _mixer_call(): pl.pallas_call(kernel, out_shape=outs, in_specs=[pl.BlockSpec(memory_spac...  122 us
    pallas_call x1, Pallas kernels, gather_all(): pl.pallas_call(functools.partial(gather_kernel, n), out_shape=(act, jax.S...  32.7 us
    unnamed x31, local copies, waits for them, and re-layouts  6.15 us

profile of v4, /device:TPU:0, one launch (start us, length us, event | category | flops | bytes accessed | tf_op | source)
XLA Modules:
  0.0 166.8 jit_solution(2519201023142952999)
XLA Ops:
  0.7 0.7 pad_maximum_fusion
  1.3 0.1 constant_dynamic-slice_fusion
  1.4 0.7 broadcast_in_dim.12.gain
  2.1 0.8 copy.33
  3.0 0.0 copy-start
  3.0 1.0 copy-done
  4.0 1.0 copy-done.3
  4.9 0.9 copy-done.6
  5.8 0.7 copy-done.11
  6.5 0.0 copy-start.8
  6.5 0.0 copy-start.10
  6.5 0.0 copy-start.12
  6.6 0.0 copy-start.13
  6.6 32.7 %gather_all.1 = (bf16[2,256,1536]{2,1,0:T(8,128)(2,1)S(1)}, s32[2,256]{1,0:T(2,128)S(1)}, bf16[8,192,256]{2,1,0:T(8,128)(2,1)S(1)}, bf16[8,192,128]{2,1,0:T(8,128)(2,1)S(1)}, bf16[8,192,768]{2,1,0:T(8,128)(2,1)S(1)}) custom-call(bf16[2,64,1536]{2,1,0:T(8,128)(2,1)S(1)} %copy-done, f32[1,1536]{1,0:T(1,128)S(1)} %broadcast_in_dim.12.gain, ...), custom_call_target="tpu_custom_call" | custom-call | flops 30000001024 | bytes 1048576 | tf_op jit(solution)/shard_map/gather_all/pallas_call | solution.py:334
  39.3 0.0 copy-done.2
  39.3 0.0 copy-done.4
  39.3 0.0 copy-done.5
  39.3 0.0 copy-done.7
  39.3 0.0 copy-done.8
  39.3 0.0 copy-done.10
  39.4 0.0 copy-done.12
  39.4 0.0 copy-done.13
  39.4 0.0 copy-start.9
  39.4 27.7 %mix_fwd.1 = (f32[2,256,768]{2,1,0:T(8,128)S(1)}, f32[2,256,768]{2,1,0:T(8,128)S(1)}, f32[2,256,256]{2,1,0:T(8,128)S(1)}, f32[2,256,128]{2,1,0:T(8,128)S(1)}, bf...) custom-call(s32[2,256]{1,0:T(2,128)S(1)} %copy-done.12, ...), custom_call_target="tpu_custom_call" | custom-call | flops 30000001024 | bytes 1048576 | tf_op jit(solution)/shard_map/mix_fwd/pallas_call | solution.py:860
  67.1 14.1 %gate_stage.1 = (f32[2,256,768]{2,1,0:T(8,128)S(1)}, bf16[2,256,768]{2,1,0:T(8,128)(2,1)S(1)}, bf16[2,128,768]{2,1,0:T(8,128)(2,1)S(1)}, bf16[2,256,1536]{2,1,0:...) custom-call(f32[2,256,768]{2,1,0:T(8,128)S(1)} %get-tuple-element.78.y_p, ...), custom_call_target="tpu_custom_call" | custom-call | flops 6000000000 | bytes 1048576 | tf_op jit(solution)/shard_map/gate_stage/pallas_call | solution.py:860
  81.2 34.3 %mix_bwd.1 = (bf16[2,256,768]{2,1,0:T(8,128)(2,1)S(1)}, bf16[2,256,256]{2,1,0:T(8,128)(2,1)S(1)}, bf16[2,256,128]{2,1,0:T(8,128)(2,1)S(1)}, f32[8,768]{1,0:T(8,1...) custom-call(f32[2,256,768]{2,1,0:T(8,128)S(1)} %get-tuple-element.85, ...), custom_call_target="tpu_custom_call" | custom-call | flops 8000000000 | bytes 1048576 | tf_op jit(solution)/shard_map/mix_bwd/pallas_call | solution.py:860
  115.5 0.0 copy-start.1
  115.5 46.0 %reduce_all.1 = (f32[2,64,1536]{2,1,0:T(8,128)S(1)}, f32[192,768]{1,0:T(8,128)S(1)}, f32[192,256]{1,0:T(8,128)S(1)}, f32[192,128]{1,0:T(8,128)S(1)}, f32[4,16,768]{2,1,0:T(8,128)S(1)}) custom-call(bf16[2,256,1536]{2,1,0:T(8,128)(2,1)S(1)} %get-tuple-element.74.normed.tokens_in, bf16[2,256,768]{2,1,0:T(8,128)(2,1)S(1)} %get-tuple-element.98.dg, ...), custom_call_target="tpu_custom_call" | custom-call | flops 6000000000 | bytes 1048576 | tf_op jit(solution)/shard_map/reduce_all/pallas_call | solution.py:860
  161.5 2.9 %emit_all.1 = (bf16[2,64,1536]{2,1,0:T(8,128)(2,1)}, f32[2,64,1536]{2,1,0:T(8,128)}, f32[1,1536]{1,0:T(1,128)S(1)}, f32[192,768]{1,0:T(8,128)}, f32[192,768]{1,0...) custom-call(bf16[2,64,1536]{2,1,0:T(8,128)(2,1)S(1)} %copy-done.1, ...), custom_call_target="tpu_custom_call" | custom-call | tf_op jit(solution)/shard_map/emit_all/pallas_call | solution.py:1527
  164.4 0.6 reduce
  165.1 0.7 copy.34
  165.7 1.1 copy.35
  (11 shorter events, 0.0 us)
Async XLA Ops:
  3.0 1.0 copy-start
  4.0 1.0 copy-start.3
  4.9 0.9 copy-start.6
  5.8 0.7 copy-start.11
  6.5 32.8 %copy-start.2 = (bf16[2,64,1536]{2,1,0:T(8,128)(2,1)S(1)}, bf16[2,64,1536]{2,1,0:T(8,128)(2,1)}, u32[]{:S(2)}) copy-start(bf16[2,64,1536]{2,1,0:T(8,128)(2,1)} %cot.3) | copy-start | bytes 1179652
  6.5 32.8 %copy-start.4 = (bf16[768,192]{0,1:T(8,128)(2,1)S(1)}, bf16[768,192]{0,1:T(8,128)(2,1)}, u32[]{:S(2)}) copy-start(bf16[768,192]{0,1:T(8,128)(2,1)} %param.32) | copy-start | bytes 884740
  6.5 32.8 %copy-start.5 = (bf16[192,768]{1,0:T(8,128)(2,1)S(1)}, bf16[192,768]{1,0:T(8,128)(2,1)}, u32[]{:S(2)}) copy-start(bf16[192,768]{1,0:T(8,128)(2,1)} %wg.1) | copy-start | bytes 884740
  6.5 32.8 %copy-start.7 = (f32[4,3072]{1,0:T(4,128)S(1)}, f32[4,3072]{1,0:T(4,128)}, u32[]{:S(2)}) copy-start(f32[4,3072]{1,0:T(4,128)} %taps_i.3) | copy-start | bytes 147460
  6.5 32.8 %copy-start.8 = (f32[3072]{0:T(1024)S(1)}, f32[3072]{0:T(1024)}, u32[]{:S(2)}) copy-start(f32[3072]{0:T(1024)} %param.25) | copy-start | bytes 36868
  6.5 32.8 %copy-start.10 = (f32[4,256]{1,0:T(4,128)S(1)}, f32[4,256]{1,0:T(4,128)}, u32[]{:S(2)}) copy-start(f32[4,256]{1,0:T(4,128)} %taps_s.3) | copy-start | bytes 12292
  6.5 32.8 %copy-start.12 = (s32[2,256]{1,0:T(2,128)S(1)}, s32[2,256]{1,0:T(2,128)}, u32[]{:S(2)}) copy-start(s32[2,256]{1,0:T(2,128)} %seg.3) | copy-start | bytes 6148
  6.6 32.8 %copy-start.13 = (f32[256]{0:T(256)S(1)}, f32[256]{0:T(256)}, u32[]{:S(2)}) copy-start(f32[256]{0:T(256)} %param.27) | copy-start | bytes 3076
  39.4 27.7 %copy-start.9 = (f32[3072]{0:T(1024)S(1)}, f32[3072]{0:T(1024)}, u32[]{:S(2)}) copy-start(f32[3072]{0:T(1024)} %param.31) | copy-start | bytes 36868
  115.5 46.0 %copy-start.1 = (bf16[2,64,1536]{2,1,0:T(8,128)(2,1)S(1)}, bf16[2,64,1536]{2,1,0:T(8,128)(2,1)}, u32[]{:S(2)}) copy-start(bf16[2,64,1536]{2,1,0:T(8,128)(2,1)} %tok.1) | copy-start | bytes 1179652

commit v5 on v4

--- a/solution.py
+++ b/solution.py
@@ -264,12 +264,16 @@
             self.copy(self.own, me, _dev(dp, 1 - seq, t), s).wait_send()
 
 
-def gather_kernel(n, tok_far, gain, seg, ws, wt, wi, normed, seg_old, fs, ft, fi,
-                  tok, zs, zr, ps, pr, ls, hs):
+def gather_kernel(n, tok_far, gain, seg, ws, wt_t, wi, normed, seg_old, fs, ft, fi,
+                  tok, wt, zs, zr, ps, pr, ls, hs):
     dp, seq, t = lax.axis_index("dp"), lax.axis_index("seq"), lax.axis_index("tensor")
     rows = tok.shape[1]
     near = pltpu.make_async_copy(tok_far, tok, ls.at[3])
     near.start()
+    v = wt_t[...].astype(F32)
+    v = jnp.concatenate([v, jnp.zeros((LANES - v.shape[0], v.shape[1]), F32)], axis=0)
+    v = jnp.concatenate([v, jnp.zeros((LANES, 256 - v.shape[1]), F32)], axis=1)
+    wt[...] = v.T[: wt.shape[0], :].astype(BF)
     _plane_barrier(n)
     planes = [
         _Plane(own, full, ps.at[i], pr.at[i], ls.at[i])
@@ -329,15 +333,20 @@
     seqs, rows, width = tokens.shape
     vm = pl.BlockSpec(memory_space=pltpu.VMEM)
     far = pl.BlockSpec(memory_space=pltpu.HBM)
-    full = lambda w: jax.ShapeDtypeStruct((8,) + w.shape, w.dtype)
+    wide = (weights[1].shape[1], LANES)
+    full = lambda *shape: jax.ShapeDtypeStruct((8,) + shape, BF)
     act = jax.ShapeDtypeStruct((seqs, n * rows, width), BF)
     return pl.pallas_call(
         functools.partial(gather_kernel, n),
-        out_shape=(act, jax.ShapeDtypeStruct(seg.shape, seg.dtype)) + tuple(full(w) for w in weights),
+        out_shape=(
+            act, jax.ShapeDtypeStruct(seg.shape, seg.dtype),
+            full(*weights[0].shape), full(*wide), full(*weights[2].shape),
+        ),
         in_specs=[far, vm, vm, far, vm, far],
         out_specs=(vm,) * 5,
         scratch_shapes=[
             pltpu.VMEM(tokens.shape, tokens.dtype),
+            pltpu.VMEM(wide, BF),
             pltpu.SemaphoreType.DMA((seqs, 2, n)),
             pltpu.SemaphoreType.DMA((seqs, n)),
             pltpu.SemaphoreType.DMA((3, 7)),
@@ -1144,26 +1153,23 @@
             acc[...] = jnp.zeros_like(acc)
 
         def pair(p, _):
-            @pl.when(jnp.logical_and(s == 0, p == 2))
-            def _():
-                planes[0].send_far()
-
             @pl.when(jnp.logical_and(s == 0, p == 3))
             def _():
-                planes[1].send_far()
                 lines[0][0](1)
 
-            @pl.when(jnp.logical_and(s == 0, p == 5))
+            @pl.when(jnp.logical_and(s == 0, p == 4))
+            def _():
+                for plane in planes:
+                    plane.send_far()
+
+            @pl.when(jnp.logical_and(s == 1, p == 0))
             def _():
                 lines[0][0](2)
 
-            @pl.when(jnp.logical_and(s == 1, p == 2))
+            @pl.when(jnp.logical_and(s == 1, p == 3))
             def _():
-                planes[0].send_near()
-
-            @pl.when(jnp.logical_and(s == 1, p == 5))
-            def _():
-                planes[1].send_near()
+                for plane in planes:
+                    plane.send_near()
 
             @pl.when(jnp.logical_and(s == 1, p == 4))
             def _():
@@ -1350,31 +1356,6 @@
     mb[0, 10:11, 512:640] = sm_h[0:1, :]
     mb[0, 10:11, 640:768] = sm_h[1:2, :]
 
-    planes = [
-        _PlaneReduce(part, pair, box, ps.at[i], pr.at[i])
-        for i, (part, pair, box) in enumerate(((gs, xs, bs), (gt, xt, bt), (gi, xi, bi)))
-    ]
-
-    def weight(d, out):
-        def one(b, _):
-            ch = pl.ds(pl.multiple_of(b * rows, LANES), rows)
-            total = None
-            for s in range(seqs):
-                part = _dot(normed[s, :, ch], d[s], 0, 0)
-                total = part if total is None else total + part
-            out[pl.ds(b * blocks, blocks)] = total.reshape(
-                blocks, wi.shape[1], d.shape[2]
-            ).astype(BF)
-            return 0
-
-        lax.fori_loop(0, model // rows, one, 0)
-
-    weight(ds, gs)
-    planes[0].begin()
-    weight(dr, gt)
-    planes[1].begin()
-    weight(di, gi)
-    planes[2].begin()
     lines = _line_reduces(n, pg, lg, rg, zs, zr)
     totals = [None] * (model // rows)
     for s in range(seqs):
@@ -1388,22 +1369,48 @@
             pg[s, :, ch] = part.astype(BF)
             part = jnp.sum(part * normed[s, :, ch].astype(F32), axis=0, keepdims=True)
             totals[b] = part if totals[b] is None else totals[b] + part
-        lines[s][0](0)
+        if s == 0:
+            lines[s][0](0)
     for b, total in enumerate(totals):
         ch = slice(b * rows, (b + 1) * rows)
         mb[0, 7 + b // 2 : 8 + b // 2, (b % 2) * rows : (b % 2 + 1) * rows] = total / gain[:, ch]
     small.copy(0, small.near(0)).start()
+    planes = [
+        _PlaneReduce(part, pair, box, ps.at[i], pr.at[i])
+        for i, (part, pair, box) in enumerate(((gs, xs, bs), (gt, xt, bt), (gi, xi, bi)))
+    ]
+
+    def weight(d, out):
+        def one(b, _):
+            ch = pl.ds(pl.multiple_of(b * rows, LANES), rows)
+            total = None
+            for s in range(seqs):
+                part = _dot(normed[s, :, ch], d[s], 0, 0)
+                total = part if total is None else total + part
+            out[pl.ds(b * blocks, blocks)] = total.reshape(
+                blocks, wi.shape[1], d.shape[2]
+            ).astype(BF)
+            return 0
+
+        lax.fori_loop(0, model // rows, one, 0)
+
+    weight(ds, gs)
+    planes[0].begin()
+    weight(dr, gt)
+    planes[1].begin()
+    small.step(0)
+    weight(di, gi)
+    planes[2].begin()
+    small.step(1)
     lines[0][0](1)
-    small.step(0)
+    small.step(2)
+    for line in lines[1:]:
+        line[0](0)
     for p in planes:
         p.send_far()
-    small.step(1)
     lines[0][0](2)
     for p in planes[:2]:
         p.send_near()
-    small.step(2)
-    lines[1][0](1)
-    planes[2].send_near()
     planes[0].final(o_gs)
     planes[1].final(o_gt)
     quarter = xp.shape[1]
@@ -1411,6 +1418,8 @@
         xp[o] = o_gs[o * quarter : (o + 1) * quarter, :].astype(BF)
     state = _LineSum(n, xp, xb, xo2, es, er)
     state.scatter()
+    lines[1][0](1)
+    planes[2].send_near()
     lines[1][0](2)
     state.gather()
     planes[2].final(o_gi)
@@ -1477,9 +1486,9 @@
     o_gg[...] = gg[...]
     o_gi[...] = gi[...]
     o_gs[...] = gs[...]
-    o_gt[...] = gt[:, :heads]
-    short = jnp.zeros((256 - go.shape[0], go.shape[1]), F32)
-    o_go[...] = jnp.concatenate([go[...], short], axis=0).T[:, : go.shape[0]]
+    short = jnp.zeros((256 - gt.shape[0], LANES), F32)
+    o_gt[...] = jnp.concatenate([gt[...], short], axis=0).T[:heads, : gt.shape[0]]
+    o_go[...] = go[...]
     width = sms.shape[2]
     shared = None
     head_rows = None
@@ -1519,10 +1528,10 @@
     width = sms.shape[2]
     outs = (
         jax.ShapeDtypeStruct(tok.shape, BF), sd(*tok.shape), sd(1, tok.shape[2]),
-        sd(*gg.shape), sd(*gi.shape), sd(*gs.shape), sd(gt.shape[0], heads),
+        sd(*gg.shape), sd(*gi.shape), sd(*gs.shape), sd(heads, gt.shape[0]),
         sd(4, n * width), sd(1, n * width), sd(4, 2 * STATE), sd(1, 2 * STATE),
         sd(1, n * heads), sd(1, n * heads), sd(1, n * heads), sd(1, n * width),
-        sd(go.shape[1], go.shape[0]),
+        sd(*go.shape),
     )
     return pl.pallas_call(
         functools.partial(emit_kernel, n, heads),
@@ -1821,10 +1830,9 @@
     tensor_count = lax.axis_size("tensor")
     tensor_rank = lax.axis_index("tensor")
     heads = step_proj.shape[1]
-    step_wide = jnp.pad(step_proj, ((0, 0), (0, 128 - heads)))
     gain_row = input_gain[None]
     normed, seg_old, s8, t8, i8 = gather_all(
-        tensor_count, tokens, gain_row, segments, (state_proj, step_wide, inner_proj)
+        tensor_count, tokens, gain_row, segments, (state_proj, step_proj.T, inner_proj)
     )
     heads_param = jnp.pad(
         lax.dynamic_slice_in_dim(
@@ -1859,7 +1867,9 @@
         shard_gate, shard_inner, shard_state, shard_step, shard_output, sms,
     )
     flat = (2, 8, 10, 11, 12, 13, 14)
-    return tuple(o[0] if i in flat else o for i, o in enumerate(outs))
+    return tuple(
+        o[0] if i in flat else o.T if i in (6, 15) else o for i, o in enumerate(outs)
+    )
 
 
 def solution(mesh):

time: 167 us -> 166 us (level)
  local copies, waits for them, and re-layouts: 6.95 us -> 5.06 us
    unnamed x31 -> x30, local copies, waits for them, and re-layouts: 6.15 us -> 4.28 us
where the time goes in v5:
time: 166 us
  Pallas kernels  159 us (96%)
  local copies, waits for them, and re-layouts  5.06 us (3%)
    pallas_call x4, Pallas kernels, _mixer_call(): pl.pallas_call(kernel, out_shape=outs, in_specs=[pl.BlockSpec(memory_spac...  123 us
    pallas_call x1, Pallas kernels, gather_all(): pl.pallas_call(functools.partial(gather_kernel, n), out_shape=(act, jax.S...  32.8 us
    unnamed x30, local copies, waits for them, and re-layouts  4.28 us

profile of v5, /device:TPU:0, one launch (start us, length us, event | category | flops | bytes accessed | tf_op | source)
XLA Modules:
  0.0 165.9 jit_solution(10682746106363387497)
XLA Ops:
  0.7 0.7 pad_maximum_fusion
  1.3 0.1 constant_dynamic-slice_fusion
  1.4 0.7 broadcast_in_dim.12.gain
  2.1 0.0 copy-start
  2.1 1.0 copy-done
  3.1 1.0 copy-done.3
  4.1 0.9 copy-done.6
  5.0 0.7 copy-done.10
  5.7 0.7 copy-done.12
  6.4 0.0 copy-start.8
  6.4 0.0 copy-start.11
  6.4 0.0 copy-start.13
  6.4 0.0 copy-start.14
  6.4 32.8 %gather_all.1 = (bf16[2,256,1536]{2,1,0:T(8,128)(2,1)S(1)}, s32[2,256]{1,0:T(2,128)S(1)}, bf16[8,192,256]{2,1,0:T(8,128)(2,1)S(1)}, bf16[8,192,128]{2,1,0:T(8,128)(2,1)S(1)}, bf16[8,192,768]{2,1,0:T(8,128)(2,1)S(1)}) custom-call(bf16[2,64,1536]{2,1,0:T(8,128)(2,1)S(1)} %copy-done, f32[1,1536]{1,0:T(1,128)S(1)} %broadcast_in_dim.12.gain, ...), custom_call_target="tpu_custom_call" | custom-call | flops 30000001024 | bytes 1048576 | tf_op jit(solution)/shard_map/gather_all/pallas_call | solution.py:339
  39.2 0.0 copy-done.2
  39.2 0.0 copy-done.4
  39.2 0.0 copy-done.5
  39.3 0.0 copy-done.7
  39.3 0.0 copy-done.8
  39.3 0.0 copy-done.11
  39.3 0.0 copy-done.13
  39.3 0.0 copy-done.14
  39.3 0.0 copy-start.9
  39.3 27.7 %mix_fwd.1 = (f32[2,256,768]{2,1,0:T(8,128)S(1)}, f32[2,256,768]{2,1,0:T(8,128)S(1)}, f32[2,256,256]{2,1,0:T(8,128)S(1)}, f32[2,256,128]{2,1,0:T(8,128)S(1)}, bf...) custom-call(s32[2,256]{1,0:T(2,128)S(1)} %copy-done.13, ...), custom_call_target="tpu_custom_call" | custom-call | flops 30000001024 | bytes 1048576 | tf_op jit(solution)/shard_map/mix_fwd/pallas_call | solution.py:869
  67.0 0.0 copy-done.9
  67.0 14.1 %gate_stage.1 = (f32[2,256,768]{2,1,0:T(8,128)S(1)}, bf16[2,256,768]{2,1,0:T(8,128)(2,1)S(1)}, bf16[2,128,768]{2,1,0:T(8,128)(2,1)S(1)}, bf16[2,256,1536]{2,1,0:...) custom-call(f32[2,256,768]{2,1,0:T(8,128)S(1)} %get-tuple-element.78.y_p, ...), custom_call_target="tpu_custom_call" | custom-call | flops 6000000000 | bytes 1048576 | tf_op jit(solution)/shard_map/gate_stage/pallas_call | solution.py:869
  81.1 39.8 %mix_bwd.1 = (bf16[2,256,768]{2,1,0:T(8,128)(2,1)S(1)}, bf16[2,256,256]{2,1,0:T(8,128)(2,1)S(1)}, bf16[2,256,128]{2,1,0:T(8,128)(2,1)S(1)}, f32[8,768]{1,0:T(8,1...) custom-call(f32[2,256,768]{2,1,0:T(8,128)S(1)} %get-tuple-element.85, ...), custom_call_target="tpu_custom_call" | custom-call | flops 8000000000 | bytes 1048576 | tf_op jit(solution)/shard_map/mix_bwd/pallas_call | solution.py:869
  120.9 0.0 copy-start.1
  120.9 41.4 %reduce_all.1 = (f32[2,64,1536]{2,1,0:T(8,128)S(1)}, f32[192,768]{1,0:T(8,128)S(1)}, f32[192,256]{1,0:T(8,128)S(1)}, f32[192,128]{1,0:T(8,128)S(1)}, f32[4,16,768]{2,1,0:T(8,128)S(1)}) custom-call(bf16[2,256,1536]{2,1,0:T(8,128)(2,1)S(1)} %get-tuple-element.74.normed.tokens_in, bf16[2,256,768]{2,1,0:T(8,128)(2,1)S(1)} %get-tuple-element.98.dg, ...), custom_call_target="tpu_custom_call" | custom-call | flops 6000000000 | bytes 1048576 | tf_op jit(solution)/shard_map/reduce_all/pallas_call | solution.py:869
  162.3 0.0 copy-done.1
  162.3 3.0 %emit_all.1 = (bf16[2,64,1536]{2,1,0:T(8,128)(2,1)}, f32[2,64,1536]{2,1,0:T(8,128)}, f32[1,1536]{1,0:T(1,128)S(1)}, f32[192,768]{1,0:T(8,128)}, f32[192,768]{1,0...) custom-call(bf16[2,64,1536]{2,1,0:T(8,128)(2,1)S(1)} %copy-done.1, ...), custom_call_target="tpu_custom_call" | custom-call | tf_op jit(solution)/shard_map/emit_all/pallas_call | solution.py:1536
  165.3 0.6 reduce
  (9 shorter events, 0.0 us)
Async XLA Ops:
  2.1 1.0 copy-start
  3.1 1.0 copy-start.3
  4.1 0.9 copy-start.6
  5.0 0.7 copy-start.10
  5.7 0.7 copy-start.12
  6.4 32.9 %copy-start.2 = (bf16[2,64,1536]{2,1,0:T(8,128)(2,1)S(1)}, bf16[2,64,1536]{2,1,0:T(8,128)(2,1)}, u32[]{:S(2)}) copy-start(bf16[2,64,1536]{2,1,0:T(8,128)(2,1)} %cot.3) | copy-start | bytes 1179652
  6.4 32.9 %copy-start.4 = (bf16[768,192]{0,1:T(8,128)(2,1)S(1)}, bf16[768,192]{0,1:T(8,128)(2,1)}, u32[]{:S(2)}) copy-start(bf16[768,192]{0,1:T(8,128)(2,1)} %param.32) | copy-start | bytes 884740
  6.4 32.9 %copy-start.5 = (bf16[192,768]{1,0:T(8,128)(2,1)S(1)}, bf16[192,768]{1,0:T(8,128)(2,1)}, u32[]{:S(2)}) copy-start(bf16[192,768]{1,0:T(8,128)(2,1)} %wg.1) | copy-start | bytes 884740
  6.4 32.9 %copy-start.7 = (f32[4,3072]{1,0:T(4,128)S(1)}, f32[4,3072]{1,0:T(4,128)}, u32[]{:S(2)}) copy-start(f32[4,3072]{1,0:T(4,128)} %taps_i.3) | copy-start | bytes 147460
  6.4 32.9 %copy-start.8 = (f32[3072]{0:T(1024)S(1)}, f32[3072]{0:T(1024)}, u32[]{:S(2)}) copy-start(f32[3072]{0:T(1024)} %param.25) | copy-start | bytes 36868
  6.4 32.9 %copy-start.11 = (f32[4,256]{1,0:T(4,128)S(1)}, f32[4,256]{1,0:T(4,128)}, u32[]{:S(2)}) copy-start(f32[4,256]{1,0:T(4,128)} %taps_s.3) | copy-start | bytes 12292
  6.4 32.9 %copy-start.13 = (s32[2,256]{1,0:T(2,128)S(1)}, s32[2,256]{1,0:T(2,128)}, u32[]{:S(2)}) copy-start(s32[2,256]{1,0:T(2,128)} %seg.3) | copy-start | bytes 6148
  6.4 32.9 %copy-start.14 = (f32[256]{0:T(256)S(1)}, f32[256]{0:T(256)}, u32[]{:S(2)}) copy-start(f32[256]{0:T(256)} %param.27) | copy-start | bytes 3076
  39.3 27.7 %copy-start.9 = (f32[3072]{0:T(1024)S(1)}, f32[3072]{0:T(1024)}, u32[]{:S(2)}) copy-start(f32[3072]{0:T(1024)} %param.31) | copy-start | bytes 36868
  120.9 41.4 %copy-start.1 = (bf16[2,64,1536]{2,1,0:T(8,128)(2,1)S(1)}, bf16[2,64,1536]{2,1,0:T(8,128)(2,1)}, u32[]{:S(2)}) copy-start(bf16[2,64,1536]{2,1,0:T(8,128)(2,1)} %tok.1) | copy-start | bytes 1179652

commit v6 on v5

--- a/solution.py
+++ b/solution.py
@@ -376,23 +376,22 @@
     def block(o):
         return part.at[:, pl.ds(pl.multiple_of(o * rows, rows), rows), :]
 
+    def begin(j):
+        for way, box, place, o in ((1, left, t, n - 1 - j), (-1, right, n - 1 - t, j)):
+            @pl.when(place == 0)
+            def _():
+                copy(block(o), box, o, way).start()
+
     def step(k):
         for way, box, place in ((1, left, t), (-1, right, n - 1 - t)):
-            target = lambda j: n - 1 - j if way > 0 else j
-            if k == 0:
-                @pl.when(place == 0)
-                def _():
-                    for j in range(n - 1):
-                        copy(block(target(j)), box, target(j), way).start()
-            else:
-                @pl.when(jnp.logical_and(place > 0, place <= k))
-                def _():
-                    o = target(k - place)
-                    copy(block(o), box, o, way).wait_recv()
-                    for s in range(part.shape[0]):
-                        own = part[s, pl.ds(pl.multiple_of(o * rows, rows), rows), :].astype(F32)
-                        box[o, s] = (box[o, s].astype(F32) + own).astype(BF)
-                    copy(box.at[o], box, o, way).start()
+            @pl.when(jnp.logical_and(place > 0, place <= k))
+            def _():
+                o = n - 1 - (k - place) if way > 0 else k - place
+                copy(block(o), box, o, way).wait_recv()
+                for s in range(part.shape[0]):
+                    own = part[s, pl.ds(pl.multiple_of(o * rows, rows), rows), :].astype(F32)
+                    box[o, s] = (box[o, s].astype(F32) + own).astype(BF)
+                copy(box.at[o], box, o, way).start()
 
     def final(out):
         mine = pl.ds(pl.multiple_of(t * rows, rows), rows)
@@ -420,7 +419,7 @@
                 def _():
                     copy(box.at[o], box, o, way).wait_send()
 
-    return step, final, finish
+    return begin, step, final, finish
 
 
 def _line_reduces(n, part, left, right, ssem, rsem):
@@ -1111,8 +1110,9 @@
     planes = (
         _PlaneReduce(go, xo, bo, ps.at[0], pr.at[0]), _PlaneReduce(gg, xg, bg, ps.at[1], pr.at[1])
     )
-    for step, _, _ in lines:
-        step(0)
+    for j in range(n - 1):
+        for begin, _, _, _ in lines:
+            begin(j)
     for plane in planes:
         plane.begin()
     sm_i[...] = jnp.zeros_like(sm_i)
@@ -1155,25 +1155,29 @@
         def pair(p, _):
             @pl.when(jnp.logical_and(s == 0, p == 3))
             def _():
-                lines[0][0](1)
-
-            @pl.when(jnp.logical_and(s == 0, p == 4))
+                lines[0][1](1)
+
+            @pl.when(jnp.logical_and(s == 0, p == 5))
             def _():
                 for plane in planes:
                     plane.send_far()
 
             @pl.when(jnp.logical_and(s == 1, p == 0))
             def _():
-                lines[0][0](2)
+                lines[1][1](1)
+
+            @pl.when(jnp.logical_and(s == 1, p == 2))
+            def _():
+                lines[0][1](2)
 
             @pl.when(jnp.logical_and(s == 1, p == 3))
             def _():
-                for plane in planes:
-                    plane.send_near()
-
-            @pl.when(jnp.logical_and(s == 1, p == 4))
+                planes[0].send_near()
+
+            @pl.when(jnp.logical_and(s == 1, p == 5))
             def _():
-                lines[1][0](1)
+                lines[1][1](2)
+                planes[1].send_near()
 
             ch = pl.ds(pl.multiple_of(p * LANES, LANES), LANES)
             at = pl.ds(pl.multiple_of(t * width + p * LANES, LANES), LANES)
@@ -1244,7 +1248,6 @@
         return 0
 
     lax.fori_loop(0, seqs, one, 0)
-    lines[1][0](2)
     dp, seq = lax.axis_index("dp"), lax.axis_index("seq")
     handed = [
         pltpu.make_async_remote_copy(
@@ -1275,11 +1278,11 @@
             c.wait_send()
 
     planes[1].final(o_gg)
-    for s, (_, final, _) in enumerate(lines):
+    for s, (_, _, final, _) in enumerate(lines):
         final(o_po.at[pl.ds(s, 1)])
     for plane in planes:
         plane.finish()
-    for _, _, finish in lines:
+    for _, _, _, finish in lines:
         finish()
 
 
@@ -1369,12 +1372,14 @@
             pg[s, :, ch] = part.astype(BF)
             part = jnp.sum(part * normed[s, :, ch].astype(F32), axis=0, keepdims=True)
             totals[b] = part if totals[b] is None else totals[b] + part
-        if s == 0:
-            lines[s][0](0)
+        lines[s][0](0)
     for b, total in enumerate(totals):
         ch = slice(b * rows, (b + 1) * rows)
         mb[0, 7 + b // 2 : 8 + b // 2, (b % 2) * rows : (b % 2 + 1) * rows] = total / gain[:, ch]
     small.copy(0, small.near(0)).start()
+    for j in range(1, n - 2):
+        for line in lines:
+            line[0](j)
     planes = [
         _PlaneReduce(part, pair, box, ps.at[i], pr.at[i])
         for i, (part, pair, box) in enumerate(((gs, xs, bs), (gt, xt, bt), (gi, xi, bi)))
@@ -1401,14 +1406,15 @@
     small.step(0)
     weight(di, gi)
     planes[2].begin()
+    lines[0][1](1)
     small.step(1)
-    lines[0][0](1)
     small.step(2)
-    for line in lines[1:]:
-        line[0](0)
+    for line in lines:
+        line[0](n - 2)
+    lines[1][1](1)
     for p in planes:
         p.send_far()
-    lines[0][0](2)
+    lines[0][1](2)
     for p in planes[:2]:
         p.send_near()
     planes[0].final(o_gs)
@@ -1418,13 +1424,12 @@
         xp[o] = o_gs[o * quarter : (o + 1) * quarter, :].astype(BF)
     state = _LineSum(n, xp, xb, xo2, es, er)
     state.scatter()
-    lines[1][0](1)
     planes[2].send_near()
-    lines[1][0](2)
+    lines[1][1](2)
     state.gather()
     planes[2].final(o_gi)
     small.final()
-    for s, (_, final, _) in enumerate(lines):
+    for s, (_, _, final, _) in enumerate(lines):
         final(o_pg.at[pl.ds(s, 1)])
     state.arrive()
     for o in range(n):
@@ -1433,7 +1438,7 @@
         p.finish()
     state.finish()
     small.finish()
-    for _, _, finish in lines:
+    for _, _, _, finish in lines:
         finish()
 
 

time: 166 us -> 161 us (0.970)
  Pallas kernels: 159 us -> 154 us
    pallas_call x4, Pallas kernels: 123 us -> 118 us  [_mixer_call(): pl.pallas_call(kernel, out_shape=outs, in_specs=[pl.BlockSpec(memory_spac...]
where the time goes in v6:
time: 161 us
  Pallas kernels  154 us (96%)
  local copies, waits for them, and re-layouts  5.06 us (3%)
    pallas_call x4, Pallas kernels, _mixer_call(): pl.pallas_call(kernel, out_shape=outs, in_specs=[pl.BlockSpec(memory_spac...  118 us
    pallas_call x1, Pallas kernels, gather_all(): pl.pallas_call(functools.partial(gather_kernel, n), out_shape=(act, jax.S...  32.8 us
    unnamed x30, local copies, waits for them, and re-layouts  4.28 us

profile of v6, /device:TPU:0, one launch (start us, length us, event | category | flops | bytes accessed | tf_op | source)
XLA Modules:
  0.0 161.2 jit_solution(759236701465210228)
XLA Ops:
  0.7 0.7 pad_maximum_fusion
  1.3 0.1 constant_dynamic-slice_fusion
  1.4 0.7 broadcast_in_dim.12.gain
  2.1 0.0 copy-start
  2.1 1.0 copy-done
  3.1 1.0 copy-done.3
  4.1 0.9 copy-done.6
  5.0 0.7 copy-done.10
  5.7 0.7 copy-done.12
  6.4 0.0 copy-start.8
  6.4 0.0 copy-start.11
  6.4 0.0 copy-start.13
  6.4 0.0 copy-start.14
  6.4 32.8 %gather_all.1 = (bf16[2,256,1536]{2,1,0:T(8,128)(2,1)S(1)}, s32[2,256]{1,0:T(2,128)S(1)}, bf16[8,192,256]{2,1,0:T(8,128)(2,1)S(1)}, bf16[8,192,128]{2,1,0:T(8,128)(2,1)S(1)}, bf16[8,192,768]{2,1,0:T(8,128)(2,1)S(1)}) custom-call(bf16[2,64,1536]{2,1,0:T(8,128)(2,1)S(1)} %copy-done, f32[1,1536]{1,0:T(1,128)S(1)} %broadcast_in_dim.12.gain, ...), custom_call_target="tpu_custom_call" | custom-call | flops 30000001024 | bytes 1048576 | tf_op jit(solution)/shard_map/gather_all/pallas_call | solution.py:339
  39.2 0.0 copy-done.2
  39.2 0.0 copy-done.4
  39.2 0.0 copy-done.5
  39.3 0.0 copy-done.7
  39.3 0.0 copy-done.8
  39.3 0.0 copy-done.11
  39.3 0.0 copy-done.13
  39.3 0.0 copy-done.14
  39.3 0.0 copy-start.9
  39.3 27.7 %mix_fwd.1 = (f32[2,256,768]{2,1,0:T(8,128)S(1)}, f32[2,256,768]{2,1,0:T(8,128)S(1)}, f32[2,256,256]{2,1,0:T(8,128)S(1)}, f32[2,256,128]{2,1,0:T(8,128)S(1)}, bf...) custom-call(s32[2,256]{1,0:T(2,128)S(1)} %copy-done.13, ...), custom_call_target="tpu_custom_call" | custom-call | flops 30000001024 | bytes 1048576 | tf_op jit(solution)/shard_map/mix_fwd/pallas_call | solution.py:868
  67.0 0.0 copy-done.9
  67.0 14.1 %gate_stage.1 = (f32[2,256,768]{2,1,0:T(8,128)S(1)}, bf16[2,256,768]{2,1,0:T(8,128)(2,1)S(1)}, bf16[2,128,768]{2,1,0:T(8,128)(2,1)S(1)}, bf16[2,256,1536]{2,1,0:...) custom-call(f32[2,256,768]{2,1,0:T(8,128)S(1)} %get-tuple-element.78.y_p, ...), custom_call_target="tpu_custom_call" | custom-call | flops 6000000000 | bytes 1048576 | tf_op jit(solution)/shard_map/gate_stage/pallas_call | solution.py:868
  81.1 33.4 %mix_bwd.1 = (bf16[2,256,768]{2,1,0:T(8,128)(2,1)S(1)}, bf16[2,256,256]{2,1,0:T(8,128)(2,1)S(1)}, bf16[2,256,128]{2,1,0:T(8,128)(2,1)S(1)}, f32[8,768]{1,0:T(8,1...) custom-call(f32[2,256,768]{2,1,0:T(8,128)S(1)} %get-tuple-element.85, ...), custom_call_target="tpu_custom_call" | custom-call | flops 8000000000 | bytes 1048576 | tf_op jit(solution)/shard_map/mix_bwd/pallas_call | solution.py:868
  114.5 0.0 copy-start.1
  114.5 43.0 %reduce_all.1 = (f32[2,64,1536]{2,1,0:T(8,128)S(1)}, f32[192,768]{1,0:T(8,128)S(1)}, f32[192,256]{1,0:T(8,128)S(1)}, f32[192,128]{1,0:T(8,128)S(1)}, f32[4,16,768]{2,1,0:T(8,128)S(1)}) custom-call(bf16[2,256,1536]{2,1,0:T(8,128)(2,1)S(1)} %get-tuple-element.74.normed.tokens_in, bf16[2,256,768]{2,1,0:T(8,128)(2,1)S(1)} %get-tuple-element.98.dg, ...), custom_call_target="tpu_custom_call" | custom-call | flops 6000000000 | bytes 1048576 | tf_op jit(solution)/shard_map/reduce_all/pallas_call | solution.py:868
  157.5 0.0 copy-done.1
  157.5 3.0 %emit_all.1 = (bf16[2,64,1536]{2,1,0:T(8,128)(2,1)}, f32[2,64,1536]{2,1,0:T(8,128)}, f32[1,1536]{1,0:T(1,128)S(1)}, f32[192,768]{1,0:T(8,128)}, f32[192,768]{1,0...) custom-call(bf16[2,64,1536]{2,1,0:T(8,128)(2,1)S(1)} %copy-done.1, ...), custom_call_target="tpu_custom_call" | custom-call | tf_op jit(solution)/shard_map/emit_all/pallas_call | solution.py:1541
  160.5 0.6 reduce
  (9 shorter events, 0.0 us)
Async XLA Ops:
  2.1 1.0 copy-start
  3.1 1.0 copy-start.3
  4.1 0.9 copy-start.6
  5.0 0.7 copy-start.10
  5.7 0.7 copy-start.12
  6.4 32.9 %copy-start.2 = (bf16[2,64,1536]{2,1,0:T(8,128)(2,1)S(1)}, bf16[2,64,1536]{2,1,0:T(8,128)(2,1)}, u32[]{:S(2)}) copy-start(bf16[2,64,1536]{2,1,0:T(8,128)(2,1)} %cot.3) | copy-start | bytes 1179652
  6.4 32.9 %copy-start.4 = (bf16[768,192]{0,1:T(8,128)(2,1)S(1)}, bf16[768,192]{0,1:T(8,128)(2,1)}, u32[]{:S(2)}) copy-start(bf16[768,192]{0,1:T(8,128)(2,1)} %param.32) | copy-start | bytes 884740
  6.4 32.9 %copy-start.5 = (bf16[192,768]{1,0:T(8,128)(2,1)S(1)}, bf16[192,768]{1,0:T(8,128)(2,1)}, u32[]{:S(2)}) copy-start(bf16[192,768]{1,0:T(8,128)(2,1)} %wg.1) | copy-start | bytes 884740
  6.4 32.9 %copy-start.7 = (f32[4,3072]{1,0:T(4,128)S(1)}, f32[4,3072]{1,0:T(4,128)}, u32[]{:S(2)}) copy-start(f32[4,3072]{1,0:T(4,128)} %taps_i.3) | copy-start | bytes 147460
  6.4 32.9 %copy-start.8 = (f32[3072]{0:T(1024)S(1)}, f32[3072]{0:T(1024)}, u32[]{:S(2)}) copy-start(f32[3072]{0:T(1024)} %param.25) | copy-start | bytes 36868
  6.4 32.9 %copy-start.11 = (f32[4,256]{1,0:T(4,128)S(1)}, f32[4,256]{1,0:T(4,128)}, u32[]{:S(2)}) copy-start(f32[4,256]{1,0:T(4,128)} %taps_s.3) | copy-start | bytes 12292
  6.4 32.9 %copy-start.13 = (s32[2,256]{1,0:T(2,128)S(1)}, s32[2,256]{1,0:T(2,128)}, u32[]{:S(2)}) copy-start(s32[2,256]{1,0:T(2,128)} %seg.3) | copy-start | bytes 6148
  6.4 32.9 %copy-start.14 = (f32[256]{0:T(256)S(1)}, f32[256]{0:T(256)}, u32[]{:S(2)}) copy-start(f32[256]{0:T(256)} %param.27) | copy-start | bytes 3076
  39.3 27.7 %copy-start.9 = (f32[3072]{0:T(1024)S(1)}, f32[3072]{0:T(1024)}, u32[]{:S(2)}) copy-start(f32[3072]{0:T(1024)} %param.31) | copy-start | bytes 36868
  114.5 43.1 %copy-start.1 = (bf16[2,64,1536]{2,1,0:T(8,128)(2,1)S(1)}, bf16[2,64,1536]{2,1,0:T(8,128)(2,1)}, u32[]{:S(2)}) copy-start(bf16[2,64,1536]{2,1,0:T(8,128)(2,1)} %tok.1) | copy-start | bytes 1179652

commit v7 on v6

--- a/solution.py
+++ b/solution.py
@@ -531,7 +531,7 @@
             self.copy(j + 1, self.near(j + 1)).start()
         else:
             t = lax.axis_index("tensor")
-            self.line[t] = total
+            self.line[t] = total.astype(self.line.dtype)
             for o in range(self.n):
                 @pl.when(t != o)
                 def _(o=o):
@@ -1199,6 +1199,8 @@
             d_c[...] += _dot(ed.astype(BF), h_in, 1, 1)
             late = qx * b_l
             dxd = q * b_l
+            sum_r = _dot(_split(ed * c_h - late, 2), fold)
+            sum_s = sum_c = None
             lane = lax.div(_iota(xb.shape, 1), HEAD_DIM)
             for a in range(2):
                 h = 2 * p + a
@@ -1206,15 +1208,18 @@
                 decay = jnp.exp(_dot(run3[...], pick) - run_t[pl.ds(h, 1), :] + bias_m[...])
                 da = jnp.where(lane == a, db, jnp.zeros_like(db))
                 ld = decay * _dot(da, xb, 1, 1)
-                d_scores[...] += ld
+                sum_s = ld if a == 0 else sum_s + ld
                 both = (ld * scores[...]).astype(BF)
                 mixing = (decay * scores[...]).astype(BF)
                 dxd = dxd + _dot(mixing, da, 0, 0)
                 col = (_iota((length, LANES), 1) == h).astype(F32).astype(BF)
                 row = (_iota((LANES, length), 0) == h).astype(F32).astype(BF)
-                acc_r[...] += _dot(both, col)
-                acc_c[...] += _dot(row, both)
-            acc_r[...] += _dot(_split(ed * c_h - late, 2), fold)
+                sum_r = sum_r + _dot(both, col)
+                part = _dot(row, both)
+                sum_c = part if a == 0 else sum_c + part
+            d_scores[...] += sum_s
+            acc_r[...] += sum_r
+            acc_c[...] += sum_c
             acc_d[...] += _dot(_split(dxd * x, 2), fold)
             total = jnp.broadcast_to(jnp.sum(late, axis=0, keepdims=True), (8, LANES))
             acc_q[...] += _dot(_split(total, 2), fold)
@@ -1408,10 +1413,10 @@
     planes[2].begin()
     lines[0][1](1)
     small.step(1)
+    lines[1][1](1)
     small.step(2)
     for line in lines:
         line[0](n - 2)
-    lines[1][1](1)
     for p in planes:
         p.send_far()
     lines[0][1](2)
@@ -1454,7 +1459,7 @@
         (normed, dg, di, ds, dr, wg, wi, ws, wt, gain, sm_i, sm_s, sm_h, g_gain),
         (sd((seqs, rows, model), F32),)
         + tuple(sd(w.shape[1:], F32) for w in (wi, ws, wt))
-        + (sd((n,) + sums, F32),),
+        + (sd((n,) + sums, BF),),
         [pltpu.VMEM((seqs, length, model), BF)]
         + [pltpu.VMEM(w.shape, BF) for w in (wi, ws, wt)]
         + [box, box]
@@ -1499,15 +1504,16 @@
     head_rows = None
     for t in range(n):
         ch = slice(t * width, (t + 1) * width)
-        o_ci[:, ch] = sms[t, 0:4, :]
-        o_ib[:, ch] = sms[t, 4:5, :]
-        o_gain[:, ch] = sms[t, 6:7, :]
-        block = sms[t, 8:16, :]
-        shared = sms[t, 7:11, :] if shared is None else shared + sms[t, 7:11, :]
+        every = sms[t].astype(F32)
+        o_ci[:, ch] = every[0:4, :]
+        o_ib[:, ch] = every[4:5, :]
+        o_gain[:, ch] = every[6:7, :]
+        block = every[8:16, :]
+        shared = every[7:11, :] if shared is None else shared + every[7:11, :]
         lanes = _iota((3 * width, LANES), 0)
         chan = lax.rem(lanes, width)
         to = _iota((3 * width, LANES), 1) == heads * t + lax.div(chan, HEAD_DIM)
-        skips = _dot(_split(sms[t, 0:8, :], 3), to.astype(F32).astype(BF))
+        skips = _dot(_split(every[0:8, :], 3), to.astype(F32).astype(BF))
         lanes = lax.rem(_iota((3 * LANES, LANES), 0), LANES)
         to = (_iota((3 * LANES, LANES), 1) == heads * t + lanes) & (lanes < heads)
         to = to.astype(F32).astype(BF)
@@ -1515,10 +1521,10 @@
         rate = _dot(_split(block[:, 640:768], 3), to)
         new = (skips[5:6, :], shift[2:3, :], rate[2:3, :])
         head_rows = new if head_rows is None else tuple(a + b for a, b in zip(head_rows, new))
-    every = n * heads
-    o_skip[...] = head_rows[0][:, :every]
-    o_shift[...] = head_rows[1][:, :every]
-    o_rate[...] = head_rows[2][:, :every]
+    count = n * heads
+    o_skip[...] = head_rows[0][:, :count]
+    o_shift[...] = head_rows[1][:, :count]
+    o_rate[...] = head_rows[2][:, :count]
     g_in[:, :width] = shared[0:1, :]
     g_in[:, width:] = shared[1:2, :]
     for k in range(4):

time: 161 us -> 159 us (0.988)
  Pallas kernels: 154 us -> 152 us
    pallas_call x4, Pallas kernels: 118 us -> 116 us  [_mixer_call(): pl.pallas_call(kernel, out_shape=outs, in_specs=[pl.BlockSpec(memory_spac...]
where the time goes in v7:
time: 159 us
  Pallas kernels  152 us (96%)
  local copies, waits for them, and re-layouts  5.06 us (3%)
    pallas_call x4, Pallas kernels, _mixer_call(): pl.pallas_call(kernel, out_shape=outs, in_specs=[pl.BlockSpec(memory_spac...  116 us
    pallas_call x1, Pallas kernels, gather_all(): pl.pallas_call(functools.partial(gather_kernel, n), out_shape=(act, jax.S...  32.8 us
    unnamed x30, local copies, waits for them, and re-layouts  4.28 us

profile of v7, /device:TPU:0, one launch (start us, length us, event | category | flops | bytes accessed | tf_op | source)
XLA Modules:
  0.0 158.7 jit_solution(23437069223563110)
XLA Ops:
  0.7 0.7 pad_maximum_fusion
  1.3 0.1 constant_dynamic-slice_fusion
  1.4 0.7 broadcast_in_dim.12.gain
  2.1 0.0 copy-start
  2.1 1.0 copy-done
  3.1 1.0 copy-done.3
  4.1 0.9 copy-done.6
  5.0 0.7 copy-done.10
  5.7 0.7 copy-done.12
  6.4 0.0 copy-start.8
  6.4 0.0 copy-start.11
  6.4 0.0 copy-start.13
  6.4 0.0 copy-start.14
  6.4 32.8 %gather_all.1 = (bf16[2,256,1536]{2,1,0:T(8,128)(2,1)S(1)}, s32[2,256]{1,0:T(2,128)S(1)}, bf16[8,192,256]{2,1,0:T(8,128)(2,1)S(1)}, bf16[8,192,128]{2,1,0:T(8,128)(2,1)S(1)}, bf16[8,192,768]{2,1,0:T(8,128)(2,1)S(1)}) custom-call(bf16[2,64,1536]{2,1,0:T(8,128)(2,1)S(1)} %copy-done, f32[1,1536]{1,0:T(1,128)S(1)} %broadcast_in_dim.12.gain, ...), custom_call_target="tpu_custom_call" | custom-call | flops 30000001024 | bytes 1048576 | tf_op jit(solution)/shard_map/gather_all/pallas_call | solution.py:339
  39.2 0.0 copy-done.2
  39.2 0.0 copy-done.4
  39.2 0.0 copy-done.5
  39.3 0.0 copy-done.7
  39.3 0.0 copy-done.8
  39.3 0.0 copy-done.11
  39.3 0.0 copy-done.13
  39.3 0.0 copy-done.14
  39.3 0.0 copy-start.9
  39.3 27.7 %mix_fwd.1 = (f32[2,256,768]{2,1,0:T(8,128)S(1)}, f32[2,256,768]{2,1,0:T(8,128)S(1)}, f32[2,256,256]{2,1,0:T(8,128)S(1)}, f32[2,256,128]{2,1,0:T(8,128)S(1)}, bf...) custom-call(s32[2,256]{1,0:T(2,128)S(1)} %copy-done.13, ...), custom_call_target="tpu_custom_call" | custom-call | flops 30000001024 | bytes 1048576 | tf_op jit(solution)/shard_map/mix_fwd/pallas_call | solution.py:868
  67.0 0.0 copy-done.9
  67.0 14.1 %gate_stage.1 = (f32[2,256,768]{2,1,0:T(8,128)S(1)}, bf16[2,256,768]{2,1,0:T(8,128)(2,1)S(1)}, bf16[2,128,768]{2,1,0:T(8,128)(2,1)S(1)}, bf16[2,256,1536]{2,1,0:...) custom-call(f32[2,256,768]{2,1,0:T(8,128)S(1)} %get-tuple-element.78.y_p, ...), custom_call_target="tpu_custom_call" | custom-call | flops 6000000000 | bytes 1048576 | tf_op jit(solution)/shard_map/gate_stage/pallas_call | solution.py:868
  81.1 33.3 %mix_bwd.1 = (bf16[2,256,768]{2,1,0:T(8,128)(2,1)S(1)}, bf16[2,256,256]{2,1,0:T(8,128)(2,1)S(1)}, bf16[2,256,128]{2,1,0:T(8,128)(2,1)S(1)}, f32[8,768]{1,0:T(8,1...) custom-call(f32[2,256,768]{2,1,0:T(8,128)S(1)} %get-tuple-element.85, ...), custom_call_target="tpu_custom_call" | custom-call | flops 8000000000 | bytes 1048576 | tf_op jit(solution)/shard_map/mix_bwd/pallas_call | solution.py:868
  114.4 0.0 copy-start.1
  114.4 40.8 %reduce_all.1 = (f32[2,64,1536]{2,1,0:T(8,128)S(1)}, f32[192,768]{1,0:T(8,128)S(1)}, f32[192,256]{1,0:T(8,128)S(1)}, f32[192,128]{1,0:T(8,128)S(1)}, bf16[4,16,768]{2,1,0:T(8,128)(2,1)S(1)}) custom-call(bf16[2,256,1536]{2,1,0:T(8,128)(2,1)S(1)} %get-tuple-element.74.normed.tokens_in, bf16[2,256,768]{2,1,0:T(8,128)(2,1)S(1)} %get-tuple-element.98.dg, ...), custom_call_target="tpu_custom_call" | custom-call | flops 6000000000 | bytes 1048576 | tf_op jit(solution)/shard_map/reduce_all/pallas_call | solution.py:868
  155.2 0.0 copy-done.1
  155.2 3.0 %emit_all.1 = (bf16[2,64,1536]{2,1,0:T(8,128)(2,1)}, f32[2,64,1536]{2,1,0:T(8,128)}, f32[1,1536]{1,0:T(1,128)S(1)}, f32[192,768]{1,0:T(8,128)}, f32[192,768]{1,0...) custom-call(bf16[2,64,1536]{2,1,0:T(8,128)(2,1)S(1)} %copy-done.1, ...), custom_call_target="tpu_custom_call" | custom-call | tf_op jit(solution)/shard_map/emit_all/pallas_call | solution.py:1547
  158.1 0.6 reduce
  (9 shorter events, 0.0 us)
Async XLA Ops:
  2.1 1.0 copy-start
  3.1 1.0 copy-start.3
  4.1 0.9 copy-start.6
  5.0 0.7 copy-start.10
  5.7 0.7 copy-start.12
  6.4 32.9 %copy-start.2 = (bf16[2,64,1536]{2,1,0:T(8,128)(2,1)S(1)}, bf16[2,64,1536]{2,1,0:T(8,128)(2,1)}, u32[]{:S(2)}) copy-start(bf16[2,64,1536]{2,1,0:T(8,128)(2,1)} %cot.3) | copy-start | bytes 1179652
  6.4 32.9 %copy-start.4 = (bf16[768,192]{0,1:T(8,128)(2,1)S(1)}, bf16[768,192]{0,1:T(8,128)(2,1)}, u32[]{:S(2)}) copy-start(bf16[768,192]{0,1:T(8,128)(2,1)} %param.32) | copy-start | bytes 884740
  6.4 32.9 %copy-start.5 = (bf16[192,768]{1,0:T(8,128)(2,1)S(1)}, bf16[192,768]{1,0:T(8,128)(2,1)}, u32[]{:S(2)}) copy-start(bf16[192,768]{1,0:T(8,128)(2,1)} %wg.1) | copy-start | bytes 884740
  6.4 32.9 %copy-start.7 = (f32[4,3072]{1,0:T(4,128)S(1)}, f32[4,3072]{1,0:T(4,128)}, u32[]{:S(2)}) copy-start(f32[4,3072]{1,0:T(4,128)} %taps_i.3) | copy-start | bytes 147460
  6.4 32.9 %copy-start.8 = (f32[3072]{0:T(1024)S(1)}, f32[3072]{0:T(1024)}, u32[]{:S(2)}) copy-start(f32[3072]{0:T(1024)} %param.25) | copy-start | bytes 36868
  6.4 32.9 %copy-start.11 = (f32[4,256]{1,0:T(4,128)S(1)}, f32[4,256]{1,0:T(4,128)}, u32[]{:S(2)}) copy-start(f32[4,256]{1,0:T(4,128)} %taps_s.3) | copy-start | bytes 12292
  6.4 32.9 %copy-start.13 = (s32[2,256]{1,0:T(2,128)S(1)}, s32[2,256]{1,0:T(2,128)}, u32[]{:S(2)}) copy-start(s32[2,256]{1,0:T(2,128)} %seg.3) | copy-start | bytes 6148
  6.4 32.9 %copy-start.14 = (f32[256]{0:T(256)S(1)}, f32[256]{0:T(256)}, u32[]{:S(2)}) copy-start(f32[256]{0:T(256)} %param.27) | copy-start | bytes 3076
  39.3 27.7 %copy-start.9 = (f32[3072]{0:T(1024)S(1)}, f32[3072]{0:T(1024)}, u32[]{:S(2)}) copy-start(f32[3072]{0:T(1024)} %param.31) | copy-start | bytes 36868
  114.4 40.8 %copy-start.1 = (bf16[2,64,1536]{2,1,0:T(8,128)(2,1)S(1)}, bf16[2,64,1536]{2,1,0:T(8,128)(2,1)}, u32[]{:S(2)}) copy-start(bf16[2,64,1536]{2,1,0:T(8,128)(2,1)} %tok.1) | copy-start | bytes 1179652

commit v8 on v7

--- a/solution.py
+++ b/solution.py
@@ -531,7 +531,10 @@
             self.copy(j + 1, self.near(j + 1)).start()
         else:
             t = lax.axis_index("tensor")
-            self.line[t] = total.astype(self.line.dtype)
+            high = total.astype(BF).astype(F32)
+            row = _iota(total.shape, 0)
+            rest = pltpu.roll(total - high, 4, 0)
+            self.line[t] = jnp.where((row > 10) & (row < 15), rest, high).astype(BF)
             for o in range(self.n):
                 @pl.when(t != o)
                 def _(o=o):
@@ -1508,8 +1511,9 @@
         o_ci[:, ch] = every[0:4, :]
         o_ib[:, ch] = every[4:5, :]
         o_gain[:, ch] = every[6:7, :]
-        block = every[8:16, :]
-        shared = every[7:11, :] if shared is None else shared + every[7:11, :]
+        whole = every[7:11, :] + every[11:15, :]
+        block = jnp.concatenate([whole, whole], axis=0)
+        shared = whole if shared is None else shared + whole
         lanes = _iota((3 * width, LANES), 0)
         chan = lax.rem(lanes, width)
         to = _iota((3 * width, LANES), 1) == heads * t + lax.div(chan, HEAD_DIM)
@@ -1519,7 +1523,7 @@
         to = to.astype(F32).astype(BF)
         shift = _dot(_split(block[:, 512:640], 3), to)
         rate = _dot(_split(block[:, 640:768], 3), to)
-        new = (skips[5:6, :], shift[2:3, :], rate[2:3, :])
+        new = (skips[5:6, :], shift[3:4, :], rate[3:4, :])
         head_rows = new if head_rows is None else tuple(a + b for a, b in zip(head_rows, new))
     count = n * heads
     o_skip[...] = head_rows[0][:, :count]

time: 159 us -> 159 us (level)
  no operation moved by 1% of the time
where the time goes in v8:
time: 159 us
  Pallas kernels  152 us (96%)
  local copies, waits for them, and re-layouts  5.06 us (3%)
    pallas_call x4, Pallas kernels, _mixer_call(): pl.pallas_call(kernel, out_shape=outs, in_specs=[pl.BlockSpec(memory_spac...  116 us
    pallas_call x1, Pallas kernels, gather_all(): pl.pallas_call(functools.partial(gather_kernel, n), out_shape=(act, jax.S...  32.8 us
    unnamed x30, local copies, waits for them, and re-layouts  4.28 us

profile of v8, /device:TPU:0, one launch (start us, length us, event | category | flops | bytes accessed | tf_op | source)
XLA Modules:
  0.0 158.8 jit_solution(9185994530889298246)
XLA Ops:
  0.7 0.7 pad_maximum_fusion
  1.3 0.1 constant_dynamic-slice_fusion
  1.4 0.7 broadcast_in_dim.12.gain
  2.1 0.0 copy-start
  2.1 1.0 copy-done
  3.1 1.0 copy-done.3
  4.1 0.9 copy-done.6
  5.0 0.7 copy-done.10
  5.7 0.7 copy-done.12
  6.4 0.0 copy-start.8
  6.4 0.0 copy-start.11
  6.4 0.0 copy-start.13
  6.4 0.0 copy-start.14
  6.4 32.8 %gather_all.1 = (bf16[2,256,1536]{2,1,0:T(8,128)(2,1)S(1)}, s32[2,256]{1,0:T(2,128)S(1)}, bf16[8,192,256]{2,1,0:T(8,128)(2,1)S(1)}, bf16[8,192,128]{2,1,0:T(8,128)(2,1)S(1)}, bf16[8,192,768]{2,1,0:T(8,128)(2,1)S(1)}) custom-call(bf16[2,64,1536]{2,1,0:T(8,128)(2,1)S(1)} %copy-done, f32[1,1536]{1,0:T(1,128)S(1)} %broadcast_in_dim.12.gain, ...), custom_call_target="tpu_custom_call" | custom-call | flops 30000001024 | bytes 1048576 | tf_op jit(solution)/shard_map/gather_all/pallas_call | solution.py:339
  39.2 0.0 copy-done.2
  39.2 0.0 copy-done.4
  39.2 0.0 copy-done.5
  39.3 0.0 copy-done.7
  39.3 0.0 copy-done.8
  39.3 0.0 copy-done.11
  39.3 0.0 copy-done.13
  39.3 0.0 copy-done.14
  39.3 0.0 copy-start.9
  39.3 27.7 %mix_fwd.1 = (f32[2,256,768]{2,1,0:T(8,128)S(1)}, f32[2,256,768]{2,1,0:T(8,128)S(1)}, f32[2,256,256]{2,1,0:T(8,128)S(1)}, f32[2,256,128]{2,1,0:T(8,128)S(1)}, bf...) custom-call(s32[2,256]{1,0:T(2,128)S(1)} %copy-done.13, ...), custom_call_target="tpu_custom_call" | custom-call | flops 30000001024 | bytes 1048576 | tf_op jit(solution)/shard_map/mix_fwd/pallas_call | solution.py:871
  67.0 0.0 copy-done.9
  67.0 14.1 %gate_stage.1 = (f32[2,256,768]{2,1,0:T(8,128)S(1)}, bf16[2,256,768]{2,1,0:T(8,128)(2,1)S(1)}, bf16[2,128,768]{2,1,0:T(8,128)(2,1)S(1)}, bf16[2,256,1536]{2,1,0:...) custom-call(f32[2,256,768]{2,1,0:T(8,128)S(1)} %get-tuple-element.78.y_p, ...), custom_call_target="tpu_custom_call" | custom-call | flops 6000000000 | bytes 1048576 | tf_op jit(solution)/shard_map/gate_stage/pallas_call | solution.py:871
  81.1 33.3 %mix_bwd.1 = (bf16[2,256,768]{2,1,0:T(8,128)(2,1)S(1)}, bf16[2,256,256]{2,1,0:T(8,128)(2,1)S(1)}, bf16[2,256,128]{2,1,0:T(8,128)(2,1)S(1)}, f32[8,768]{1,0:T(8,1...) custom-call(f32[2,256,768]{2,1,0:T(8,128)S(1)} %get-tuple-element.85, ...), custom_call_target="tpu_custom_call" | custom-call | flops 8000000000 | bytes 1048576 | tf_op jit(solution)/shard_map/mix_bwd/pallas_call | solution.py:871
  114.4 0.0 copy-start.1
  114.4 40.8 %reduce_all.1 = (f32[2,64,1536]{2,1,0:T(8,128)S(1)}, f32[192,768]{1,0:T(8,128)S(1)}, f32[192,256]{1,0:T(8,128)S(1)}, f32[192,128]{1,0:T(8,128)S(1)}, bf16[4,16,768]{2,1,0:T(8,128)(2,1)S(1)}) custom-call(bf16[2,256,1536]{2,1,0:T(8,128)(2,1)S(1)} %get-tuple-element.74.normed.tokens_in, bf16[2,256,768]{2,1,0:T(8,128)(2,1)S(1)} %get-tuple-element.98.dg, ...), custom_call_target="tpu_custom_call" | custom-call | flops 6000000000 | bytes 1048576 | tf_op jit(solution)/shard_map/reduce_all/pallas_call | solution.py:871
  155.2 0.0 copy-done.1
  155.2 3.0 %emit_all.1 = (bf16[2,64,1536]{2,1,0:T(8,128)(2,1)}, f32[2,64,1536]{2,1,0:T(8,128)}, f32[1,1536]{1,0:T(1,128)S(1)}, f32[192,768]{1,0:T(8,128)}, f32[192,768]{1,0...) custom-call(bf16[2,64,1536]{2,1,0:T(8,128)(2,1)S(1)} %copy-done.1, ...), custom_call_target="tpu_custom_call" | custom-call | tf_op jit(solution)/shard_map/emit_all/pallas_call | solution.py:1551
  158.2 0.6 reduce
  (9 shorter events, 0.0 us)
Async XLA Ops:
  2.1 1.0 copy-start
  3.1 1.0 copy-start.3
  4.1 0.9 copy-start.6
  5.0 0.7 copy-start.10
  5.7 0.7 copy-start.12
  6.4 32.9 %copy-start.2 = (bf16[2,64,1536]{2,1,0:T(8,128)(2,1)S(1)}, bf16[2,64,1536]{2,1,0:T(8,128)(2,1)}, u32[]{:S(2)}) copy-start(bf16[2,64,1536]{2,1,0:T(8,128)(2,1)} %cot.3) | copy-start | bytes 1179652
  6.4 32.9 %copy-start.4 = (bf16[768,192]{0,1:T(8,128)(2,1)S(1)}, bf16[768,192]{0,1:T(8,128)(2,1)}, u32[]{:S(2)}) copy-start(bf16[768,192]{0,1:T(8,128)(2,1)} %param.32) | copy-start | bytes 884740
  6.4 32.9 %copy-start.5 = (bf16[192,768]{1,0:T(8,128)(2,1)S(1)}, bf16[192,768]{1,0:T(8,128)(2,1)}, u32[]{:S(2)}) copy-start(bf16[192,768]{1,0:T(8,128)(2,1)} %wg.1) | copy-start | bytes 884740
  6.4 32.9 %copy-start.7 = (f32[4,3072]{1,0:T(4,128)S(1)}, f32[4,3072]{1,0:T(4,128)}, u32[]{:S(2)}) copy-start(f32[4,3072]{1,0:T(4,128)} %taps_i.3) | copy-start | bytes 147460
  6.4 32.9 %copy-start.8 = (f32[3072]{0:T(1024)S(1)}, f32[3072]{0:T(1024)}, u32[]{:S(2)}) copy-start(f32[3072]{0:T(1024)} %param.25) | copy-start | bytes 36868
  6.4 32.9 %copy-start.11 = (f32[4,256]{1,0:T(4,128)S(1)}, f32[4,256]{1,0:T(4,128)}, u32[]{:S(2)}) copy-start(f32[4,256]{1,0:T(4,128)} %taps_s.3) | copy-start | bytes 12292
  6.4 32.9 %copy-start.13 = (s32[2,256]{1,0:T(2,128)S(1)}, s32[2,256]{1,0:T(2,128)}, u32[]{:S(2)}) copy-start(s32[2,256]{1,0:T(2,128)} %seg.3) | copy-start | bytes 6148
  6.4 32.9 %copy-start.14 = (f32[256]{0:T(256)S(1)}, f32[256]{0:T(256)}, u32[]{:S(2)}) copy-start(f32[256]{0:T(256)} %param.27) | copy-start | bytes 3076
  39.3 27.7 %copy-start.9 = (f32[3072]{0:T(1024)S(1)}, f32[3072]{0:T(1024)}, u32[]{:S(2)}) copy-start(f32[3072]{0:T(1024)} %param.31) | copy-start | bytes 36868
  114.4 40.8 %copy-start.1 = (bf16[2,64,1536]{2,1,0:T(8,128)(2,1)S(1)}, bf16[2,64,1536]{2,1,0:T(8,128)(2,1)}, u32[]{:S(2)}) copy-start(bf16[2,64,1536]{2,1,0:T(8,128)(2,1)} %tok.1) | copy-start | bytes 1179652
